TPU v7x, 32 devices: a whole 2x2x4 slice. The times are simulated.
32 devices in a mesh: dp: 8 (over z, core), tensor: 4 (over y, x).
Axes of the slice: x: 2, y: 2, z: 4, core: 2. Of those that a mesh axis runs over, the one named last changes fastest.
Arguments:
- tokens: bfloat16 [18432, 2048], P(('dp', 'tensor')), may hold values from -6 to 6
- cotangent: bfloat16 [18432, 2048], P(('dp', 'tensor')), may hold values from -6 to 6
- ln_gain: float32 [2048], replicated, may hold values from 0.5 to 1.5
- ln_bias: float32 [2048], replicated, may hold values from -3 to 3
- w_qkv: bfloat16 [3, 2048, 2048], P(None, 'dp', 'tensor')
- b_qkv: float32 [3, 2048], P(None, 'tensor'), may hold values from -3 to 3
- w_out: bfloat16 [2048, 2048], P('tensor', 'dp'), may hold values from -0.5 to 0.5
- w_fc1: bfloat16 [2048, 8192], P('dp', 'tensor'), may hold values from -0.125 to 0.125
- b_fc1: float32 [8192], P('tensor'), may hold values from -3 to 3
- w_fc2: bfloat16 [8192, 2048], P('tensor', 'dp'), may hold values from -0.0625 to 0.0625
- resid_bias: float32 [2048], replicated, may hold values from -3 to 3
- parents: int32 [8, 18], P('dp'), may hold values from 0 to 9, as said below
Outputs:
- output_rows: bfloat16 [18432, 2048], P(('dp', 'tensor'))
- input_grad: float32 [18432, 2048], P(('dp', 'tensor'))
- grad_small: float32 [3, 2048], P(None, ('dp', 'tensor'))
- grad_w_qkv: float32 [3, 2048, 2048], P(None, 'dp', 'tensor')
- grad_b_qkv: float32 [3, 2048], P(None, 'tensor')
- grad_w_out: float32 [2048, 2048], P('tensor', 'dp')
- grad_w_fc1: float32 [2048, 8192], P('dp', 'tensor')
- grad_b_fc1: float32 [8192], P('tensor')
- grad_w_fc2: float32 [8192, 2048], P('tensor', 'dp')
- clipped_qk: bfloat16 [2, 2048, 2048], P(None, 'dp', 'tensor')
Inputs may be any that keep to these rules, and one draw needn't show every extreme that they name: `parents`: in each tree, segment 0 is its own parent and segment i < 6 has parent i - 1; the next 4 segments have parent 6 - 1; each of these is the parent of exactly 2 of the remaining segments.
All inputs are finite; a program needn't handle non-finite values.
Results may differ from a plain program's by a relative error of at most 0.014.
Values may be sent and summed in bfloat16 or wider, within the bound.
A program may use at most 384 MiB of HBM per device.

v0:
```python
import jax
import jax.numpy as jnp
from jax import lax
from jax.sharding import PartitionSpec as P

HDIM = 64
ROT = 32
SEG = 128
QBLK = 768


clip_tau = 10.0
norm_eps = 1e-05
rope_base = 10000.0


def tree_layout(parent_ids, seg_len):
    seg_count = parent_ids.shape[0]
    labels = jnp.arange(seg_count, dtype=jnp.int32)
    current = labels
    depth_seg = jnp.zeros((seg_count,), jnp.int32)
    ancestry = labels[:, None] == labels[None, :]
    for step_index in range(seg_count):
        depth_seg = depth_seg + (current != 0).astype(jnp.int32)
        current = jnp.sum(
            jnp.where(current[:, None] == labels[None, :], parent_ids[None, :], 0), axis=1
        )
        ancestry = ancestry | (current[:, None] == labels[None, :])
    positions = jnp.repeat(depth_seg, seg_len) * seg_len + jnp.tile(
        jnp.arange(seg_len, dtype=jnp.int32), seg_count
    )
    return (positions, ancestry)


def rotary_tables(positions):
    half_rot = ROT // 2
    inverse_freq = 1.0 / rope_base ** (jnp.arange(half_rot, dtype=jnp.float32) * (2.0 / ROT))
    angles = positions.astype(jnp.float32)[:, None] * inverse_freq[None, :]
    return (jnp.cos(angles), jnp.sin(angles))


def rotate(block_in, cos_rows, sin_rows):
    half_rot = ROT // 2
    first_half = block_in[..., :half_rot]
    second_half = block_in[..., half_rot:ROT]
    cos_heads = cos_rows[:, None, :]
    sin_heads = sin_rows[:, None, :]
    return jnp.concatenate(
        [
            first_half * cos_heads - second_half * sin_heads,
            second_half * cos_heads + first_half * sin_heads,
            block_in[..., ROT:],
        ],
        axis=-1,
    )


def unrotate(grad_in, cos_rows, sin_rows):
    half_rot = ROT // 2
    first_half = grad_in[..., :half_rot]
    second_half = grad_in[..., half_rot:ROT]
    cos_heads = cos_rows[:, None, :]
    sin_heads = sin_rows[:, None, :]
    return jnp.concatenate(
        [
            first_half * cos_heads + second_half * sin_heads,
            second_half * cos_heads - first_half * sin_heads,
            grad_in[..., ROT:],
        ],
        axis=-1,
    )


def block_mask(ancestry, row_start, row_count, total_rows, seg_len):
    row_ids = row_start + jnp.arange(row_count, dtype=jnp.int32)
    col_ids = jnp.arange(total_rows, dtype=jnp.int32)
    seg_rows = lax.dynamic_slice_in_dim(ancestry, row_start // seg_len, row_count // seg_len, 0)
    widened = jnp.repeat(jnp.repeat(seg_rows, seg_len, axis=0), seg_len, axis=1)
    same_seg = row_ids[:, None] // seg_len == col_ids[None, :] // seg_len
    return widened & (~same_seg | (col_ids[None, :] <= row_ids[:, None]))


def norm_rows(rows_in, gain_in, shift_in):
    row_mean = jnp.mean(rows_in, axis=-1, keepdims=True)
    centred = rows_in - row_mean
    inverse = lax.rsqrt(jnp.mean(centred * centred, axis=-1, keepdims=True) + norm_eps)
    return centred * inverse * gain_in + shift_in


def gelu_tanh(values_in):
    return jax.nn.gelu(values_in, approximate=True)


def body(
    tokens,
    cotangent,
    ln_gain,
    ln_bias,
    w_qkv,
    b_qkv,
    w_out,
    w_fc1,
    b_fc1,
    w_fc2,
    resid_bias,
    parents,
):
    local_rows = tokens.shape[0]
    total_rows = local_rows * lax.axis_size("tensor")
    own_start = lax.axis_index("tensor") * local_rows
    head_count = w_qkv.shape[2] // HDIM
    score_scale = HDIM ** (-0.5)
    positions, ancestry = tree_layout(parents[0], SEG)
    cos_rows, sin_rows = rotary_tables(positions)
    block_starts = jnp.arange(total_rows // QBLK, dtype=jnp.int32) * QBLK
    tokens_f = tokens.astype(jnp.float32)
    normed_local = norm_rows(tokens_f, ln_gain, ln_bias).astype(jnp.bfloat16)
    qkv_w, out_w, up_w, down_w = (
        lax.all_gather(w_qkv, "dp", axis=1, tiled=True),
        lax.all_gather(w_out, "dp", axis=1, tiled=True),
        lax.all_gather(w_fc1, "dp", axis=0, tiled=True),
        lax.all_gather(w_fc2, "dp", axis=1, tiled=True),
    )
    normed = lax.all_gather(normed_local, "tensor", axis=0, tiled=True)
    projected = (
        jnp.einsum("td,cdh->cth", normed, qkv_w, preferred_element_type=jnp.float32)
        + b_qkv[:, None, :]
    )
    heads_view = projected.reshape(3, total_rows, head_count, HDIM)
    queries = rotate(heads_view[0], cos_rows, sin_rows).astype(jnp.bfloat16)
    keys_rot = rotate(heads_view[1], cos_rows, sin_rows).astype(jnp.bfloat16)
    values_all = heads_view[2].astype(jnp.bfloat16)

    def attend_block(row_start):
        query_rows = lax.dynamic_slice_in_dim(queries, row_start, QBLK, 0)
        raw_scores = (
            jnp.einsum("qhe,khe->hqk", query_rows, keys_rot, preferred_element_type=jnp.float32)
            * score_scale
        )
        allowed = block_mask(ancestry, row_start, QBLK, total_rows, SEG)
        masked = jnp.where(allowed[None], raw_scores, -1e30)
        row_top = jnp.max(masked, axis=2)
        exponent = jnp.exp(masked - row_top[..., None])
        row_total = jnp.sum(exponent, axis=2)
        probs_low = (exponent / row_total[..., None]).astype(jnp.bfloat16)
        attended_rows = jnp.einsum(
            "hqk,khe->qhe", probs_low, values_all, preferred_element_type=jnp.float32
        ).astype(jnp.bfloat16)
        return (attended_rows, row_top + jnp.log(row_total), jnp.max(row_top, axis=1))

    attended, log_totals, block_tops = lax.map(attend_block, block_starts)
    attended = attended.reshape(total_rows, head_count * HDIM)
    hidden_pre = jnp.dot(normed, up_w, preferred_element_type=jnp.float32) + b_fc1
    activated = gelu_tanh(hidden_pre).astype(jnp.bfloat16)
    branch_whole = lax.psum(
        jnp.dot(attended, out_w, preferred_element_type=jnp.float32)
        + jnp.dot(activated, down_w, preferred_element_type=jnp.float32),
        "tensor",
    )
    branch_sum = lax.dynamic_slice_in_dim(branch_whole, own_start, local_rows, 0)
    output_rows = (tokens_f + branch_sum + resid_bias).astype(jnp.bfloat16)
    head_top = lax.pmax(jnp.max(block_tops, axis=0), "dp")
    factor = jnp.sqrt(clip_tau / jnp.maximum(head_top, clip_tau))
    clipped_qk = (w_qkv[:2].astype(jnp.float32) * jnp.repeat(factor, HDIM)[None, None, :]).astype(
        jnp.bfloat16
    )
    cot_full = lax.all_gather(cotangent, "tensor", axis=0, tiled=True)
    grad_attended = jnp.einsum(
        "td,hd->th", cot_full, out_w, preferred_element_type=jnp.float32
    ).astype(jnp.bfloat16)
    grad_w_out = jnp.einsum("th,td->hd", attended, cot_full, preferred_element_type=jnp.float32)
    grad_act = jnp.einsum("td,fd->tf", cot_full, down_w, preferred_element_type=jnp.float32)
    ignored, gelu_back = jax.vjp(gelu_tanh, hidden_pre)
    grad_hidden = gelu_back(grad_act)[0].astype(jnp.bfloat16)
    grad_w_fc2 = jnp.einsum("tf,td->fd", activated, cot_full, preferred_element_type=jnp.float32)
    grad_w_fc1 = jnp.einsum("td,tf->df", normed, grad_hidden, preferred_element_type=jnp.float32)
    grad_b_fc1 = jnp.sum(grad_hidden.astype(jnp.float32), axis=0)
    grad_heads = grad_attended.reshape(total_rows, head_count, HDIM)

    def back_block(carry, block_pair):
        grad_keys, grad_values = carry
        row_start, log_rows = block_pair
        query_rows = lax.dynamic_slice_in_dim(queries, row_start, QBLK, 0)
        grad_rows = lax.dynamic_slice_in_dim(grad_heads, row_start, QBLK, 0)
        raw_scores = (
            jnp.einsum("qhe,khe->hqk", query_rows, keys_rot, preferred_element_type=jnp.float32)
            * score_scale
        )
        allowed = block_mask(ancestry, row_start, QBLK, total_rows, SEG)
        masked = jnp.where(allowed[None], raw_scores, -1e30)
        probs_f = jnp.exp(masked - log_rows[..., None])
        probs_low = probs_f.astype(jnp.bfloat16)
        grad_probs = jnp.einsum(
            "qhe,khe->hqk", grad_rows, values_all, preferred_element_type=jnp.float32
        )
        grad_scores = (
            probs_f * (grad_probs - jnp.sum(probs_f * grad_probs, axis=2, keepdims=True))
        ).astype(jnp.bfloat16)
        grad_queries = (
            jnp.einsum("hqk,khe->qhe", grad_scores, keys_rot, preferred_element_type=jnp.float32)
            * score_scale
        )
        grad_keys = (
            grad_keys
            + jnp.einsum(
                "hqk,qhe->khe", grad_scores, query_rows, preferred_element_type=jnp.float32
            )
            * score_scale
        )
        grad_values = grad_values + jnp.einsum(
            "hqk,qhe->khe", probs_low, grad_rows, preferred_element_type=jnp.float32
        )
        return ((grad_keys, grad_values), grad_queries)

    zero_heads = jnp.zeros((total_rows, head_count, HDIM), jnp.float32)
    (grad_keys, grad_values), grad_queries = lax.scan(
        back_block, (zero_heads, zero_heads), (block_starts, log_totals)
    )
    grad_queries = grad_queries.reshape(total_rows, head_count, HDIM)
    grad_qkv = jnp.stack(
        [
            unrotate(grad_queries, cos_rows, sin_rows),
            unrotate(grad_keys, cos_rows, sin_rows),
            grad_values,
        ]
    )
    grad_qkv = grad_qkv.reshape(3, total_rows, head_count * HDIM).astype(jnp.bfloat16)
    grad_w_qkv = jnp.einsum("td,cth->cdh", normed, grad_qkv, preferred_element_type=jnp.float32)
    grad_b_qkv = jnp.sum(grad_qkv.astype(jnp.float32), axis=1)
    summed_qkv, summed_out, summed_fc1, summed_fc2 = (
        lax.psum_scatter(
            grad_w_qkv.astype(jnp.bfloat16), "dp", scatter_dimension=1, tiled=True
        ).astype(jnp.float32),
        lax.psum_scatter(
            grad_w_out.astype(jnp.bfloat16), "dp", scatter_dimension=1, tiled=True
        ).astype(jnp.float32),
        lax.psum_scatter(
            grad_w_fc1.astype(jnp.bfloat16), "dp", scatter_dimension=0, tiled=True
        ).astype(jnp.float32),
        lax.psum_scatter(
            grad_w_fc2.astype(jnp.bfloat16), "dp", scatter_dimension=1, tiled=True
        ).astype(jnp.float32),
    )
    bias_qkv, bias_fc1 = lax.psum((grad_b_qkv, grad_b_fc1), "dp")
    normed_all = lax.psum(
        (
            jnp.einsum("cth,cdh->td", grad_qkv, qkv_w, preferred_element_type=jnp.float32)
            + jnp.einsum("tf,df->td", grad_hidden, up_w, preferred_element_type=jnp.float32)
        ).astype(jnp.bfloat16),
        "tensor",
    ).astype(jnp.float32)
    grad_normed = lax.dynamic_slice_in_dim(normed_all, own_start, local_rows, 0)
    ignored_rows, norm_back = jax.vjp(norm_rows, tokens_f, ln_gain, ln_bias)
    grad_tokens, gain_part, shift_part = norm_back(grad_normed)
    cot_local = cotangent.astype(jnp.float32)
    input_grad = cot_local + grad_tokens
    small_terms = jnp.stack([gain_part, shift_part, jnp.sum(cot_local, axis=0)])
    grad_small = lax.psum_scatter(small_terms, ("dp", "tensor"), scatter_dimension=1, tiled=True)
    return (
        output_rows,
        input_grad,
        grad_small,
        summed_qkv,
        bias_qkv,
        summed_out,
        summed_fc1,
        bias_fc1,
        summed_fc2,
        clipped_qk,
    )


def solution(mesh):
    return jax.shard_map(
        body,
        mesh=mesh,
        in_specs=(
            P(("dp", "tensor"), None),
            P(("dp", "tensor"), None),
            P(),
            P(),
            P(None, "dp", "tensor"),
            P(None, "tensor"),
            P("tensor", "dp"),
            P("dp", "tensor"),
            P("tensor"),
            P("tensor", "dp"),
            P(),
            P("dp", None),
        ),
        out_specs=(
            P(("dp", "tensor"), None),
            P(("dp", "tensor"), None),
            P(None, ("dp", "tensor")),
            P(None, "dp", "tensor"),
            P(None, "tensor"),
            P("tensor", "dp"),
            P("dp", "tensor"),
            P("tensor"),
            P("tensor", "dp"),
            P(None, "dp", "tensor"),
        ),
        check_vma=False,
    )
```

profile of v0, /device:TPU:0, one launch (start us, length us, event | category | flops | bytes accessed | tf_op | source)
XLA Modules:
  0.0 2248.9 jit_solution(18235470847636643022)
XLA Ops:
  21.2 56.9 %all-gather.9.cloned.1.call-done = bf16[3,2048,512]{1,2,0:T(8,128)(2,1)} async-done(((bf16[3,256,512]{1,2,0:T(8,128)(2,1)}), bf16[3,2048,512]{1,2,0:T(8,128)(2,1)}) %all-gather.9.cloned.1.call-update) | async-done | bytes 6291472 | tf_op jit(solution)/shard_map/all_gather | solution.py:119
  78.1 96.4 %all-gather.7.cloned.1.call-done = bf16[2304,2048]{1,0:T(8,128)(2,1)} async-done(((bf16[576,2048]{1,0:T(8,128)(2,1)}), bf16[2304,2048]{1,0:T(8,128)(2,1)}) %all-gather.7.cloned.1.call-update) | async-done | bytes 9437200 | tf_op jit(solution)/shard_map/all_gather | solution.py:124
  207.6 261.1 %while.35 = (s32[]{:T(128)}, bf16[3,768,8,64]{1,3,2,0:T(8,128)(2,1)}, f32[3,8,768]{2,1,0:T(8,128)}, f32[3,8]{1,0:T(4,128)}, s32[3]{0:T(128)S(1)}, /*index=5*/pre...) while((s32[]{:T(128)}, ...), condition=%wide.region_24.25_spmd, body=%wide.region_20.24_spmd.sunk | while | flops 3817168896 | bytes 187103536 | solution.py:151
  229.4 25.1 %fusion.171 = (f32[8,768]{1,0:T(8,128)S(1)}, f32[8,768,2304]{2,1,0:T(8,128)}) fusion(pred[768,2304]{1,0:T(8,128)(4,1)S(1)} %copy.75, bf16[2304,8,64]{0,2,1:T(8,128)(2,1)} %get-tuple-element.657, bf16[2304,8,64]{0,2,1:T(8,128)(2,1)} %get-tuple-element.656, s32[]{:T(128)S(6)} %select_n.269), kind=kOutput, calls=%fused_computation.5.clone.1 | convolution fusion | flops 1854400512 | bytes 61562884 | tf_op jit(solution)/shard_map/while/body/eval_jaxpr/qhe,khe->hqk/dot_general | solution.py:137
  359.7 24.6 %fusion.173 = bf16[3,768,8,64]{1,3,2,0:T(8,128)(2,1)} fusion(bf16[3,768,8,64]{1,3,2,0:T(8,128)(2,1)} %get-tuple-element.634, s32[]{:T(128)} %get-tuple-element.633, bf16[2304,8,64]{0,2,1:T(8,128)(2,1)} %get-tuple-element.658, f32[8,768,2304]{2,1,0:T(8,128)} %get-tuple-element.597, f32[8,768]{1,0:T(8,128)S(1)} %get-tuple-element.599, ...), kind=kOutput, calls=%fused_computation.12.clone.1 | convolution fusion | flops 1883111424 | bytes 61587968 | tf_op jit(solution)/shard_map/while/body/eval_jaxpr/hqk,khe->qhe/dot_general | solution.py:146
  442.8 24.6 %fusion.173 = bf16[3,768,8,64]{1,3,2,0:T(8,128)(2,1)} fusion(bf16[3,768,8,64]{1,3,2,0:T(8,128)(2,1)} %get-tuple-element.634, s32[]{:T(128)} %get-tuple-element.633, bf16[2304,8,64]{0,2,1:T(8,128)(2,1)} %get-tuple-element.658, f32[8,768,2304]{2,1,0:T(8,128)} %get-tuple-element.597, f32[8,768]{1,0:T(8,128)S(1)} %get-tuple-element.599, ...), kind=kOutput, calls=%fused_computation.12.clone.1 | convolution fusion | flops 1883111424 | bytes 61587968 | tf_op jit(solution)/shard_map/while/body/eval_jaxpr/hqk,khe->qhe/dot_general | solution.py:146
  479.2 657.4 %while.36 = (s32[]{:T(128)}, f32[2304,8,64]{0,2,1:T(8,128)}, f32[2304,8,64]{0,2,1:T(8,128)}, f32[3,768,8,64]{1,0,3,2:T(4,128)}, s32[3]{0:T(128)S(1)}, /*index=5*...) while((s32[]{:T(128)}, f32[2304,8,64]{0,2,1:T(8,128)}, ...), condition=%wide.region_28.29_spmd.clone, body=%wide.region_26.28_spmd.clone.sunk | while | flops 9287196672 | bytes 472552672 | solution.py:216
  529.8 42.9 %multiply_reduce_fusion.2 = (f32[8,768]{1,0:T(8,128)S(1)}, f32[8,768,2304]{2,1,0:T(8,128)}) fusion(f32[8,768,2304]{2,1,0:T(8,128)} %fusion.183, f32[8,768]{1,0:T(8,128)S(1)} %dynamic-slice_bitcast_fusion.2, pred[768,2304]{1,0:T(8,128)(4,1)S(1)} %copy.77, bf16[2304,8,64]{0,2,1:T(8,128)(2,1)} %get-tuple-element.715, ...), kind=kOutput, calls=%fused_computation.38.clone.1 | convolution fusion | flops 1882712064 | bytes 118210560 | tf_op jit(solution)/shard_map/while/body/eval_jaxpr/qhe,khe->hqk/dot_general | solution.py:193
  572.7 44.8 %multiply_convert_fusion.6 = bf16[8,768,2304]{2,1,0:T(8,128)(2,1)} fusion(f32[8,768,2304]{2,1,0:T(8,128)} %get-tuple-element.614, f32[8,768,2304]{2,1,0:T(8,128)} %fusion.183, f32[8,768]{1,0:T(8,128)S(1)} %get-tuple-element.615, f32[8,768]{1,0:T(8,128)S(1)} %dynamic-slice_bitcast_fusion.2, pred[768,2304]{1,0:T(8,128)(4,1)S(1)} %copy.77), kind=kLoop, calls=%fused_computation.37.clone.1 | loop fusion | flops 84934656 | bytes 143376384 | tf_op jit(solution)/shard_map/while/body/eval_jaxpr/convert_element_type | solution.py:198
  634.2 30.3 %dynamic_update_slice.42 = f32[3,768,8,64]{1,0,3,2:T(4,128)} dynamic-update-slice(f32[3,768,8,64]{1,0,3,2:T(4,128)} %get-tuple-element.689, f32[1,768,8,64]{1,0,3,2:T(1,128)} %copy.78, s32[]{:T(128)} %get-tuple-element.686, s32[]{:T(128)} %constant.247.clone.1..sunk.1, s32[]{:T(128)} %constant.247.clone.1..sunk.1, s32[]{:T(128)} %constant.247.clone.1..sunk.1) | dynamic-update-slice | bytes 3145732 | tf_op jit(solution)/shard_map/while/body/jit(dynamic_update_index_in_dim)/dynamic_update_slice | solution.py:216
  681.1 25.6 %fusion.186 = f32[2304,8,64]{0,2,1:T(8,128)} fusion(f32[8,768,2304]{2,1,0:T(8,128)} %fusion.183, f32[8,768]{1,0:T(8,128)S(1)} %dynamic-slice_bitcast_fusion.2, pred[768,2304]{1,0:T(8,128)(4,1)S(1)} %copy.77, f32[2304,8,64]{0,2,1:T(8,128)} %get-tuple-element.688, pred[]{:T(512)S(6)} %compare.54, bf16[2304,8,64]{0,2,1:T(8,128)(2,1)} %get-tuple-element.714, ...), kind=kOutput, calls=%fused_computation.48.clone.1 | convolution fusion | flops 1870921728 | bytes 68640776 | tf_op jit(solution)/shard_map/while/body/eval_jaxpr/hqk,qhe->khe/dot_general | solution.py:210
  741.9 42.9 %multiply_reduce_fusion.2 = (f32[8,768]{1,0:T(8,128)S(1)}, f32[8,768,2304]{2,1,0:T(8,128)}) fusion(f32[8,768,2304]{2,1,0:T(8,128)} %fusion.183, f32[8,768]{1,0:T(8,128)S(1)} %dynamic-slice_bitcast_fusion.2, pred[768,2304]{1,0:T(8,128)(4,1)S(1)} %copy.77, bf16[2304,8,64]{0,2,1:T(8,128)(2,1)} %get-tuple-element.715, ...), kind=kOutput, calls=%fused_computation.38.clone.1 | convolution fusion | flops 1882712064 | bytes 118210560 | tf_op jit(solution)/shard_map/while/body/eval_jaxpr/qhe,khe->hqk/dot_general | solution.py:193
  784.8 44.8 %multiply_convert_fusion.6 = bf16[8,768,2304]{2,1,0:T(8,128)(2,1)} fusion(f32[8,768,2304]{2,1,0:T(8,128)} %get-tuple-element.614, f32[8,768,2304]{2,1,0:T(8,128)} %fusion.183, f32[8,768]{1,0:T(8,128)S(1)} %get-tuple-element.615, f32[8,768]{1,0:T(8,128)S(1)} %dynamic-slice_bitcast_fusion.2, pred[768,2304]{1,0:T(8,128)(4,1)S(1)} %copy.77), kind=kLoop, calls=%fused_computation.37.clone.1 | loop fusion | flops 84934656 | bytes 143376384 | tf_op jit(solution)/shard_map/while/body/eval_jaxpr/convert_element_type | solution.py:198
  846.3 30.3 %dynamic_update_slice.42 = f32[3,768,8,64]{1,0,3,2:T(4,128)} dynamic-update-slice(f32[3,768,8,64]{1,0,3,2:T(4,128)} %get-tuple-element.689, f32[1,768,8,64]{1,0,3,2:T(1,128)} %copy.78, s32[]{:T(128)} %get-tuple-element.686, s32[]{:T(128)} %constant.247.clone.1..sunk.1, s32[]{:T(128)} %constant.247.clone.1..sunk.1, s32[]{:T(128)} %constant.247.clone.1..sunk.1) | dynamic-update-slice | bytes 3145732 | tf_op jit(solution)/shard_map/while/body/jit(dynamic_update_index_in_dim)/dynamic_update_slice | solution.py:216
  894.5 27.0 %fusion.186 = f32[2304,8,64]{0,2,1:T(8,128)} fusion(f32[8,768,2304]{2,1,0:T(8,128)} %fusion.183, f32[8,768]{1,0:T(8,128)S(1)} %dynamic-slice_bitcast_fusion.2, pred[768,2304]{1,0:T(8,128)(4,1)S(1)} %copy.77, f32[2304,8,64]{0,2,1:T(8,128)} %get-tuple-element.688, pred[]{:T(512)S(6)} %compare.54, bf16[2304,8,64]{0,2,1:T(8,128)(2,1)} %get-tuple-element.714, ...), kind=kOutput, calls=%fused_computation.48.clone.1 | convolution fusion | flops 1870921728 | bytes 68640776 | tf_op jit(solution)/shard_map/while/body/eval_jaxpr/hqk,qhe->khe/dot_general | solution.py:210
  956.7 42.9 %multiply_reduce_fusion.2 = (f32[8,768]{1,0:T(8,128)S(1)}, f32[8,768,2304]{2,1,0:T(8,128)}) fusion(f32[8,768,2304]{2,1,0:T(8,128)} %fusion.183, f32[8,768]{1,0:T(8,128)S(1)} %dynamic-slice_bitcast_fusion.2, pred[768,2304]{1,0:T(8,128)(4,1)S(1)} %copy.77, bf16[2304,8,64]{0,2,1:T(8,128)(2,1)} %get-tuple-element.715, ...), kind=kOutput, calls=%fused_computation.38.clone.1 | convolution fusion | flops 1882712064 | bytes 118210560 | tf_op jit(solution)/shard_map/while/body/eval_jaxpr/qhe,khe->hqk/dot_general | solution.py:193
  999.6 44.8 %multiply_convert_fusion.6 = bf16[8,768,2304]{2,1,0:T(8,128)(2,1)} fusion(f32[8,768,2304]{2,1,0:T(8,128)} %get-tuple-element.614, f32[8,768,2304]{2,1,0:T(8,128)} %fusion.183, f32[8,768]{1,0:T(8,128)S(1)} %get-tuple-element.615, f32[8,768]{1,0:T(8,128)S(1)} %dynamic-slice_bitcast_fusion.2, pred[768,2304]{1,0:T(8,128)(4,1)S(1)} %copy.77), kind=kLoop, calls=%fused_computation.37.clone.1 | loop fusion | flops 84934656 | bytes 143376384 | tf_op jit(solution)/shard_map/while/body/eval_jaxpr/convert_element_type | solution.py:198
  1061.1 30.3 %dynamic_update_slice.42 = f32[3,768,8,64]{1,0,3,2:T(4,128)} dynamic-update-slice(f32[3,768,8,64]{1,0,3,2:T(4,128)} %get-tuple-element.689, f32[1,768,8,64]{1,0,3,2:T(1,128)} %copy.78, s32[]{:T(128)} %get-tuple-element.686, s32[]{:T(128)} %constant.247.clone.1..sunk.1, s32[]{:T(128)} %constant.247.clone.1..sunk.1, s32[]{:T(128)} %constant.247.clone.1..sunk.1) | dynamic-update-slice | bytes 3145732 | tf_op jit(solution)/shard_map/while/body/jit(dynamic_update_index_in_dim)/dynamic_update_slice | solution.py:216
  1109.3 27.0 %fusion.186 = f32[2304,8,64]{0,2,1:T(8,128)} fusion(f32[8,768,2304]{2,1,0:T(8,128)} %fusion.183, f32[8,768]{1,0:T(8,128)S(1)} %dynamic-slice_bitcast_fusion.2, pred[768,2304]{1,0:T(8,128)(4,1)S(1)} %copy.77, f32[2304,8,64]{0,2,1:T(8,128)} %get-tuple-element.688, pred[]{:T(512)S(6)} %compare.54, bf16[2304,8,64]{0,2,1:T(8,128)(2,1)} %get-tuple-element.714, ...), kind=kOutput, calls=%fused_computation.48.clone.1 | convolution fusion | flops 1870921728 | bytes 68640776 | tf_op jit(solution)/shard_map/while/body/eval_jaxpr/hqk,qhe->khe/dot_general | solution.py:210
  1185.1 26.4 %fusion.123 = f32[2304,2048]{1,0:T(8,128)} fusion(bf16[2304,2048]{1,0:T(8,128)(2,1)} %all-gather.7.cloned.1.call-done, bf16[2048,2048]{1,0:T(8,128)(2,1)} %all-gather.13.cloned.1.call-done), kind=kOutput, calls=%fused_computation.256 | convolution fusion | flops 19327352832 | bytes 36700160 | tf_op jit(solution)/shard_map/dot_general | solution.py:153
  1211.5 39.5 %convert_reduce_fusion = (f32[2048]{0:T(1024)}, bf16[2304,2048]{1,0:T(8,128)(2,1)}) fusion(f32[2304,2048]{1,0:T(8,128)} %fusion.123, f32[2048]{0:T(1024)S(1)} %copy-done.25, bf16[2304,2048]{1,0:T(8,128)(2,1)} %all-gather.17.cloned.1.call-done, bf16[2048,2048]{1,0:T(8,128)(2,1)} %all-gather.15.cloned.1.call-done), kind=kOutput, calls=%fused_computation.94 | convolution fusion | flops 19435878400 | bytes 46153728 | tf_op jit(solution)/shard_map/td,fd->tf/dot_general | solution.py:172
  1251.1 28.0 %fusion.59 = bf16[2304,2048]{1,0:T(8,128)(2,1)} fusion(f32[2304,2048,1]{1,0,2:T(8,128)} %fusion.119, bf16[2304,2048]{1,0:T(8,128)(2,1)} %get-tuple-element.444, bf16[2048,2048]{1,0:T(8,128)(2,1)} %all-gather.13.cloned.1.call-done), kind=kOutput, calls=%fused_computation.93 | convolution fusion | flops 19336790016 | bytes 46137344 | tf_op jit(solution)/shard_map/tf,df->td/dot_general | solution.py:248
  1294.2 32.4 %convolution_add_fusion = f32[2304,2048]{1,0:T(8,128)} fusion(f32[2304,2048]{1,0:T(8,128)} %fusion.122, bf16[2048,2048]{1,0:T(8,128)(2,1)} %all-gather.15.cloned.1.call-done, f32[2304,2048]{1,0:T(8,128)} %fusion.123, f32[2048]{0:T(1024)S(1)} %copy-done.25), kind=kOutput, calls=%fused_computation.98 | convolution fusion | flops 19379257344 | bytes 65019904 | tf_op jit(solution)/shard_map/dot_general | solution.py:157
  1358.0 26.6 %convolution_convert_fusion.1 = bf16[2048,2048]{1,0:T(8,128)(2,1)} fusion(bf16[2304,2048]{1,0:T(8,128)(2,1)} %all-gather.7.cloned.1.call-done, bf16[2304,2048]{1,0:T(8,128)(2,1)} %get-tuple-element.444), kind=kOutput, calls=%fused_computation.104 | convolution fusion | flops 19331547136 | bytes 27262976 | tf_op jit(solution)/shard_map/td,tf->df/dot_general | solution.py:176
  1384.7 31.1 %convolution_convert_fusion = bf16[2048,2048]{1,0:T(8,128)(2,1)} fusion(bf16[2304,2048]{1,0:T(8,128)(2,1)} %all-gather.17.cloned.1.call-done, f32[2304,2048]{1,0:T(8,128)} %fusion.123, f32[2048]{0:T(1024)S(1)} %copy-done.25), kind=kOutput, calls=%fused_computation.103 | convolution fusion | flops 19378733056 | bytes 36708352 | tf_op jit(solution)/shard_map/tf,td->fd/dot_general | solution.py:175
  1437.2 30.7 %all-reduce.6.cloned.1.call-done = bf16[2304,2048]{1,0:T(8,128)(2,1)} async-done(((bf16[2304,2048]{1,0:T(8,128)(2,1)}), bf16[2304,2048]{1,0:T(8,128)(2,1)}) %all-reduce.6.cloned.1.call-update) | async-done | bytes 9437200 | tf_op jit(solution)/shard_map/psum | solution.py:245
  1474.5 338.8 %all-reduce.4.cloned.1.call-done = f32[2304,2048]{1,0:T(8,128)} async-done(((f32[2304,2048]{1,0:T(8,128)}), f32[2304,2048]{1,0:T(8,128)}) %all-reduce.4.cloned.1.call-update) | async-done | bytes 18874384 | tf_op jit(solution)/shard_map/psum | solution.py:155
  1823.4 29.3 %all-reduce = (f32[3,512]{1,0:T(4,128)}, f32[2048]{0:T(1024)}) all-reduce(f32[3,512]{1,0:T(4,128)S(1)} %convert_reduce_fusion.1, f32[2048]{0:T(1024)S(1)} %copy-done.21), channel_id=1, replica_groups=mesh['dp'=8,'tensor'=4] {'dp'}, use_global_device_ids=true, to_apply=%region_38.39 | all-reduce | flops 3584 | bytes 28672 | tf_op jit(solution)/shard_map/psum | solution.py:244
  1855.2 69.3 %reduce-scatter.8.cloned.1.call-done = bf16[3,256,512]{1,2,0:T(8,128)(2,1)} async-done(((bf16[3,2048,512]{1,2,0:T(8,128)(2,1)}), bf16[3,256,512]{1,2,0:T(8,128)(2,1)}) %reduce-scatter.8.cloned.1.call-update) | async-done | bytes 786448 | tf_op jit(solution)/shard_map/reduce_scatter | solution.py:231
  1927.0 87.8 %reduce-scatter.12.cloned.1.call-done = bf16[256,2048]{1,0:T(8,128)(2,1)} async-done(((bf16[2048,2048]{1,0:T(8,128)(2,1)}), bf16[256,2048]{1,0:T(8,128)(2,1)}) %reduce-scatter.12.cloned.1.call-update) | async-done | bytes 1048592 | tf_op jit(solution)/shard_map/reduce_scatter | solution.py:237
  2017.6 87.4 %reduce-scatter.14.cloned.1.call-done = bf16[2048,256]{1,0:T(8,128)(2,1)} async-done(((bf16[2048,2048]{1,0:T(8,128)(2,1)}), bf16[2048,256]{1,0:T(8,128)(2,1)}) %reduce-scatter.14.cloned.1.call-update) | async-done | bytes 1048592 | tf_op jit(solution)/shard_map/reduce_scatter | solution.py:240
  2107.8 133.0 %reduce-scatter.16.cloned.1.call-done = f32[64,3]{1,0:T(8,128)} async-done(((f32[2048,3]{1,0:T(8,128)}), f32[64,3]{1,0:T(8,128)}) %reduce-scatter.16.cloned.1.call-update) | async-done | bytes 784
  (245 shorter events, 562.1 us)
Async XLA Ops:
  7.2 4.7 copy-start.1
  7.2 6.6 copy-start.13
  7.2 6.6 copy-start.20
  7.2 70.9 %all-gather.9.cloned.1.call-start = ((), (), s32[]{:S(2)}) async-start(), calls=%async_computation.6 | async-start | bytes 7077888 | tf_op jit(solution)/shard_map/all_gather | solution.py:119
  9.7 164.8 %all-gather.7.cloned.1.call-start = ((), (), s32[]{:S(2)}) async-start(), calls=%async_computation.5 | async-start | bytes 11796480 | tf_op jit(solution)/shard_map/all_gather | solution.py:124
  16.2 158.4 %copy-start.24 = (f32[3,512]{1,0:T(4,128)S(1)}, f32[3,512]{1,0:T(4,128)}, u32[]{:S(2)}) copy-start(f32[3,512]{1,0:T(4,128)} %param.21) | copy-start | bytes 18436
  16.2 452.5 %all-gather.11.cloned.1.call-start = ((), (), s32[]{:S(2)}) async-start(), calls=%async_computation.7 | async-start | bytes 2359296 | tf_op jit(solution)/shard_map/all_gather | solution.py:120
  16.9 451.8 %all-gather.17.cloned.1.call-start = ((), (), s32[]{:S(2)}) async-start(), calls=%async_computation.11 | async-start | bytes 11796480 | tf_op jit(solution)/shard_map/all_gather | solution.py:167
  17.5 1167.6 %all-gather.13.cloned.1.call-start = ((), (), s32[]{:S(2)}) async-start(), calls=%async_computation.8 | async-start | bytes 9437184 | tf_op jit(solution)/shard_map/all_gather | solution.py:121
  18.1 1193.4 %all-gather.15.cloned.1.call-start = ((), (), s32[]{:S(2)}) async-start(), calls=%async_computation.9 | async-start | bytes 9437184 | tf_op jit(solution)/shard_map/all_gather | solution.py:122
  18.7 1449.3 %all-reduce.6.cloned.1.call-start = ((), (), s32[]{:S(2)}) async-start(), calls=%async_computation.12 | async-start | bytes 18874368 | tf_op jit(solution)/shard_map/psum | solution.py:245
  21.2 183.4 %copy-start.7 = (f32[2304,16]{0,1:T(8,128)}, f32[2304,16]{0,1:T(8,128)S(1)}, u32[]{:S(2)}) copy-start(f32[2304,16]{0,1:T(8,128)S(1)} %get-tuple-element.470) | copy-start | bytes 442372
  21.2 183.3 %copy-start.9 = (f32[2304,16]{0,1:T(8,128)}, f32[2304,16]{0,1:T(8,128)S(1)}, u32[]{:S(2)}) copy-start(f32[2304,16]{0,1:T(8,128)S(1)} %get-tuple-element.471) | copy-start | bytes 442372
  1136.6 12.4 copy-start.8
  1136.6 12.4 copy-start.10
  1145.1 3.9 copy-start
  1185.1 26.4 %copy-start.25 = (f32[2048]{0:T(1024)S(1)}, f32[2048]{0:T(1024)}, u32[]{:S(2)}) copy-start(f32[2048]{0:T(1024)} %param.24) | copy-start | bytes 24580
  1279.1 534.1 %all-reduce.4.cloned.1.call-start = ((), (), s32[]{:S(2)}) async-start(), calls=%async_computation.10 | async-start | bytes 37748736 | tf_op jit(solution)/shard_map/psum | solution.py:155
  1326.6 9.6 copy-start.3
  1326.7 526.7 %reduce-scatter.10.cloned.1.call-start = ((), (), s32[]{:S(2)}) async-start(), calls=%async_computation.14 | async-start | bytes 2359296 | tf_op jit(solution)/shard_map/reduce_scatter | solution.py:234
  1336.2 588.3 %reduce-scatter.8.cloned.1.call-start = ((), (), s32[]{:S(2)}) async-start(), calls=%async_computation.13 | async-start | bytes 7077888 | tf_op jit(solution)/shard_map/reduce_scatter | solution.py:231
  1357.9 656.9 %reduce-scatter.12.cloned.1.call-start = ((), (), s32[]{:S(2)}) async-start(), calls=%async_computation.15 | async-start | bytes 9437184 | tf_op jit(solution)/shard_map/reduce_scatter | solution.py:237
  1384.6 720.5 %reduce-scatter.14.cloned.1.call-start = ((), (), s32[]{:S(2)}) async-start(), calls=%async_computation.16 | async-start | bytes 9437184 | tf_op jit(solution)/shard_map/reduce_scatter | solution.py:240
  1415.8 52.2 %copy-start.2 = (bf16[576,2048]{1,0:T(8,128)(2,1)S(1)}, bf16[576,2048]{1,0:T(8,128)(2,1)}, u32[]{:S(2)}) copy-start(bf16[576,2048]{1,0:T(8,128)(2,1)} %param.16) | copy-start | bytes 7077892
  1415.8 52.2 %copy-start.12 = (f32[576]{0:T(1024)S(1)}, f32[576]{0:T(1024)}, u32[]{:S(2)}) copy-start(f32[576]{0:T(1024)} %copy-done.11) | copy-start | bytes 6916
  1415.8 52.2 %copy-start.14 = (f32[2048]{0:T(1024)S(1)}, f32[2048]{0:T(1024)}, u32[]{:S(2)}) copy-start(f32[2048]{0:T(1024)} %param.18) | copy-start | bytes 24580
  1415.8 824.9 %reduce-scatter.16.cloned.1.call-start = ((), (), s32[]{:S(2)}) async-start(), calls=%async_computation.17 | async-start | bytes 1081344
  1433.1 37.6 %copy-start.18 = (f32[576]{0:T(1024)S(1)}, f32[576]{0:T(1024)}, u32[]{:S(2)}) copy-start(f32[576]{0:T(1024)} %copy-done.17) | copy-start | bytes 6916
  1433.1 37.6 %copy-start.16 = (f32[576]{0:T(1024)S(1)}, f32[576]{0:T(1024)}, u32[]{:S(2)}) copy-start(f32[576]{0:T(1024)} %copy-done.15) | copy-start | bytes 6916
  1437.2 376.1 %copy-start.19 = (f32[2048]{0:T(1024)S(1)}, f32[2048]{0:T(1024)}, u32[]{:S(2)}) copy-start(f32[2048]{0:T(1024)} %param.26) | copy-start | bytes 24580
  1474.5 348.0 %copy-start.6 = (bf16[3,256,512]{2,1,0:T(8,128)(2,1)S(1)}, bf16[3,256,512]{2,1,0:T(8,128)(2,1)}, u32[]{:S(2)}) copy-start(bf16[3,256,512]{2,1,0:T(8,128)(2,1)} %param.20) | copy-start | bytes 2359300
  1474.5 348.9 %copy-start.21 = (f32[2048]{0:T(1024)S(1)}, f32[2048]{0:T(1024)}, u32[]{:S(2)}) copy-start(f32[2048]{0:T(1024)} %get-tuple-element.443) | copy-start | bytes 24580
  (8 other events, 12.8 us)
Sparse Core Ops, SparseCore 0:
  10.2 67.8 all-gather.8
  80.0 94.5 all-gather.6
  176.2 30.8 all-gather.10
  208.7 95.3 all-gather.16
  305.6 82.0 all-gather.12
  389.1 81.0 all-gather.14
  1279.2 188.6 all-reduce.5
  1471.5 341.7 all-reduce.3
  1816.2 37.0 reduce-scatter.9
  1855.6 68.7 reduce-scatter.7
  1926.9 87.9 reduce-scatter.11
  2017.1 87.9 reduce-scatter.13
  2107.4 133.2 reduce-scatter.15
where the time goes:
time: 2260 us; the launch traced here: 2250 us
  waiting for transfers between devices  903 us (40%)
  matrix products  798 us (35%)
  other arithmetic  263 us (12%)
  local copies, waits for them, and re-layouts  174 us (8%)
  loops' own time  50.7 us (2%)
  blocking collectives  45.8 us (2%)
    psum x1, waiting for transfers between devices, body(): lax.psum(jnp.dot(attended, out_w, preferred_element_type=jnp.float32) + j...  339 us
    unnamed x14, waiting for transfers between devices  135 us
    convert_element_type x3, other arithmetic, back_block(): grad_scores = (probs_f * (grad_probs - jnp.sum(probs_f * grad_probs, axis...  134 us
    dot_general x3, matrix products, back_block(): jnp.einsum('qhe,khe->hqk', grad_rows, values_all, preferred_element_type=...  129 us
    dynamic_update_slice x6, local copies, waits for them, and re-layouts, body(): lax.scan(back_block, (zero_heads, zero_heads), (block_starts, log_totals))  99.3 us
    all_gather x1, waiting for transfers between devices, body(): normed = lax.all_gather(normed_local, 'tensor', axis=0, tiled=True)  96.4 us
    reduce_scatter x1, waiting for transfers between devices, body(): lax.psum_scatter(grad_w_fc1.astype(jnp.bfloat16), 'dp', scatter_dimension...  87.8 us
    reduce_scatter x1, waiting for transfers between devices, body(): lax.psum_scatter(grad_w_fc2.astype(jnp.bfloat16), 'dp', scatter_dimension...  87.4 us
  transfers between devices with their start and end apart: 13, of which 9 were waited for; matrix products, arithmetic and copies ran while one was open for 51% of the time, Pallas kernels for 0%

commit v1 on v0

v1 whole, which is shorter than its diff:
```python
import jax
import jax.numpy as jnp
from jax import lax
from jax.experimental import pallas as pl
from jax.experimental.pallas import tpu as pltpu
from jax.sharding import PartitionSpec as P

HDIM = 64
ROT = 32
SEG = 128
TRUNK = 6
BRANCHES = 4
LEAVES = 2
TREE_SEGS = TRUNK + BRANCHES + BRANCHES * LEAVES
bf16 = jnp.bfloat16
f32 = jnp.float32
NEG = -1e30
rope_base = 10000.0


def dot_nn(a, b):
    return lax.dot_general(a, b, (((1,), (0,)), ((), ())), preferred_element_type=f32)


def dot_nt(a, b):
    return lax.dot_general(a, b, (((1,), (1,)), ((), ())), preferred_element_type=f32)


def rope_tables():
    seg = jnp.arange(TREE_SEGS, dtype=jnp.int32)
    depth = jnp.where(seg < TRUNK, seg, jnp.where(seg < TRUNK + BRANCHES, TRUNK, TRUNK + 1))
    pos = (depth[:, None] * SEG + jnp.arange(SEG, dtype=jnp.int32)[None, :]).reshape(-1)
    half = ROT // 2
    inverse_freq = 1.0 / rope_base ** (jnp.arange(half, dtype=f32) * (2.0 / ROT))
    angles = pos.astype(f32)[:, None] * inverse_freq[None, :]
    cos, sin = jnp.cos(angles), jnp.sin(angles)
    rows = pos.shape[0]
    ones = jnp.ones((rows, HDIM - ROT), f32)
    cos_h = jnp.concatenate([cos, cos, ones], axis=1)
    sin_h = jnp.concatenate([-sin, sin, 0.0 * ones], axis=1)
    return jnp.concatenate([cos_h, cos_h], axis=1), jnp.concatenate([sin_h, sin_h], axis=1)


def partner(x):
    lane = lax.broadcasted_iota(jnp.int32, x.shape, 1) % HDIM
    half = ROT // 2
    return jnp.where(lane < half, pltpu.roll(x, 2 * HDIM - half, 1), pltpu.roll(x, half, 1))


def attn_kernel(par, cos_ref, sin_ref, qkv_ref, do_ref, att_ref, g_ref, aux_ref,
                qs, kr, kt, vt, ot, dqt, dk, dv, s_ref, p_ref, top):
    rows = TREE_SEGS * SEG
    step = 2 * SEG
    lane_low = lax.broadcasted_iota(jnp.int32, (step, 2 * HDIM), 1) < HDIM

    @pl.loop(0, rows // step)
    def _(i):
        at = pl.ds(pl.multiple_of(i * step, step), step)
        cos, sin = cos_ref[at, :], sin_ref[at, :]
        q = qkv_ref[0, at, :].astype(f32)
        k = qkv_ref[1, at, :].astype(f32)
        v = qkv_ref[2, at, :].astype(f32)
        qs[at, :] = ((q * cos + partner(q) * sin) * (HDIM ** -0.5)).astype(bf16)
        k = k * cos + partner(k) * sin
        kr[at, :] = k.astype(bf16)
        kt[:, at] = k.T.astype(bf16)
        vt[:, at] = v.T.astype(bf16)
        dk[at, :] = jnp.zeros((step, 2 * HDIM), f32)
        dv[at, :] = jnp.zeros((step, 2 * HDIM), f32)

    top[...] = jnp.full((2, 8, step), NEG, f32)
    key_id = lax.broadcasted_iota(jnp.int32, (SEG, step), 0)
    query_id = lax.broadcasted_iota(jnp.int32, (SEG, step), 1) % SEG
    pair_mask = key_id <= query_id
    tri_mask = lax.broadcasted_iota(jnp.int32, (step, step), 0) <= lax.broadcasted_iota(
        jnp.int32, (step, step), 1)

    def seg_at(start, size):
        if isinstance(start, int):
            return pl.ds(start, size)
        return pl.ds(pl.multiple_of(start, SEG), size)

    def block(q0, q1, chunks, diag):
        halves = [seg_at(q0, SEG), seg_at(q1, SEG)]
        q_all = jnp.concatenate([qs[halves[0], :], qs[halves[1], :]], axis=0)
        do_all = jnp.concatenate([do_ref[halves[0], :], do_ref[halves[1], :]], axis=0)
        zero = jnp.zeros_like(q_all)
        pieces = []
        off = 0
        for start, size in chunks:
            pieces.append((off, start, size, 'full'))
            off += size
        if diag:
            pieces.append((off, q0, step, 'tri'))
            off += step
        else:
            pieces.append((off, None, SEG, 'pair'))
            off += SEG
        for h in range(2):
            qh = jnp.where(lane_low if h == 0 else ~lane_low, q_all, zero)
            dh = jnp.where(lane_low if h == 0 else ~lane_low, do_all, zero)

            def left(ref, piece, rhs):
                o, start, size, kind = piece
                if kind == 'pair':
                    return jnp.concatenate(
                        [dot_nt(ref[halves[i], :], rhs[i * SEG:(i + 1) * SEG]) for i in range(2)], axis=1)
                return dot_nt(ref[seg_at(start, size), :], rhs)

            m = None
            for piece in pieces:
                o, start, size, kind = piece
                s = left(kr, piece, qh)
                if kind == 'tri':
                    s = jnp.where(tri_mask, s, NEG)
                if kind == 'pair':
                    s = jnp.where(pair_mask, s, NEG)
                s_ref[h, o:o + size, :] = s
                mp = jnp.max(s.reshape(size // 8, 8, step), axis=0)
                m = mp if m is None else jnp.maximum(m, mp)
            top[h] = jnp.maximum(top[h], m)
            m = jnp.max(m, axis=0, keepdims=True)
            total = jnp.zeros((8, step), f32)
            for o, start, size, kind in pieces:
                e = jnp.exp(s_ref[h, o:o + size, :] - m)
                s_ref[h, o:o + size, :] = e
                total = total + jnp.sum(e.reshape(size // 8, 8, step), axis=0)
            inv = 1.0 / jnp.sum(total, axis=0, keepdims=True)
            delta = jnp.zeros((8, step), f32)
            o_acc = jnp.zeros((HDIM, step), f32)
            for piece in pieces:
                o, start, size, kind = piece
                p = s_ref[h, o:o + size, :] * inv
                pb = p.astype(bf16)
                if kind == 'pair':
                    o_acc = o_acc + jnp.concatenate(
                        [dot_nn(vt[h * HDIM:(h + 1) * HDIM, halves[i]], pb[:, i * SEG:(i + 1) * SEG])
                         for i in range(2)], axis=1)
                    for i in range(2):
                        dv[halves[i], :] += dot_nn(pb[:, i * SEG:(i + 1) * SEG], dh[i * SEG:(i + 1) * SEG])
                else:
                    at = seg_at(start, size)
                    o_acc = o_acc + dot_nn(vt[h * HDIM:(h + 1) * HDIM, at], pb)
                    dv[at, :] += dot_nn(pb, dh)
                s_ref[h, o:o + size, :] = p
                dp = left_v(piece, dh, halves)
                p_ref[h, o:o + size, :] = dp
                delta = delta + jnp.sum((p * dp).reshape(size // 8, 8, step), axis=0)
            delta = jnp.sum(delta, axis=0, keepdims=True)
            dq_acc = jnp.zeros((HDIM, step), f32)
            for piece in pieces:
                o, start, size, kind = piece
                ds = (s_ref[h, o:o + size, :] * (p_ref[h, o:o + size, :] - delta)).astype(bf16)
                if kind == 'pair':
                    dq_acc = dq_acc + jnp.concatenate(
                        [dot_nn(kt[h * HDIM:(h + 1) * HDIM, halves[i]], ds[:, i * SEG:(i + 1) * SEG])
                         for i in range(2)], axis=1)
                    for i in range(2):
                        dk[halves[i], :] += dot_nn(ds[:, i * SEG:(i + 1) * SEG], qh[i * SEG:(i + 1) * SEG])
                else:
                    at = seg_at(start, size)
                    dq_acc = dq_acc + dot_nn(kt[h * HDIM:(h + 1) * HDIM, at], ds)
                    dk[at, :] += dot_nn(ds, qh)
            for i in range(2):
                ot[h * HDIM:(h + 1) * HDIM, halves[i]] = o_acc[:, i * SEG:(i + 1) * SEG]
                dqt[h * HDIM:(h + 1) * HDIM, halves[i]] = dq_acc[:, i * SEG:(i + 1) * SEG]

    def left_v(piece, rhs, halves):
        o, start, size, kind = piece
        if kind == 'pair':
            return jnp.concatenate(
                [dot_nt(qkv_ref[2, halves[i], :], rhs[i * SEG:(i + 1) * SEG]) for i in range(2)], axis=1)
        return dot_nt(qkv_ref[2, seg_at(start, size), :], rhs)

    for b in range(TRUNK // 2):
        block(b * step, b * step + SEG, [(c * step, step) for c in range(b)], True)
    trunk_chunks = [(c * step, step) for c in range(TRUNK // 2)]

    @pl.loop(0, BRANCHES // 2)
    def _(i):
        start = (TRUNK + 2 * i) * SEG
        block(start, start + SEG, trunk_chunks, False)

    @pl.loop(0, BRANCHES)
    def _(i):
        branch = TRUNK + i
        first = TREE_SEGS - 1
        last = TRUNK + BRANCHES
        for leaf in range(TREE_SEGS - 1, TRUNK + BRANCHES - 1, -1):
            first = jnp.where(par[leaf] == branch, leaf, first)
        for leaf in range(TRUNK + BRANCHES, TREE_SEGS):
            last = jnp.where(par[leaf] == branch, leaf, last)
        block(first * SEG, last * SEG, trunk_chunks + [(branch * SEG, SEG)], False)

    sums = [jnp.zeros((8, 2 * HDIM), f32)] * 3

    @pl.loop(0, rows // step, init_carry=tuple(sums))
    def totals(i, carry):
        at = pl.ds(pl.multiple_of(i * step, step), step)
        cos, sin = cos_ref[at, :], sin_ref[at, :]
        att_ref[at, :] = ot[:, at].T.astype(bf16)
        dq = dqt[:, at].T * (HDIM ** -0.5)
        dkr = dk[at, :]
        parts = [dq * cos - partner(dq) * sin, dkr * cos - partner(dkr) * sin, dv[at, :]]
        out = []
        for c in range(3):
            low = parts[c].astype(bf16)
            g_ref[c, at, :] = low
            out.append(carry[c] + jnp.sum(low.astype(f32).reshape(step // 8, 8, 2 * HDIM), axis=0))
        return tuple(out)

    rows_out = [jnp.sum(t, axis=0, keepdims=True) for t in totals]
    for h in range(2):
        rows_out.append(jnp.full((1, 2 * HDIM), jnp.max(top[h]), f32))
    rows_out.append(jnp.zeros((3, 2 * HDIM), f32))
    aux_ref[0] = jnp.concatenate(rows_out, axis=0)


def attention(parents, cos, sin, qkv, grad_att):
    rows, width = grad_att.shape
    pairs = width // (2 * HDIM)
    step = 2 * SEG
    wide = 2 * HDIM
    keys = TRUNK * SEG + 2 * SEG
    blk = lambda: pl.BlockSpec((rows, wide), lambda p, par: (0, p))
    blk3 = lambda: pl.BlockSpec((3, rows, wide), lambda p, par: (0, 0, p))
    tab = lambda: pl.BlockSpec((rows, wide), lambda p, par: (0, 0))
    return pl.pallas_call(
        attn_kernel,
        out_shape=(
            jax.ShapeDtypeStruct((rows, width), bf16),
            jax.ShapeDtypeStruct((3, rows, width), bf16),
            jax.ShapeDtypeStruct((pairs, 8, wide), f32),
        ),
        grid_spec=pltpu.PrefetchScalarGridSpec(
            num_scalar_prefetch=1,
            grid=(pairs,),
            in_specs=[tab(), tab(), blk3(), blk()],
            out_specs=[blk(), blk3(), pl.BlockSpec((1, 8, wide), lambda p, par: (p, 0, 0))],
            scratch_shapes=[
                pltpu.VMEM((rows, wide), bf16),
                pltpu.VMEM((rows, wide), bf16),
                pltpu.VMEM((wide, rows), bf16),
                pltpu.VMEM((wide, rows), bf16),
                pltpu.VMEM((wide, rows), f32),
                pltpu.VMEM((wide, rows), f32),
                pltpu.VMEM((rows, wide), f32),
                pltpu.VMEM((rows, wide), f32),
                pltpu.VMEM((2, keys, step), f32),
                pltpu.VMEM((2, keys, step), f32),
                pltpu.VMEM((2, 8, step), f32),
            ],
        ),
        compiler_params=pltpu.CompilerParams(
            dimension_semantics=("arbitrary",), vmem_limit_bytes=40 << 20),
        cost_estimate=pl.CostEstimate(flops=60 * 10**9, transcendentals=17 * 10**6, bytes_accessed=24 << 20),
    )(parents, cos, sin, qkv, grad_att)


clip_tau = 10.0
norm_eps = 1e-05


def dot_tn(a, b):
    return lax.dot_general(a, b, (((0,), (0,)), ((), ())), preferred_element_type=f32)


def xor_send(x, bits, size):
    return lax.ppermute(x, "tensor", [(i, i ^ bits) for i in range(size)])


def gather_rows(x, size):
    if size != 4:
        return [x] + [xor_send(x, i, size) for i in range(1, size)]
    half = x.shape[0] // 2
    one = xor_send(x, 1, size)
    two = xor_send(x, 2, size)
    low = xor_send(two[:half], 1, size)
    high = xor_send(one[half:], 2, size)
    return [x, one, two, jnp.concatenate([low, high], axis=0)]


def scatter_sum(parts, size):
    total = parts[0].astype(f32)
    if size != 4:
        for i in range(1, size):
            total = total + xor_send(parts[i], i, size).astype(f32)
        return total
    half = parts[0].shape[0] // 2
    low = xor_send(parts[3][:half], 1, size)
    high = xor_send(parts[3][half:], 2, size)
    two = jnp.concatenate(
        [(parts[2][:half].astype(f32) + low.astype(f32)).astype(bf16), parts[2][half:]], axis=0)
    one = jnp.concatenate(
        [parts[1][:half], (parts[1][half:].astype(f32) + high.astype(f32)).astype(bf16)], axis=0)
    return total + xor_send(one, 1, size).astype(f32) + xor_send(two, 2, size).astype(f32)


def norm_parts(rows_in):
    row_mean = jnp.mean(rows_in, axis=-1, keepdims=True)
    centred = rows_in - row_mean
    inverse = lax.rsqrt(jnp.mean(centred * centred, axis=-1, keepdims=True) + norm_eps)
    return centred * inverse, inverse


def gelu_tanh(values_in):
    return jax.nn.gelu(values_in, approximate=True)


def body(
    tokens,
    cotangent,
    ln_gain,
    ln_bias,
    w_qkv,
    b_qkv,
    w_out,
    w_fc1,
    b_fc1,
    w_fc2,
    resid_bias,
    parents,
):
    size = lax.axis_size("tensor")
    groups = lax.axis_size("dp")
    local_rows, model = tokens.shape
    total_rows = local_rows * size
    me = lax.axis_index("tensor")
    width = w_qkv.shape[2]
    heads = width // HDIM

    def to_tree(parts):
        out = jnp.zeros((total_rows,) + parts[0].shape[1:], parts[0].dtype)
        for i, part in enumerate(parts):
            out = lax.dynamic_update_slice_in_dim(out, part, (me ^ i) * local_rows, 0)
        return out

    def from_tree(x):
        return [
            lax.dynamic_slice_in_dim(x, (me ^ i) * local_rows, local_rows, 0) for i in range(size)
        ]

    cos, sin = rope_tables()
    tokens_f = tokens.astype(f32)
    xhat, inverse = norm_parts(tokens_f)
    normed_local = (xhat * ln_gain + ln_bias).astype(bf16)
    qkv_w = lax.all_gather(w_qkv, "dp", axis=1, tiled=True)
    out_w = lax.all_gather(w_out, "dp", axis=1, tiled=True)
    up_w = lax.all_gather(w_fc1, "dp", axis=0, tiled=True)
    down_w = lax.all_gather(w_fc2, "dp", axis=1, tiled=True)
    normed = to_tree(gather_rows(normed_local, size))
    cot_full = to_tree(gather_rows(cotangent, size))

    projected = (
        jnp.einsum("td,cdh->cth", normed, qkv_w, preferred_element_type=f32) + b_qkv[:, None, :]
    ).astype(bf16)
    grad_attended = dot_nt(cot_full, out_w).astype(bf16)
    attended, grad_qkv, aux = attention(parents[0], cos, sin, projected, grad_attended)
    grad_b_qkv = jnp.transpose(aux[:, :3], (1, 0, 2)).reshape(-1)
    tops = aux[:, 3:5, 0].reshape(-1)

    hidden_pre = dot_nn(normed, up_w) + b_fc1
    activated = gelu_tanh(hidden_pre).astype(bf16)
    hidden_low = hidden_pre.astype(bf16)
    grad_w_out = dot_tn(attended, cot_full).astype(bf16)
    grad_w_qkv = jnp.einsum("td,cth->cdh", normed, grad_qkv, preferred_element_type=f32).astype(bf16)
    grad_w_fc2 = dot_tn(activated, cot_full).astype(bf16)
    branch = (dot_nn(attended, out_w) + dot_nn(activated, down_w)).astype(bf16)
    grad_act = dot_nt(cot_full, down_w)
    ignored, gelu_back = jax.vjp(gelu_tanh, hidden_low.astype(f32))
    grad_hidden = gelu_back(grad_act)[0].astype(bf16)
    grad_w_fc1 = dot_tn(normed, grad_hidden).astype(bf16)
    grad_b_fc1 = jnp.sum(grad_hidden.astype(f32), axis=0)
    normed_part = (
        jnp.einsum("cth,cdh->td", grad_qkv, qkv_w, preferred_element_type=f32)
        + dot_nt(grad_hidden, up_w)
    ).astype(bf16)

    summed_fc2 = lax.psum_scatter(grad_w_fc2, "dp", scatter_dimension=1, tiled=True).astype(f32)
    summed_qkv = lax.psum_scatter(grad_w_qkv, "dp", scatter_dimension=1, tiled=True).astype(f32)
    summed_out = lax.psum_scatter(grad_w_out, "dp", scatter_dimension=1, tiled=True).astype(f32)
    summed_fc1 = lax.psum_scatter(grad_w_fc1, "dp", scatter_dimension=0, tiled=True).astype(f32)

    branch_sum = scatter_sum(from_tree(branch), size)
    output_rows = (tokens_f + branch_sum + resid_bias).astype(bf16)

    small = jnp.concatenate([grad_b_qkv, grad_b_fc1, tops])
    small_all = lax.all_gather(small[None], "dp", axis=0, tiled=True)
    small_sum = jnp.sum(small_all[:, : -heads], axis=0)
    bias_qkv = small_sum[: 3 * width].reshape(3, width)
    bias_fc1 = small_sum[3 * width :]
    head_top = jnp.max(small_all[:, -heads:], axis=0)
    factor = jnp.sqrt(clip_tau / jnp.maximum(head_top, clip_tau))
    clipped_qk = (w_qkv[:2].astype(f32) * jnp.repeat(factor, HDIM)[None, None, :]).astype(bf16)

    grad_normed = scatter_sum(from_tree(normed_part), size)
    grad_xhat = grad_normed * ln_gain
    cot_local = cotangent.astype(f32)
    input_grad = cot_local + inverse * (
        grad_xhat
        - jnp.mean(grad_xhat, axis=-1, keepdims=True)
        - xhat * jnp.mean(grad_xhat * xhat, axis=-1, keepdims=True)
    )
    terms = jnp.stack(
        [jnp.sum(grad_normed * xhat, axis=0), jnp.sum(grad_normed, axis=0), jnp.sum(cot_local, axis=0)]
    )
    every = size * groups
    pieces = jnp.transpose(terms.reshape(3, every, model // every), (1, 0, 2)).reshape(every, -1)
    pieces = lax.all_to_all(pieces, ("dp", "tensor"), 0, 0, tiled=True)
    grad_small = jnp.sum(pieces, axis=0).reshape(3, model // every)
    return (
        output_rows,
        input_grad,
        grad_small,
        summed_qkv,
        bias_qkv,
        summed_out,
        summed_fc1,
        bias_fc1,
        summed_fc2,
        clipped_qk,
    )


def solution(mesh):
    return jax.shard_map(
        body,
        mesh=mesh,
        in_specs=(
            P(("dp", "tensor"), None),
            P(("dp", "tensor"), None),
            P(),
            P(),
            P(None, "dp", "tensor"),
            P(None, "tensor"),
            P("tensor", "dp"),
            P("dp", "tensor"),
            P("tensor"),
            P("tensor", "dp"),
            P(),
            P("dp", None),
        ),
        out_specs=(
            P(("dp", "tensor"), None),
            P(("dp", "tensor"), None),
            P(None, ("dp", "tensor")),
            P(None, "dp", "tensor"),
            P(None, "tensor"),
            P("tensor", "dp"),
            P("dp", "tensor"),
            P("tensor"),
            P("tensor", "dp"),
            P(None, "dp", "tensor"),
        ),
        check_vma=False,
    )
```

time: 2260 us -> 750 us (0.33)
  waiting for transfers between devices: 903 us -> 200 us
  matrix products: 798 us -> 276 us
  other arithmetic: 263 us -> 51.5 us
  Pallas kernels: 0 us -> 109 us
  local copies, waits for them, and re-layouts: 174 us -> 65.9 us
  loops' own time: 50.7 us -> 0 us
  blocking collectives: 45.8 us -> 0 us
  starting transfers between devices: 0.52 us -> 27.9 us
    dot_general x33 -> x12, matrix products: 798 us -> 276 us  [the longest x3 78.3 us: dot_nt(): lax.dot_general(a, b, (((1,), (1,)), ((), ())), preferred_element_type=f32)]
    psum x2 -> x0, waiting for transfers between devices: 369 us -> none  [the longest x1 339 us: body(): lax.psum(jnp.dot(attended, out_w, preferred_element_type=jnp.float32) + j...]
    reduce_scatter x4, waiting for transfers between devices: 245 us -> 0.01 us  [the longest x1 0.01 us: body(): lax.psum_scatter(grad_w_out, 'dp', scatter_dimension=1, tiled=True)]
    ppermute x0 -> x16, waiting for transfers between devices: none -> 194 us  [xor_send(): return lax.ppermute(x, 'tensor', [(i, i ^ bits) for i in range(size)])]
    all_gather x6 -> x4, waiting for transfers between devices: 153 us -> 0.03 us  [the longest x1 0.02 us: body(): up_w = lax.all_gather(w_fc1, 'dp', axis=0, tiled=True)]
    unnamed x14 -> x10, waiting for transfers between devices: 135 us -> 2.16 us
    convert_element_type x9 -> x7, other arithmetic: 145 us -> 15.8 us  [the longest x2 6.51 us: scatter_sum(): (parts[1][half:].astype(f32) + high.astype(f32)).astype(bf16)]
    pallas_call x0 -> x1, Pallas kernels: none -> 109 us  [attention(): pl.pallas_call(attn_kernel, out_shape=(jax.ShapeDtypeStruct((rows, width)...]
  transfers between devices with their start and end apart: 13 -> 26, of which waited for: 9 -> 11; matrix products, arithmetic and copies ran while one was open for 51% -> 46% of each run, Pallas kernels for 0% -> 15%
where the time goes in v1:
time: 750 us; the launch traced here: 746 us
  matrix products  276 us (37%)
  waiting for transfers between devices  200 us (27%)
  Pallas kernels  109 us (15%)
  local copies, waits for them, and re-layouts  65.9 us (9%)
  other arithmetic  51.5 us (7%)
  starting transfers between devices  27.9 us (4%)
  between operations  15.1 us (2%)
    ppermute x16, waiting for transfers between devices, xor_send(): return lax.ppermute(x, 'tensor', [(i, i ^ bits) for i in range(size)])  194 us
    pallas_call x1, Pallas kernels, attention(): pl.pallas_call(attn_kernel, out_shape=(jax.ShapeDtypeStruct((rows, width)...  109 us
    dot_general x3, matrix products, dot_nt(): lax.dot_general(a, b, (((1,), (1,)), ((), ())), preferred_element_type=f32)  78.3 us
    dot_general x3, matrix products, dot_nn(): lax.dot_general(a, b, (((1,), (0,)), ((), ())), preferred_element_type=f32)  68.4 us
    dot_general x3, matrix products, dot_tn(): lax.dot_general(a, b, (((0,), (0,)), ((), ())), preferred_element_type=f32)  66.8 us
    ppermute x16, starting transfers between devices, xor_send(): return lax.ppermute(x, 'tensor', [(i, i ^ bits) for i in range(size)])  21.7 us
    dot_general x1, matrix products, body(): jnp.einsum('cth,cdh->td', grad_qkv, qkv_w, preferred_element_type=f32)  21.2 us
    dot_general x1, matrix products, body(): jnp.einsum('td,cth->cdh', normed, grad_qkv, preferred_element_type=f32)  20.7 us
  transfers between devices with their start and end apart: 26, of which 11 were waited for; matrix products, arithmetic and copies ran while one was open for 46% of the time, Pallas kernels for 15%

profile of v1, /device:TPU:0, one launch (start us, length us, event | category | flops | bytes accessed | tf_op | source)
XLA Modules:
  0.0 745.9 jit_solution(5904016241918394685)
XLA Ops:
  16.0 3.7 copy-done.7
  25.0 5.4 multiply_sine_fusion
  30.4 44.6 %collective-permute-done = bf16[576,2048]{1,0:T(8,128)(2,1)} collective-permute-done((bf16[576,2048]{1,0:T(8,128)(2,1)}, bf16[576,2048]{1,0:T(8,128)(2,1)}, u32[]{:S(2)}, u32[]{:S(2)}) %collective-permute-start) | collective-permute-done | bytes 2359328 | tf_op jit(solution)/shard_map/ppermute | solution.py:269
  83.4 4.8 broadcast.110.clone.1
  92.7 3.9 concatenate.32.cos_ref
  98.9 4.5 concatenate.33.sin_ref
  103.5 22.1 %collective-permute-done.4 = bf16[576,2048]{1,0:T(8,128)(2,1)} collective-permute-done((bf16[576,2048]{1,0:T(8,128)(2,1)}, bf16[576,2048]{1,0:T(8,128)(2,1)}, u32[]{:S(2)}, u32[]{:S(2)}) %collective-permute-start.4) | collective-permute-done | bytes 2359328 | tf_op jit(solution)/shard_map/ppermute | solution.py:269
  138.8 3.5 constant_dynamic-update-slice_fusion.3
  145.7 7.3 collective-permute-done.3
  156.3 20.4 %collective-permute-done.7 = bf16[288,2048]{1,0:T(8,128)(2,1)S(1)} collective-permute-done((bf16[288,2048]{1,0:T(8,128)(2,1)S(1)}, bf16[288,2048]{1,0:T(8,128)(2,1)S(1)}, u32[]{:S(2)}, u32[]{:S(2)}) %collective-permute-start.7) | collective-permute-done | bytes 1179680 | tf_op jit(solution)/shard_map/ppermute | solution.py:269
  178.3 10.5 %convolution_convert_fusion.2.do_ref = bf16[2304,512]{1,0:T(8,128)(2,1)} fusion(bf16[2304,2048]{1,0:T(8,128)(2,1)} %maximum_dynamic-update-slice_fusion.1, bf16[512,2048]{1,0:T(8,128)(2,1)} %all-gather.8.cloned.1.call-done), kind=kOutput, calls=%fused_computation.57 | convolution fusion | flops 4833017856 | bytes 13893632 | tf_op jit(solution)/shard_map/dot_general | solution.py:26
  188.8 20.5 %fusion.24.qkv_ref = bf16[3,2304,512]{2,1,0:T(8,128)(2,1)} fusion(f32[3,512]{1,0:T(4,128)S(1)} %copy-done.18, bf16[3,2048,512]{2,1,0:T(8,128)(2,1)} %all-gather.6.cloned.1.call-done, bf16[2304,2048]{1,0:T(8,128)(2,1)} %maximum_dynamic-update-slice_fusion), kind=kOutput, calls=%fused_computation.40 | convolution fusion | flops 14502592512 | bytes 22812672 | tf_op jit(solution)/shard_map/td,cdh->cth/dot_general | solution.py:355
  209.3 109.1 %shard_map.195 = (bf16[2304,512]{1,0:T(8,128)(2,1)S(1)}, bf16[3,2304,512]{2,1,0:T(8,128)(2,1)S(1)}, f32[4,8,128]{2,1,0:T(8,128)S(1)}) custom-call(s32[18]{0:T(128)S(1)} %bitcast.49, f32[2304,128]{1,0:T(8,128)S(1)} %concatenate.32.cos_ref, f32[2304,128]{1,0:T(8,128)S(1)} %concatenate.33.sin_ref, bf16[3,2304,512]{2,1,0:T(8,128)(2,1)} %fusion.24.qkv_ref, ...), custom_call_target="tpu_custom_call" | custom-call | flops 60000002048 | bytes 25165824 | tf_op jit(solution)/shard_map/pallas_call | solution.py:228
  322.9 26.4 %fusion.51 = f32[2304,2048]{1,0:T(8,128)} fusion(bf16[2304,2048]{1,0:T(8,128)(2,1)} %maximum_dynamic-update-slice_fusion, bf16[2048,2048]{1,0:T(8,128)(2,1)} %all-gather.10.cloned.1.call-done), kind=kOutput, calls=%fused_computation.105 | convolution fusion | flops 19327352832 | bytes 36700160 | tf_op jit(solution)/shard_map/dot_general | solution.py:22
  349.3 39.4 %convert_reduce_fusion = (f32[2048]{0:T(1024)S(1)}, bf16[2304,2048]{1,0:T(8,128)(2,1)}) fusion(f32[2304,2048]{1,0:T(8,128)} %fusion.51, f32[2048]{0:T(1024)S(1)} %copy-done.19, bf16[2304,2048]{1,0:T(8,128)(2,1)} %maximum_dynamic-update-slice_fusion.1, bf16[2048,2048]{1,0:T(8,128)(2,1)} %all-gather.12.cloned.1.call-done), kind=kOutput, calls=%fused_computation.24 | convolution fusion | flops 19445315584 | bytes 46153728 | tf_op jit(solution)/shard_map/dot_general | solution.py:26
  389.6 10.0 %convolution_convert_fusion.3 = bf16[512,2048]{1,0:T(8,128)(2,1)} fusion(bf16[2304,512]{1,0:T(8,128)(2,1)S(1)} %copy-done.2, bf16[2304,2048]{1,0:T(8,128)(2,1)} %maximum_dynamic-update-slice_fusion.1), kind=kOutput, calls=%fused_computation.59 | convolution fusion | flops 4832886784 | bytes 13893632 | tf_op jit(solution)/shard_map/dot_general | solution.py:265
  399.7 20.7 %convert_bitcast_fusion = bf16[3,2048,512]{1,2,0:T(8,128)(2,1)} fusion(bf16[3,2304,512]{2,1,0:T(8,128)(2,1)} %copy-done.3, bf16[2304,2048]{1,0:T(8,128)(2,1)} %maximum_dynamic-update-slice_fusion), kind=kOutput, calls=%fused_computation.37 | convolution fusion | flops 14498660352 | bytes 22806528 | tf_op jit(solution)/shard_map/td,cth->cdh/dot_general | solution.py:366
  420.5 26.4 %convolution_convert_fusion.1 = bf16[2048,2048]{1,0:T(8,128)(2,1)} fusion(bf16[2304,2048]{1,0:T(8,128)(2,1)} %maximum_dynamic-update-slice_fusion, bf16[2304,2048]{1,0:T(8,128)(2,1)} %get-tuple-element.71), kind=kOutput, calls=%fused_computation.33 | convolution fusion | flops 19331547136 | bytes 27262976 | tf_op jit(solution)/shard_map/dot_general | solution.py:265
  446.9 21.2 %fusion.52 = f32[2304,2048,1]{1,0,2:T(8,128)} fusion(bf16[3,2304,512]{2,1,0:T(8,128)(2,1)} %copy-done.3, bf16[3,2048,512]{2,1,0:T(8,128)(2,1)} %all-gather.6.cloned.1.call-done), kind=kOutput, calls=%fused_computation.106 | convolution fusion | flops 14495514624 | bytes 32243712 | tf_op jit(solution)/shard_map/cth,cdh->td/dot_general | solution.py:375
  468.1 30.5 %convolution_convert_fusion = bf16[2048,2048]{1,0:T(8,128)(2,1)} fusion(bf16[2304,2048]{1,0:T(8,128)(2,1)} %maximum_dynamic-update-slice_fusion.1, f32[2304,2048]{1,0:T(8,128)} %fusion.51, f32[2048]{0:T(1024)S(1)} %copy-done.19), kind=kOutput, calls=%fused_computation.32 | convolution fusion | flops 19378733056 | bytes 36708352 | tf_op jit(solution)/shard_map/dot_general | solution.py:265
  498.7 10.8 %fusion.50 = f32[2304,2048]{1,0:T(8,128)} fusion(bf16[2304,512]{1,0:T(8,128)(2,1)S(1)} %copy-done.2, bf16[512,2048]{1,0:T(8,128)(2,1)} %all-gather.8.cloned.1.call-done), kind=kOutput, calls=%fused_computation.104 | convolution fusion | flops 4831838208 | bytes 23330816 | tf_op jit(solution)/shard_map/dot_general | solution.py:22
  509.4 28.5 %fusion.17 = bf16[2304,2048]{1,0:T(8,128)(2,1)} fusion(f32[2304,2048,1]{1,0,2:T(8,128)} %fusion.52, bf16[2304,2048]{1,0:T(8,128)(2,1)} %get-tuple-element.71, bf16[2048,2048]{1,0:T(8,128)(2,1)} %all-gather.10.cloned.1.call-done), kind=kOutput, calls=%fused_computation.23 | convolution fusion | flops 19336790016 | bytes 46137344 | tf_op jit(solution)/shard_map/dot_general | solution.py:26
  537.9 4.3 constant_dynamic-slice_fusion.1
  544.2 31.2 %add_convert_fusion = bf16[2304,2048]{1,0:T(8,128)(2,1)} fusion(f32[2304,2048]{1,0:T(8,128)} %fusion.50, bf16[2048,2048]{1,0:T(8,128)(2,1)} %all-gather.12.cloned.1.call-done, f32[2304,2048]{1,0:T(8,128)} %fusion.51, f32[2048]{0:T(1024)S(1)} %copy-done.19), kind=kOutput, calls=%fused_computation.25 | convolution fusion | flops 19383975936 | bytes 55582720 | tf_op jit(solution)/shard_map/dot_general | solution.py:22
  575.4 4.4 constant_dynamic-slice_fusion.3
  590.3 18.7 %collective-permute-done.8 = bf16[288,2048]{1,0:T(8,128)(2,1)} collective-permute-done((bf16[288,2048]{1,0:T(8,128)(2,1)}, bf16[288,2048]{1,0:T(8,128)(2,1)}, u32[]{:S(2)}, u32[]{:S(2)}) %collective-permute-start.8) | collective-permute-done | bytes 1179680 | tf_op jit(solution)/shard_map/ppermute | solution.py:269
  622.3 37.2 %collective-permute-done.15 = bf16[576,2048]{1,0:T(8,128)(2,1)} collective-permute-done((bf16[576,2048]{1,0:T(8,128)(2,1)}, bf16[576,2048]{1,0:T(8,128)(2,1)}, u32[]{:S(2)}, u32[]{:S(2)}) %collective-permute-start.15) | collective-permute-done | bytes 2359328 | tf_op jit(solution)/shard_map/ppermute | solution.py:269
  659.9 5.3 fusion.38
  665.2 42.2 %collective-permute-done.11 = bf16[576,2048]{1,0:T(8,128)(2,1)} collective-permute-done((bf16[576,2048]{1,0:T(8,128)(2,1)}, bf16[576,2048]{1,0:T(8,128)(2,1)}, u32[]{:S(2)}, u32[]{:S(2)}) %collective-permute-start.11) | collective-permute-done | bytes 2359328 | tf_op jit(solution)/shard_map/ppermute | solution.py:269
  707.7 8.2 %convert_reduce_fusion.2 = (f32[2048]{0:T(1024)S(1)}, f32[576,2048]{1,0:T(8,128)}, bf16[576,2048]{1,0:T(8,128)(2,1)}) fusion(bf16[576,2048]{1,0:T(8,128)(2,1)} %param.13, f32[576]{0:T(1024)S(1)} %get-tuple-element.93, f32[576]{0:T(1024)S(1)} %copy-done.11, bf16[576,2048]{1,0:T(8,128)(2,1)S(1)} %copy-done.6, f32[576]{0:T(1024)S(1)} %get-tuple-element.94, ...), kind=kLoop, calls=%fused_computation.38 | loop fusion | flops 22411264 | bytes 23626756 | tf_op jit(solution)/shard_map/reduce_sum | solution.py:405
  716.9 5.7 all-to-all-start
  725.6 4.8 all-to-all-done
  (150 shorter events, 94.8 us)
Async XLA Ops:
  7.2 171.1 %all-gather.8.cloned.1.call-start = ((), (), s32[]{:S(2)}) async-start(), calls=%async_computation.6 | async-start | bytes 2359296 | tf_op jit(solution)/shard_map/all_gather | solution.py:348
  7.9 180.8 %all-gather.6.cloned.1.call-start = ((), (), s32[]{:S(2)}) async-start(), calls=%async_computation.5 | async-start | bytes 7077888 | tf_op jit(solution)/shard_map/all_gather | solution.py:347
  8.7 314.2 %all-gather.10.cloned.1.call-start = ((), (), s32[]{:S(2)}) async-start(), calls=%async_computation.7 | async-start | bytes 9437184 | tf_op jit(solution)/shard_map/all_gather | solution.py:349
  9.4 339.9 %all-gather.12.cloned.1.call-start = ((), (), s32[]{:S(2)}) async-start(), calls=%async_computation.8 | async-start | bytes 9437184 | tf_op jit(solution)/shard_map/all_gather | solution.py:350
  19.7 55.3 %collective-permute-start = (bf16[576,2048]{1,0:T(8,128)(2,1)}, bf16[576,2048]{1,0:T(8,128)(2,1)}, u32[]{:S(2)}, u32[]{:S(2)}) collective-permute-start(bf16[576,2048]{1,0:T(8,128)(2,1)} %get-tuple-element.74), channel_id=1, source_target_pairs={{0,1},{1,0},{2,3},{3,2},{4,5},{5,4},{6,7},{7,6},{8,9},{9,8},{10,11... | collective-permute-start | bytes 7077896 | tf_op jit(solution)/shard_map/ppermute | solution.py:269
  22.6 56.9 %collective-permute-start.1 = (bf16[576,2048]{1,0:T(8,128)(2,1)}, bf16[576,2048]{1,0:T(8,128)(2,1)}, u32[]{:S(2)}, u32[]{:S(2)}) collective-permute-start(bf16[576,2048]{1,0:T(8,128)(2,1)} %get-tuple-element.74), channel_id=1, source_target_pairs={{0,2},{1,3},{2,0},{3,1},{4,6},{5,7},{6,4},{7,5},{8,10},{9,11},{10,... | collective-permute-start | bytes 7077896 | tf_op jit(solution)/shard_map/ppermute | solution.py:269
  24.1 101.4 %collective-permute-start.4 = (bf16[576,2048]{1,0:T(8,128)(2,1)}, bf16[576,2048]{1,0:T(8,128)(2,1)}, u32[]{:S(2)}, u32[]{:S(2)}) collective-permute-start(bf16[576,2048]{1,0:T(8,128)(2,1)} %param.13), channel_id=1, source_target_pairs={{0,1},{1,0},{2,3},{3,2},{4,5},{5,4},{6,7},{7,6},{8,9},{9,8},{10,11... | collective-permute-start | bytes 7077896 | tf_op jit(solution)/shard_map/ppermute | solution.py:269
  24.7 104.4 %collective-permute-start.5 = (bf16[576,2048]{1,0:T(8,128)(2,1)}, bf16[576,2048]{1,0:T(8,128)(2,1)}, u32[]{:S(2)}, u32[]{:S(2)}) collective-permute-start(bf16[576,2048]{1,0:T(8,128)(2,1)} %param.13), channel_id=1, source_target_pairs={{0,2},{1,3},{2,0},{3,1},{4,6},{5,7},{6,4},{7,5},{8,10},{9,11},{10,... | collective-permute-start | bytes 7077896 | tf_op jit(solution)/shard_map/ppermute | solution.py:269
  24.7 594.5 %all-reduce.3.cloned.1.call-start = ((), (), s32[]{:S(2)}) async-start(), calls=%async_computation.13 | async-start | bytes 237568
  77.4 75.5 %collective-permute-start.3 = (bf16[288,2048]{1,0:T(8,128)(2,1)}, bf16[288,2048]{1,0:T(8,128)(2,1)}, u32[]{:S(2)}, u32[]{:S(2)}) collective-permute-start(bf16[288,2048]{1,0:T(8,128)(2,1)} %slice.104), channel_id=1, source_target_pairs={{0,2},{1,3},{2,0},{3,1},{4,6},{5,7},{6,4},{7,5},{8,10},{9,11},{10,... | collective-permute-start | bytes 3538952 | tf_op jit(solution)/shard_map/ppermute | solution.py:269
  81.9 71.0 %collective-permute-start.2 = (bf16[288,2048]{1,0:T(8,128)(2,1)}, bf16[288,2048]{1,0:T(8,128)(2,1)}, u32[]{:S(2)}, u32[]{:S(2)}) collective-permute-start(bf16[288,2048]{1,0:T(8,128)(2,1)} %slice.103), channel_id=1, source_target_pairs={{0,1},{1,0},{2,3},{3,2},{4,5},{5,4},{6,7},{7,6},{8,9},{9,8},{10,11... | collective-permute-start | bytes 3538952 | tf_op jit(solution)/shard_map/ppermute | solution.py:269
  126.9 49.7 %collective-permute-start.7 = (bf16[288,2048]{1,0:T(8,128)(2,1)S(1)}, bf16[288,2048]{1,0:T(8,128)(2,1)S(1)}, u32[]{:S(2)}, u32[]{:S(2)}) collective-permute-start(bf16[288,2048]{1,0:T(8,128)(2,1)S(1)} %slice.106), channel_id=1, source_target_pairs={{0,2},{1,3},{2,0},{3,1},{4,6},{5,7},{6,4},{7,5},{8,10},{9,11},{10,... | collective-permute-start | bytes 3538952 | tf_op jit(solution)/shard_map/ppermute | solution.py:269
  130.4 46.2 %collective-permute-start.6 = (bf16[288,2048]{1,0:T(8,128)(2,1)S(1)}, bf16[288,2048]{1,0:T(8,128)(2,1)S(1)}, u32[]{:S(2)}, u32[]{:S(2)}) collective-permute-start(bf16[288,2048]{1,0:T(8,128)(2,1)S(1)} %slice.105), channel_id=1, source_target_pairs={{0,1},{1,0},{2,3},{3,2},{4,5},{5,4},{6,7},{7,6},{8,9},{9,8},{10,11... | collective-permute-start | bytes 3538952 | tf_op jit(solution)/shard_map/ppermute | solution.py:269
  349.3 40.3 %copy-start.2 = (bf16[2304,512]{1,0:T(8,128)(2,1)S(1)}, bf16[2304,512]{1,0:T(8,128)(2,1)}, u32[]{:S(2)}) copy-start(bf16[2304,512]{1,0:T(8,128)(2,1)} %copy-done.1) | copy-start | bytes 7077892
  389.6 334.3 %reduce-scatter.7.cloned.1.call-start = ((), (), s32[]{:S(2)}) async-start(), calls=%async_computation.10 | async-start | bytes 2359296 | tf_op jit(solution)/shard_map/reduce_scatter | solution.py:381
  399.6 331.5 %reduce-scatter.5.cloned.1.call-start = ((), (), s32[]{:S(2)}) async-start(), calls=%async_computation.9 | async-start | bytes 7077888 | tf_op jit(solution)/shard_map/reduce_scatter | solution.py:380
  420.4 313.3 %reduce-scatter.9.cloned.1.call-start = ((), (), s32[]{:S(2)}) async-start(), calls=%async_computation.11 | async-start | bytes 9437184 | tf_op jit(solution)/shard_map/reduce_scatter | solution.py:382
  446.9 289.7 %reduce-scatter.11.cloned.1.call-start = ((), (), s32[]{:S(2)}) async-start(), calls=%async_computation.12 | async-start | bytes 9437184 | tf_op jit(solution)/shard_map/reduce_scatter | solution.py:379
  542.2 39.7 %collective-permute-start.12 = (bf16[288,2048]{1,0:T(8,128)(2,1)}, bf16[288,2048]{1,0:T(8,128)(2,1)}, u32[]{:S(2)}, u32[]{:S(2)}) collective-permute-start(bf16[288,2048]{1,0:T(8,128)(2,1)} %get-tuple-element.76), channel_id=1, source_target_pairs={{0,2},{1,3},{2,0},{3,1},{4,6},{5,7},{6,4},{7,5},{8,10},{9,11},{10,... | collective-permute-start | bytes 3538952 | tf_op jit(solution)/shard_map/ppermute | solution.py:269
  543.7 38.2 %collective-permute-start.14 = (bf16[288,2048]{1,0:T(8,128)(2,1)}, bf16[288,2048]{1,0:T(8,128)(2,1)}, u32[]{:S(2)}, u32[]{:S(2)}) collective-permute-start(bf16[288,2048]{1,0:T(8,128)(2,1)} %get-tuple-element.78), channel_id=1, source_target_pairs={{0,1},{1,0},{2,3},{3,2},{4,5},{5,4},{6,7},{7,6},{8,9},{9,8},{10,11... | collective-permute-start | bytes 3538952 | tf_op jit(solution)/shard_map/ppermute | solution.py:269
  579.8 29.2 %collective-permute-start.8 = (bf16[288,2048]{1,0:T(8,128)(2,1)}, bf16[288,2048]{1,0:T(8,128)(2,1)}, u32[]{:S(2)}, u32[]{:S(2)}) collective-permute-start(bf16[288,2048]{1,0:T(8,128)(2,1)} %get-tuple-element.82), channel_id=1, source_target_pairs={{0,2},{1,3},{2,0},{3,1},{4,6},{5,7},{6,4},{7,5},{8,10},{9,11},{10,... | collective-permute-start | bytes 3538952 | tf_op jit(solution)/shard_map/ppermute | solution.py:269
  580.1 29.2 %collective-permute-start.10 = (bf16[288,2048]{1,0:T(8,128)(2,1)}, bf16[288,2048]{1,0:T(8,128)(2,1)}, u32[]{:S(2)}, u32[]{:S(2)}) collective-permute-start(bf16[288,2048]{1,0:T(8,128)(2,1)} %get-tuple-element.84), channel_id=1, source_target_pairs={{0,1},{1,0},{2,3},{3,2},{4,5},{5,4},{6,7},{7,6},{8,9},{9,8},{10,11... | collective-permute-start | bytes 3538952 | tf_op jit(solution)/shard_map/ppermute | solution.py:269
  586.7 72.9 %collective-permute-start.15 = (bf16[576,2048]{1,0:T(8,128)(2,1)}, bf16[576,2048]{1,0:T(8,128)(2,1)}, u32[]{:S(2)}, u32[]{:S(2)}) collective-permute-start(bf16[576,2048]{1,0:T(8,128)(2,1)} %pad_maximum_fusion.3), channel_id=1, source_target_pairs={{0,2},{1,3},{2,0},{3,1},{4,6},{5,7},{6,4},{7,5},{8,10},{9,11},{10,... | collective-permute-start | bytes 7077896 | tf_op jit(solution)/shard_map/ppermute | solution.py:269
  589.8 70.1 %collective-permute-start.13 = (bf16[576,2048]{1,0:T(8,128)(2,1)}, bf16[576,2048]{1,0:T(8,128)(2,1)}, u32[]{:S(2)}, u32[]{:S(2)}) collective-permute-start(bf16[576,2048]{1,0:T(8,128)(2,1)} %pad_maximum_fusion.2), channel_id=1, source_target_pairs={{0,1},{1,0},{2,3},{3,2},{4,5},{5,4},{6,7},{7,6},{8,9},{9,8},{10,11... | collective-permute-start | bytes 7077896 | tf_op jit(solution)/shard_map/ppermute | solution.py:269
  612.6 47.3 %copy-start.6 = (bf16[576,2048]{1,0:T(8,128)(2,1)S(1)}, bf16[576,2048]{1,0:T(8,128)(2,1)}, u32[]{:S(2)}) copy-start(bf16[576,2048]{1,0:T(8,128)(2,1)} %param.12) | copy-start | bytes 7077892
  612.6 47.3 %copy-start.11 = (f32[576]{0:T(1024)S(1)}, f32[576]{0:T(1024)}, u32[]{:S(2)}) copy-start(f32[576]{0:T(1024)} %copy-done.10) | copy-start | bytes 6916
  612.6 47.3 %copy-start.13 = (f32[2048]{0:T(1024)S(1)}, f32[2048]{0:T(1024)}, u32[]{:S(2)}) copy-start(f32[2048]{0:T(1024)} %param.14) | copy-start | bytes 24580
  612.7 47.3 %copy-start.15 = (f32[576]{0:T(1024)S(1)}, f32[576]{0:T(1024)}, u32[]{:S(2)}) copy-start(f32[576]{0:T(1024)} %copy-done.14) | copy-start | bytes 6916
  614.2 93.2 %collective-permute-start.11 = (bf16[576,2048]{1,0:T(8,128)(2,1)}, bf16[576,2048]{1,0:T(8,128)(2,1)}, u32[]{:S(2)}, u32[]{:S(2)}) collective-permute-start(bf16[576,2048]{1,0:T(8,128)(2,1)} %pad_maximum_fusion.1), channel_id=1, source_target_pairs={{0,2},{1,3},{2,0},{3,1},{4,6},{5,7},{6,4},{7,5},{8,10},{9,11},{10,... | collective-permute-start | bytes 7077896 | tf_op jit(solution)/shard_map/ppermute | solution.py:269
  617.5 90.2 %collective-permute-start.9 = (bf16[576,2048]{1,0:T(8,128)(2,1)}, bf16[576,2048]{1,0:T(8,128)(2,1)}, u32[]{:S(2)}, u32[]{:S(2)}) collective-permute-start(bf16[576,2048]{1,0:T(8,128)(2,1)} %pad_maximum_fusion), channel_id=1, source_target_pairs={{0,1},{1,0},{2,3},{3,2},{4,5},{5,4},{6,7},{7,6},{8,9},{9,8},{10,11... | collective-permute-start | bytes 7077896 | tf_op jit(solution)/shard_map/ppermute | solution.py:269
  622.3 85.4 %copy-start.16 = (f32[2048]{0:T(1024)S(1)}, f32[2048]{0:T(1024)}, u32[]{:S(2)}) copy-start(f32[2048]{0:T(1024)} %param.22) | copy-start | bytes 24580
  716.9 13.5 %all-to-all-start = ((f32[32,1,192]{2,1,0:T(1,128)}), f32[32,1,192]{2,1,0:T(1,128)S(1)}, u32[]{:S(2)}, u32[]{:S(2)}) async-start(f32[32,1,192]{2,1,0:T(1,128)} %all_to_all.8), calls=%async_computation | async-start | bytes 65536 | tf_op jit(solution)/shard_map/all_to_all | solution.py:409
  (15 other events, 124.5 us)
Sparse Core Ops, SparseCore 0:
  9.6 33.5 all-gather.7
  44.8 63.7 all-gather.5
  110.2 80.7 all-gather.9
  192.4 81.0 all-gather.11
  389.7 52.1 all-reduce.2
  444.7 37.0 reduce-scatter.6
  484.3 68.4 reduce-scatter.4
  555.1 87.9 reduce-scatter.8
  645.6 88.4 reduce-scatter.10

commit v2 on v1

v2 whole, which is shorter than its diff:
```python
import functools

import jax
import jax.numpy as jnp
from jax import lax
from jax.experimental import pallas as pl
from jax.experimental.pallas import tpu as pltpu
from jax.sharding import PartitionSpec as P

HDIM = 64
ROT = 32
SEG = 128
TRUNK = 6
BRANCHES = 4
LEAVES = 2
TREE_SEGS = TRUNK + BRANCHES + BRANCHES * LEAVES
bf16 = jnp.bfloat16
f32 = jnp.float32
NEG = -1e30
rope_base = 10000.0


def dot_nn(a, b):
    return lax.dot_general(a, b, (((1,), (0,)), ((), ())), preferred_element_type=f32)


def dot_nt(a, b):
    return lax.dot_general(a, b, (((1,), (1,)), ((), ())), preferred_element_type=f32)


def rope_tables():
    seg = jnp.arange(TREE_SEGS, dtype=jnp.int32)
    depth = jnp.where(seg < TRUNK, seg, jnp.where(seg < TRUNK + BRANCHES, TRUNK, TRUNK + 1))
    pos = (depth[:, None] * SEG + jnp.arange(SEG, dtype=jnp.int32)[None, :]).reshape(-1)
    half = ROT // 2
    inverse_freq = 1.0 / rope_base ** (jnp.arange(half, dtype=f32) * (2.0 / ROT))
    angles = pos.astype(f32)[:, None] * inverse_freq[None, :]
    cos, sin = jnp.cos(angles), jnp.sin(angles)
    rows = pos.shape[0]
    ones = jnp.ones((rows, HDIM - ROT), f32)
    cos_h = jnp.concatenate([cos, cos, ones], axis=1)
    sin_h = jnp.concatenate([-sin, sin, 0.0 * ones], axis=1)
    return jnp.concatenate([cos_h, cos_h], axis=1), jnp.concatenate([sin_h, sin_h], axis=1)


def partner(x):
    lane = lax.broadcasted_iota(jnp.int32, x.shape, 1) % HDIM
    half = ROT // 2
    return jnp.where(lane < half, pltpu.roll(x, 2 * HDIM - half, 1), pltpu.roll(x, half, 1))


def attn_kernel(size, par, me, cos_ref, sin_ref, qkv_ref, do_in, att_ref, g_ref, aux_ref,
                qs, kr, vr, do_ref, kt, vt, dot_t, att, dqn, dk, dv, s_ref, top):
    rows = TREE_SEGS * SEG
    step = 2 * SEG
    local = rows // size
    lane_low = lax.broadcasted_iota(jnp.int32, (step, 2 * HDIM), 1) < HDIM

    def unit(n):
        return jnp.where(
            lax.broadcasted_iota(jnp.int32, (n, n), 0) == lax.broadcasted_iota(jnp.int32, (n, n), 1),
            1.0, 0.0).astype(bf16)

    unit_wide = unit(2 * HDIM)

    def places(i):
        here = pl.ds(i * local, local)
        there = pl.ds(pl.multiple_of((me[0] ^ i) * local, local), local)
        return here, there

    for i in range(size):
        here, there = places(i)
        cos, sin = cos_ref[there, :], sin_ref[there, :]
        q = qkv_ref[0, here, :].astype(f32)
        k = qkv_ref[1, here, :].astype(f32)
        qs[there, :] = ((q * cos + partner(q) * sin) * (HDIM ** -0.5)).astype(bf16)
        kr[there, :] = (k * cos + partner(k) * sin).astype(bf16)
        vr[there, :] = qkv_ref[2, here, :]
        do_ref[there, :] = do_in[here, :]

    for i in range(rows // step):
        at = pl.ds(i * step, step)
        kt[:, at] = dot_nt(unit_wide, kr[at, :]).astype(bf16)
        vt[:, at] = dot_nt(unit_wide, vr[at, :]).astype(bf16)
        dot_t[:, at] = dot_nt(unit_wide, do_ref[at, :]).astype(bf16)
        dk[at, :] = jnp.zeros((step, 2 * HDIM), f32)
        dv[at, :] = jnp.zeros((step, 2 * HDIM), f32)

    top[...] = jnp.full((2, 8, step), NEG, f32)
    key_id = lax.broadcasted_iota(jnp.int32, (SEG, step), 0)
    query_id = lax.broadcasted_iota(jnp.int32, (SEG, step), 1) % SEG
    pair_mask = key_id <= query_id
    tri_mask = lax.broadcasted_iota(jnp.int32, (step, step), 0) <= lax.broadcasted_iota(
        jnp.int32, (step, step), 1)

    def seg_at(start, size):
        if isinstance(start, int):
            return pl.ds(start, size)
        return pl.ds(pl.multiple_of(start, SEG), size)

    def block(q0, q1, chunks, diag):
        halves = [seg_at(q0, SEG), seg_at(q1, SEG)]
        q_all = jnp.concatenate([qs[halves[0], :], qs[halves[1], :]], axis=0)
        do_all = jnp.concatenate([do_ref[halves[0], :], do_ref[halves[1], :]], axis=0)
        zero = jnp.zeros_like(q_all)
        pieces = []
        off = 0
        for start, size in chunks:
            pieces.append((off, start, size, 'full'))
            off += size
        pieces.append((off, q0, step, 'tri') if diag else (off, None, SEG, 'pair'))
        both = range(2)
        qh = [jnp.where(lane_low if h == 0 else ~lane_low, q_all, zero) for h in both]
        dh = [jnp.where(lane_low if h == 0 else ~lane_low, do_all, zero) for h in both]
        q_stack = jnp.concatenate(qh, axis=0)
        d_stack = jnp.concatenate(dh, axis=0)

        def part(x, i):
            return x[i * SEG:(i + 1) * SEG]

        def lanes(x, i):
            return x[:, i * SEG:(i + 1) * SEG]

        def left(ref, piece, rhs):
            o, start, size, kind = piece
            if kind == 'pair':
                return jnp.concatenate(
                    [dot_nt(ref[halves[i], :], part(rhs, i)) for i in both], axis=1)
            return dot_nt(ref[seg_at(start, size), :], rhs)

        def turned(ref, h, piece, x):
            o, start, size, kind = piece
            rows_h = slice(h * HDIM, (h + 1) * HDIM)
            if kind == 'pair':
                return jnp.concatenate(
                    [dot_nn(ref[rows_h, halves[i]], lanes(x, i)) for i in both], axis=1)
            return dot_nn(ref[rows_h, seg_at(start, size)], x)

        def add_rows(ref, piece, xs, stack):
            o, start, size, kind = piece
            if kind == 'pair':
                for i in both:
                    ref[halves[i], :] += dot_nn(
                        jnp.concatenate([lanes(x, i) for x in xs], axis=1),
                        jnp.concatenate([part(stack, i), part(stack, 2 + i)], axis=0))
            else:
                ref[seg_at(start, size), :] += dot_nn(jnp.concatenate(xs, axis=1), stack)

        def fold(x, op):
            return op(x.reshape(x.shape[0] // 8, 8, step), axis=0)

        tops = [[], []]
        sums = [[], []]
        for piece in pieces:
            o, start, size, kind = piece
            for h in both:
                s = left(kr, piece, qh[h])
                if kind == 'tri':
                    s = jnp.where(tri_mask, s, NEG)
                if kind == 'pair':
                    s = jnp.where(pair_mask, s, NEG)
                m = fold(s, jnp.max)
                top[h] = jnp.maximum(top[h], m)
                m = jnp.max(m, axis=0, keepdims=True)
                e = jnp.exp(s - m)
                s_ref[h, o:o + size, :] = e
                tops[h].append(m)
                sums[h].append(jnp.sum(fold(e, jnp.sum), axis=0, keepdims=True))
        scales = []
        for h in both:
            m = functools.reduce(jnp.maximum, tops[h])
            w = [jnp.exp(mc - m) for mc in tops[h]]
            inv = 1.0 / sum(wc * sc for wc, sc in zip(w, sums[h]))
            scales.append([wc * inv for wc in w])
        o_acc = [jnp.zeros((HDIM, step), f32)] * 2
        for n, piece in enumerate(pieces):
            o, start, size, kind = piece
            low = []
            for h in both:
                p = s_ref[h, o:o + size, :] * scales[h][n]
                s_ref[h, o:o + size, :] = p
                low.append(p.astype(bf16))
                o_acc[h] = o_acc[h] + turned(vt, h, piece, low[h])
            add_rows(dv, piece, low, d_stack)
        deltas = []
        for h in both:
            d_turned = jnp.concatenate(
                [dot_t[h * HDIM:(h + 1) * HDIM, halves[i]] for i in both], axis=1)
            deltas.append(jnp.sum(o_acc[h] * d_turned.astype(f32), axis=0, keepdims=True))
        dq_acc = [jnp.zeros((HDIM, step), f32)] * 2
        for n, piece in enumerate(pieces):
            o, start, size, kind = piece
            low = []
            for h in both:
                dp = left(vr, piece, dh[h])
                low.append((s_ref[h, o:o + size, :] * (dp - deltas[h])).astype(bf16))
                dq_acc[h] = dq_acc[h] + turned(kt, h, piece, low[h])
            add_rows(dk, piece, low, q_stack)
        o_rows = jnp.concatenate(o_acc, axis=0).T.astype(bf16)
        dq_rows = jnp.concatenate(dq_acc, axis=0).T
        for i in both:
            att[halves[i], :] = part(o_rows, i)
            dqn[halves[i], :] = part(dq_rows, i)

    for b in range(TRUNK // 2):
        block(b * step, b * step + SEG, [(c * step, step) for c in range(b)], True)
    trunk_chunks = [(c * step, step) for c in range(TRUNK // 2)]

    @pl.loop(0, BRANCHES // 2)
    def _(i):
        start = (TRUNK + 2 * i) * SEG
        block(start, start + SEG, trunk_chunks, False)

    @pl.loop(0, BRANCHES)
    def _(i):
        branch = TRUNK + i
        first = TREE_SEGS - 1
        last = TRUNK + BRANCHES
        for leaf in range(TREE_SEGS - 1, TRUNK + BRANCHES - 1, -1):
            first = jnp.where(par[leaf] == branch, leaf, first)
        for leaf in range(TRUNK + BRANCHES, TREE_SEGS):
            last = jnp.where(par[leaf] == branch, leaf, last)
        block(first * SEG, last * SEG, trunk_chunks + [(branch * SEG, SEG)], False)

    totals = [jnp.zeros((8, 2 * HDIM), f32)] * 3
    for i in range(size):
        here, there = places(i)
        cos, sin = cos_ref[there, :], sin_ref[there, :]
        att_ref[here, :] = att[there, :]
        dq = dqn[there, :] * (HDIM ** -0.5)
        dkr = dk[there, :]
        parts = [dq * cos - partner(dq) * sin, dkr * cos - partner(dkr) * sin, dv[there, :]]
        for c in range(3):
            low = parts[c].astype(bf16)
            g_ref[c, here, :] = low
            totals[c] = totals[c] + jnp.sum(low.astype(f32).reshape(local // 8, 8, 2 * HDIM), axis=0)

    rows_out = [jnp.sum(t, axis=0, keepdims=True) for t in totals]
    for h in range(2):
        rows_out.append(jnp.full((1, 2 * HDIM), jnp.max(top[h]), f32))
    rows_out.append(jnp.zeros((3, 2 * HDIM), f32))
    aux_ref[0] = jnp.concatenate(rows_out, axis=0)


def attention(parents, me, size, cos, sin, qkv, grad_att):
    rows, width = grad_att.shape
    pairs = width // (2 * HDIM)
    step = 2 * SEG
    wide = 2 * HDIM
    keys = TRUNK * SEG + 2 * SEG
    blk = lambda: pl.BlockSpec((rows, wide), lambda p, par, me: (0, p))
    blk3 = lambda: pl.BlockSpec((3, rows, wide), lambda p, par, me: (0, 0, p))
    tab = lambda: pl.BlockSpec((rows, wide), lambda p, par, me: (0, 0))
    return pl.pallas_call(
        functools.partial(attn_kernel, size),
        out_shape=(
            jax.ShapeDtypeStruct((rows, width), bf16),
            jax.ShapeDtypeStruct((3, rows, width), bf16),
            jax.ShapeDtypeStruct((pairs, 8, wide), f32),
        ),
        grid_spec=pltpu.PrefetchScalarGridSpec(
            num_scalar_prefetch=2,
            grid=(pairs,),
            in_specs=[tab(), tab(), blk3(), blk()],
            out_specs=[blk(), blk3(), pl.BlockSpec((1, 8, wide), lambda p, par, me: (p, 0, 0))],
            scratch_shapes=[
                pltpu.VMEM((rows, wide), bf16),
                pltpu.VMEM((rows, wide), bf16),
                pltpu.VMEM((rows, wide), bf16),
                pltpu.VMEM((rows, wide), bf16),
                pltpu.VMEM((wide, rows), bf16),
                pltpu.VMEM((wide, rows), bf16),
                pltpu.VMEM((wide, rows), bf16),
                pltpu.VMEM((rows, wide), bf16),
                pltpu.VMEM((rows, wide), f32),
                pltpu.VMEM((rows, wide), f32),
                pltpu.VMEM((rows, wide), f32),
                pltpu.VMEM((2, keys, step), f32),
                pltpu.VMEM((2, 8, step), f32),
            ],
        ),
        compiler_params=pltpu.CompilerParams(
            dimension_semantics=("arbitrary",), vmem_limit_bytes=40 << 20),
        cost_estimate=pl.CostEstimate(flops=60 * 10**9, transcendentals=17 * 10**6, bytes_accessed=24 << 20),
    )(parents, me, cos, sin, qkv, grad_att)


clip_tau = 10.0
norm_eps = 1e-05


def dot_tn(a, b):
    return lax.dot_general(a, b, (((0,), (0,)), ((), ())), preferred_element_type=f32)


def xor_send(x, bits, size):
    return lax.ppermute(x, "tensor", [(i, i ^ bits) for i in range(size)])


def gather_first(x, size):
    return [xor_send(x, i, size) for i in (range(1, size) if size != 4 else (1, 2))]


def gather_last(first, size):
    if size != 4:
        return first
    one, two = first
    half = one.shape[0] // 2
    low = xor_send(two[:half], 1, size)
    high = xor_send(one[half:], 2, size)
    return [one, two, low, high]


def add_low(a, b):
    return (a.astype(f32) + b.astype(f32)).astype(bf16)


def scatter_rest(parts, size):
    low, high = parts[0].astype(f32), parts[1].astype(f32)
    for i in range(1, size):
        low = low + xor_send(parts[2 * i], i, size).astype(f32)
        high = high + xor_send(parts[2 * i + 1], i, size).astype(f32)
    return [low, high]


def turn(values, *others):
    if not values:
        return values
    return list(lax.optimization_barrier(tuple(values) + others)[: len(values)])


def after(x, *others):
    return lax.optimization_barrier((x,) + others)[0]


class Carry:
    def __init__(self, sends, tag):
        self.sends, self.tag = sends, tag
        self.count = len(sends)
        self.specs = [pl.BlockSpec(memory_space=pl.ANY)] * self.count
        self.shapes = [jax.ShapeDtypeStruct(a.shape, a.dtype) for a, way in sends]
        self.arrays = [a for a, way in sends]
        self.scratch = [pltpu.SemaphoreType.DMA((2, self.count))] if sends else []

    def params(self, dims):
        extra = {"collective_id": self.tag, "has_side_effects": True} if self.sends else {}
        return pltpu.CompilerParams(
            dimension_semantics=("arbitrary",) * dims, vmem_limit_bytes=48 << 20, **extra)

    def run(self, grid, sources, targets, sems, compute):
        if not self.sends:
            compute()
            return
        at = [pl.program_id(n) for n in range(len(grid))]
        first, last = at[0] == 0, at[0] == grid[0] - 1
        for n in range(1, len(grid)):
            first, last = first & (at[n] == 0), last & (at[n] == grid[n] - 1)
        t = lax.axis_index("tensor")
        near = {1: t + 1 - 2 * (t % 2), 2: t + 2 - 4 * ((t // 2) % 2)}

        def copies():
            return [
                pltpu.make_async_remote_copy(
                    src_ref=sources[n],
                    dst_ref=targets[n],
                    send_sem=sems[0].at[0, n],
                    recv_sem=sems[0].at[1, n],
                    device_id={"tensor": near[way]},
                    device_id_type=pl.DeviceIdType.MESH,
                )
                for n, (a, way) in enumerate(self.sends)
            ]

        @pl.when(first)
        def _():
            barrier = pltpu.get_barrier_semaphore()
            for way in (1, 2):
                pl.semaphore_signal(
                    barrier, inc=1, device_id={"tensor": near[way]},
                    device_id_type=pl.DeviceIdType.MESH)
            pl.semaphore_wait(barrier, 2)
            for copy in copies():
                copy.start()

        compute()

        @pl.when(last)
        def _():
            for copy in copies():
                copy.wait()


def hint():
    return pl.CostEstimate(flops=10**10, transcendentals=0, bytes_accessed=2 << 20)


def chunk_matmul(pairs, columns, tile, count, starts, carry):
    x0 = pairs[0][0]
    local = x0.shape[-2] // count
    blocks = len(starts)
    x_specs, w_specs = [], []
    slope_of = (starts[-1] - starts[0]) // max(blocks - 1, 1)
    at = lambda i: starts[0] + slope_of * i
    for x, w, c in pairs:
        depth = x.shape[-1]
        if c is None or c < 0:
            x_specs.append(pl.BlockSpec((local, depth), lambda j, i: (at(i), 0)))
        else:
            x_specs.append(pl.BlockSpec((None, local, depth), lambda j, i, c=c: (c, at(i), 0)))
        if c is None:
            w_specs.append(pl.BlockSpec((depth, tile), lambda j, i: (0, j)))
        elif c < 0:
            w_specs.append(pl.BlockSpec((tile, depth), lambda j, i: (j, 0)))
        else:
            w_specs.append(pl.BlockSpec((None, tile, depth), lambda j, i, c=c: (c, j, 0)))
    terms = len(pairs)
    grid = (columns // tile, blocks)
    half = local // 2

    def kernel(*refs):
        ins = refs[: 2 * terms]
        sources = refs[2 * terms : 2 * terms + carry.count]
        outs = refs[2 * terms + carry.count :]
        targets, sems = outs[2 * blocks : 2 * blocks + carry.count], outs[2 * blocks + carry.count :]

        def compute():
            acc = None
            for n in range(terms):
                dot = dot_nn if pairs[n][2] is None else dot_nt
                term = dot(ins[n][...], ins[terms + n][...])
                acc = term if acc is None else acc + term
            low = acc.astype(bf16)
            for i in range(blocks):
                @pl.when(pl.program_id(1) == i)
                def _(i=i):
                    outs[2 * i][...] = low[:half]
                    outs[2 * i + 1][...] = low[half:]

        carry.run(grid, sources, targets, sems, compute)

    outs = pl.pallas_call(
        kernel,
        grid=grid,
        in_specs=x_specs + w_specs + carry.specs,
        out_specs=[pl.BlockSpec((half, tile), lambda j, i: (0, j))] * (2 * blocks) + carry.specs,
        out_shape=[jax.ShapeDtypeStruct((half, columns), bf16)] * (2 * blocks) + carry.shapes,
        scratch_shapes=carry.scratch,
        compiler_params=carry.params(2),
        cost_estimate=hint(),
    )(*[p[0] for p in pairs], *[p[1] for p in pairs], *carry.arrays)
    pieces = {}
    for n, b in enumerate(starts):
        pieces[2 * b], pieces[2 * b + 1] = outs[2 * n], outs[2 * n + 1]
    return pieces, list(outs[2 * blocks :])


def weight_grad(x, y, m_tile, n_tile, carry):
    rows, m = x.shape
    n = y.shape[-1]
    if y.ndim == 3:
        grid = (y.shape[0], m // m_tile, n // n_tile)
        y_spec = pl.BlockSpec((None, rows, n_tile), lambda c, i, j: (c, 0, j))
        o_spec = pl.BlockSpec((None, m_tile, n_tile), lambda c, i, j: (c, i, j))
        shape = (y.shape[0], m, n)
    else:
        grid = (1, m // m_tile, n // n_tile)
        y_spec = pl.BlockSpec((rows, n_tile), lambda c, i, j: (0, j))
        o_spec = pl.BlockSpec((m_tile, n_tile), lambda c, i, j: (i, j))
        shape = (m, n)

    def kernel(x_ref, y_ref, *refs):
        sources, (o_ref, *rest) = refs[: carry.count], refs[carry.count :]
        targets, sems = rest[: carry.count], rest[carry.count :]

        def compute():
            o_ref[...] = dot_tn(x_ref[...], y_ref[...]).astype(bf16)

        carry.run(grid, sources, targets, sems, compute)

    outs = pl.pallas_call(
        kernel,
        grid=grid,
        in_specs=[pl.BlockSpec((rows, m_tile), lambda c, i, j: (0, i)), y_spec] + carry.specs,
        out_specs=[o_spec] + carry.specs,
        out_shape=[jax.ShapeDtypeStruct(shape, bf16)] + carry.shapes,
        scratch_shapes=carry.scratch,
        compiler_params=carry.params(3),
        cost_estimate=hint(),
    )(x, y, *carry.arrays)
    return outs[0], list(outs[1:])


def hidden_grad(cot, down_w, slope, r_tile, f_tile, carry):
    rows, model = cot.shape
    ff = down_w.shape[0]
    grid = (ff // f_tile, rows // r_tile)

    def kernel(c_ref, w_ref, s_ref, *refs):
        sources, (g_ref, b_ref, *rest) = refs[: carry.count], refs[carry.count :]
        targets, sems = rest[: carry.count], rest[carry.count :]

        def compute():
            low = (dot_nt(c_ref[...], w_ref[...]) * s_ref[...].astype(f32)).astype(bf16)
            g_ref[...] = low
            part = jnp.sum(low.astype(f32).reshape(r_tile // 8, 8, f_tile), axis=0)

            @pl.when(pl.program_id(1) == 0)
            def _():
                b_ref[...] = part

            @pl.when(pl.program_id(1) > 0)
            def _():
                b_ref[...] += part

        carry.run(grid, sources, targets, sems, compute)

    outs = pl.pallas_call(
        kernel,
        grid=grid,
        in_specs=[
            pl.BlockSpec((r_tile, model), lambda j, i: (i, 0)),
            pl.BlockSpec((f_tile, model), lambda j, i: (j, 0)),
            pl.BlockSpec((r_tile, f_tile), lambda j, i: (i, j)),
        ] + carry.specs,
        out_specs=[
            pl.BlockSpec((r_tile, f_tile), lambda j, i: (i, j)),
            pl.BlockSpec((8, f_tile), lambda j, i: (0, j)),
        ] + carry.specs,
        out_shape=[
            jax.ShapeDtypeStruct((rows, ff), bf16),
            jax.ShapeDtypeStruct((8, ff), f32),
        ] + carry.shapes,
        scratch_shapes=carry.scratch,
        compiler_params=carry.params(2),
        cost_estimate=hint(),
    )(cot, down_w, slope, *carry.arrays)
    return outs[0], jnp.sum(outs[1], axis=0), list(outs[2:])


def dp_totals(sums, tops, groups, start):
    step = 1
    sums, tops = turn([sums, tops], start)
    while step < groups:
        way = [(i, i ^ step) for i in range(groups)]
        both = jnp.concatenate([sums, jnp.zeros((1, 128), f32).at[0, : tops.shape[0]].set(tops)], axis=0)
        other = lax.ppermute(both, "dp", way)
        sums = sums + other[:-1]
        tops = jnp.maximum(tops, other[-1, : tops.shape[0]])
        step *= 2
    return sums, tops


def norm_parts(rows_in):
    row_mean = jnp.mean(rows_in, axis=-1, keepdims=True)
    centred = rows_in - row_mean
    inverse = lax.rsqrt(jnp.mean(centred * centred, axis=-1, keepdims=True) + norm_eps)
    return centred * inverse, inverse


def gelu_parts(v):
    scale = (2.0 / jnp.pi) ** 0.5
    square = v * v
    t = jnp.tanh(scale * (v + 0.044715 * v * square))
    half = 0.5 * (1.0 + t)
    slope = half + 0.5 * v * (1.0 - t * t) * (scale * (1.0 + (3 * 0.044715) * square))
    return v * half, slope


def body(
    tokens,
    cotangent,
    ln_gain,
    ln_bias,
    w_qkv,
    b_qkv,
    w_out,
    w_fc1,
    b_fc1,
    w_fc2,
    resid_bias,
    parents,
):
    size = lax.axis_size("tensor")
    groups = lax.axis_size("dp")
    local_rows, model = tokens.shape
    total_rows = local_rows * size
    me = lax.axis_index("tensor")
    width = w_qkv.shape[2]
    heads = width // HDIM

    cos, sin = rope_tables()
    tokens_f = tokens.astype(f32)
    xhat, inverse = norm_parts(tokens_f)
    normed_local = (xhat * ln_gain + ln_bias).astype(bf16)
    up_w = lax.all_gather(w_fc1, "dp", axis=0, tiled=True)
    qkv_w = lax.all_gather(w_qkv, "dp", axis=1, tiled=True)
    out_w = lax.all_gather(w_out, "dp", axis=1, tiled=True)
    down_w = lax.all_gather(w_fc2, "dp", axis=1, tiled=True)
    normed_first = gather_first(normed_local, size)
    normed_parts = gather_last(normed_first, size)
    normed = jnp.concatenate([normed_local] + normed_parts, axis=0)
    cot_first = gather_first(after(cotangent, normed_first[0]), size)
    normed, cos, sin = lax.optimization_barrier((normed, cos, sin))

    hidden_pre = dot_nn(normed, up_w) + b_fc1
    activated, slope = gelu_parts(hidden_pre)
    activated, slope = lax.optimization_barrier((activated.astype(bf16), slope.astype(bf16)))
    cot_first = turn(cot_first, activated)
    cot_parts = gather_last(cot_first, size)
    projected = (
        jnp.einsum("td,cdh->cth", after(normed, activated, *cot_first), qkv_w, preferred_element_type=f32)
        + b_qkv[:, None, :]
    ).astype(bf16)
    cot_parts = turn(cot_parts, projected)
    cot_full = jnp.concatenate([cotangent] + cot_parts, axis=0)
    grad_w_fc2 = dot_tn(activated, cot_full).astype(bf16)
    summed_fc2 = lax.psum_scatter(grad_w_fc2, "dp", scatter_dimension=1, tiled=True)
    grad_attended = dot_nt(after(cot_full, grad_w_fc2), out_w).astype(bf16)
    attended, grad_qkv, aux = attention(
        parents[0], me[None], size, cos, sin, projected, grad_attended)
    grad_b_qkv = jnp.transpose(aux[:, :3], (1, 0, 2)).reshape(-1)
    tops = aux[:, 3:5, 0].reshape(-1)

    four = size == 4
    none = lambda: Carry([], 0)
    backs = [(grad_qkv, qkv_w, c) for c in range(3)]
    everyone = tuple(range(size - 1, -1, -1))
    far, near = everyone[0::2], everyone[1::2]
    half_rows = model // 2
    grad_w_out = dot_tn(attended, cot_full).astype(bf16)
    summed_out = lax.psum_scatter(grad_w_out, "dp", scatter_dimension=1, tiled=True)
    branch, ignored = chunk_matmul(
        [(after(attended, grad_w_out), out_w, None), (activated, down_w, None)],
        model, half_rows, size, everyone, none())
    grad_w_qkv, got = weight_grad(
        after(normed, branch[0]), grad_qkv, half_rows, width,
        Carry([(branch[6], 1), (branch[7], 2)], 0) if four else none())
    summed_qkv = lax.psum_scatter(grad_w_qkv, "dp", scatter_dimension=1, tiled=True)
    branch_next = [add_low(branch[3], got[1]), add_low(branch[4], got[0])] if four else []
    grad_hidden, grad_b_fc1, got = hidden_grad(
        after(cot_full, grad_w_qkv, *branch_next), down_w, slope, local_rows, half_rows,
        Carry([(branch[2], 1), (branch[5], 2)], 1) if four else none())
    sums = jnp.concatenate([grad_b_qkv, grad_b_fc1]).reshape(-1, 128)
    normed_part, more = chunk_matmul(
        backs + [(after(grad_hidden, summed_fc2), up_w, -1)], model, half_rows, size, far,
        Carry([(branch_next[0], 1), (branch_next[1], 2)], 2) if four else none())
    sums, tops = dp_totals(sums, tops, groups, normed_part[2 * far[0]])
    if four:
        branch_sum = [
            branch[0].astype(f32) + got[0].astype(f32) + more[1].astype(f32),
            branch[1].astype(f32) + more[0].astype(f32) + got[1].astype(f32)]
    else:
        branch_sum = scatter_rest(branch, size)
    output_rows = (tokens_f + jnp.concatenate(branch_sum, axis=0) + resid_bias).astype(bf16)
    grad_w_fc1, got = weight_grad(
        after(normed, normed_part[2 * far[0]], summed_out), grad_hidden, half_rows, half_rows,
        Carry([(normed_part[6], 1), (normed_part[7], 2)], 3) if four else none())
    summed_fc1 = lax.psum_scatter(grad_w_fc1, "dp", scatter_dimension=0, tiled=True)
    late, more = chunk_matmul(
        backs + [(after(grad_hidden, grad_w_fc1, output_rows), up_w, -1)],
        model, half_rows, size, near,
        Carry([(normed_part[2], 1)], 4) if four else none())
    normed_part |= late
    if four:
        one = xor_send(add_low(normed_part[3], got[1]), 1, size).astype(f32)
        two = xor_send(add_low(normed_part[4], got[0]), 2, size).astype(f32)
        side = xor_send(normed_part[5], 2, size).astype(f32)
        grad_normed = [
            normed_part[0].astype(f32) + more[0].astype(f32) + two,
            normed_part[1].astype(f32) + one + side]
    else:
        grad_normed = scatter_rest(normed_part, size)
    grad_normed = jnp.concatenate(grad_normed, axis=0)
    summed_fc1, summed_out, summed_qkv, summed_fc2 = (
        w.astype(f32) for w in (summed_fc1, summed_out, summed_qkv, summed_fc2))

    sums = sums.reshape(-1)
    bias_qkv = sums[: 3 * width].reshape(3, width)
    bias_fc1 = sums[3 * width :]
    head_top = tops
    factor = jnp.sqrt(clip_tau / jnp.maximum(head_top, clip_tau))
    clipped_qk = (w_qkv[:2].astype(f32) * jnp.repeat(factor, HDIM)[None, None, :]).astype(bf16)

    grad_xhat = grad_normed * ln_gain
    cot_local = cotangent.astype(f32)
    input_grad = cot_local + inverse * (
        grad_xhat
        - jnp.mean(grad_xhat, axis=-1, keepdims=True)
        - xhat * jnp.mean(grad_xhat * xhat, axis=-1, keepdims=True)
    )
    terms = jnp.stack(
        [jnp.sum(grad_normed * xhat, axis=0), jnp.sum(grad_normed, axis=0), jnp.sum(cot_local, axis=0)]
    )
    every = size * groups
    pieces = jnp.transpose(terms.reshape(3, every, model // every), (1, 0, 2)).reshape(every, -1)
    pieces = lax.all_to_all(pieces, ("dp", "tensor"), 0, 0, tiled=True)
    grad_small = jnp.sum(pieces, axis=0).reshape(3, model // every)
    return (
        output_rows,
        input_grad,
        grad_small,
        summed_qkv,
        bias_qkv,
        summed_out,
        summed_fc1,
        bias_fc1,
        summed_fc2,
        clipped_qk,
    )


def solution(mesh):
    return jax.shard_map(
        body,
        mesh=mesh,
        in_specs=(
            P(("dp", "tensor"), None),
            P(("dp", "tensor"), None),
            P(),
            P(),
            P(None, "dp", "tensor"),
            P(None, "tensor"),
            P("tensor", "dp"),
            P("dp", "tensor"),
            P("tensor"),
            P("tensor", "dp"),
            P(),
            P("dp", None),
        ),
        out_specs=(
            P(("dp", "tensor"), None),
            P(("dp", "tensor"), None),
            P(None, ("dp", "tensor")),
            P(None, "dp", "tensor"),
            P(None, "tensor"),
            P("tensor", "dp"),
            P("dp", "tensor"),
            P("tensor"),
            P("tensor", "dp"),
            P(None, "dp", "tensor"),
        ),
        check_vma=False,
    )
```

time: 750 us -> 638 us (0.85)
  matrix products: 276 us -> 100 us
  Pallas kernels: 109 us -> 273 us
  waiting for transfers between devices: 200 us -> 103 us
    pallas_call x1 -> x7, Pallas kernels: 109 us -> 273 us  [the longest x3 94.7 us: chunk_matmul(): pl.pallas_call(kernel, grid=grid, in_specs=x_specs + w_specs + carry.spec...]
    ppermute x16 -> x11, waiting for transfers between devices: 194 us -> 94.7 us  [xor_send(): return lax.ppermute(x, 'tensor', [(i, i ^ bits) for i in range(size)])]
    dot_general x3 -> x1, matrix products: 78.3 us -> 9.52 us  [dot_nt(): lax.dot_general(a, b, (((1,), (1,)), ((), ())), preferred_element_type=f32)]
    dot_general x3 -> x1, matrix products: 62.4 us -> 20.8 us  [body(): jnp.einsum('td,cdh->cth', after(normed, activated, *cot_first), qkv_w, pr...]
    dot_general x3 -> x2, matrix products: 66.8 us -> 33.4 us  [dot_tn(): lax.dot_general(a, b, (((0,), (0,)), ((), ())), preferred_element_type=f32)]
    dot_general x3 -> x1, matrix products: 68.4 us -> 36.7 us  [dot_nn(): lax.dot_general(a, b, (((1,), (0,)), ((), ())), preferred_element_type=f32)]
    unnamed x45 -> x103, local copies, waits for them, and re-layouts: 11.9 us -> 35.1 us
    dynamic_update_slice x5 -> x0, local copies, waits for them, and re-layouts: 17 us -> none  [to_tree(): out = lax.dynamic_update_slice_in_dim(out, part, (me ^ i) * local_rows, 0)]
  transfers between devices with their start and end apart: 26 -> 23, of which waited for: 11 -> 8; matrix products, arithmetic and copies ran while one was open for 46% -> 32% of each run, Pallas kernels for 15% -> 43%
where the time goes in v2:
time: 638 us; the launch traced here: 634 us
  Pallas kernels  273 us (43%)
  waiting for transfers between devices  103 us (16%)
  matrix products  100 us (16%)
  local copies, waits for them, and re-layouts  65.1 us (10%)
  other arithmetic  55 us (9%)
  starting transfers between devices  22.5 us (4%)
  between operations  14.9 us (2%)
    ppermute x11, waiting for transfers between devices, xor_send(): return lax.ppermute(x, 'tensor', [(i, i ^ bits) for i in range(size)])  94.7 us
    pallas_call x3, Pallas kernels, chunk_matmul(): pl.pallas_call(kernel, grid=grid, in_specs=x_specs + w_specs + carry.spec...  94.7 us
    pallas_call x1, Pallas kernels, attention(): pl.pallas_call(functools.partial(attn_kernel, size), out_shape=(jax.Shape...  93.3 us
    pallas_call x2, Pallas kernels, weight_grad(): pl.pallas_call(kernel, grid=grid, in_specs=[pl.BlockSpec((rows, m_tile),...  56.9 us
    dot_general x1, matrix products, dot_nn(): lax.dot_general(a, b, (((1,), (0,)), ((), ())), preferred_element_type=f32)  36.7 us
    unnamed x103, local copies, waits for them, and re-layouts  35.1 us
    dot_general x2, matrix products, dot_tn(): lax.dot_general(a, b, (((0,), (0,)), ((), ())), preferred_element_type=f32)  33.4 us
    pallas_call x1, Pallas kernels, hidden_grad(): pl.pallas_call(kernel, grid=grid, in_specs=[pl.BlockSpec((r_tile, model),...  28.3 us
  transfers between devices with their start and end apart: 23, of which 8 were waited for; matrix products, arithmetic and copies ran while one was open for 32% of the time, Pallas kernels for 43%

profile of v2, /device:TPU:0, one launch (start us, length us, event | category | flops | bytes accessed | tf_op | source)
XLA Modules:
  0.0 634.5 jit_solution(15081596637781178144)
XLA Ops:
  20.5 49.5 %collective-permute-done.1 = bf16[576,2048]{1,0:T(8,128)(2,1)S(1)} collective-permute-done((bf16[576,2048]{1,0:T(8,128)(2,1)}, bf16[576,2048]{1,0:T(8,128)(2,1)S(1)}, u32[]{:S(2)}, u32[]{:S(2)}) %collective-permute-start.1) | collective-permute-done | bytes 2359328 | tf_op jit(solution)/shard_map/ppermute | solution.py:297
  76.8 5.4 multiply_sine_fusion
  83.3 3.8 concatenate.42.cos_ref
  88.2 4.6 concatenate.43.sin_ref
  92.8 3.4 constant_dynamic-update-slice_fusion.9
  97.0 3.5 constant_dynamic-update-slice_fusion.3
  107.1 36.7 %add_convert_fusion = (bf16[2304,2048]{1,0:T(8,128)(2,1)}, bf16[2304,2048]{1,0:T(8,128)(2,1)}) fusion(f32[2048]{0:T(1024)S(1)} %copy-done.43, bf16[2304,2048]{1,0:T(8,128)(2,1)} %constant_dynamic-update-slice_fusion.x_ref, bf16[2048,2048]{1,0:T(8,128)(2,1)} %all-gather.5.cloned.1.call-done.refs_7_), kind=kOutput, calls=%fused_computation | convolution fusion | flops 19421724672 | bytes 36708352 | tf_op jit(solution)/shard_map/dot_general | solution.py:24
  143.8 9.0 %collective-permute-done.5 = bf16[576,2048]{1,0:T(8,128)(2,1)} collective-permute-done((bf16[576,2048]{1,0:T(8,128)(2,1)}, bf16[576,2048]{1,0:T(8,128)(2,1)}, u32[]{:S(2)}, u32[]{:S(2)}) %collective-permute-start.5) | collective-permute-done | bytes 2359328 | tf_op jit(solution)/shard_map/ppermute | solution.py:297
  159.7 20.8 %fusion.4.qkv_ref = bf16[3,2304,512]{2,1,0:T(8,128)(2,1)} fusion(f32[3,512]{1,0:T(4,128)S(1)} %copy-done.44, bf16[3,2048,512]{2,1,0:T(8,128)(2,1)} %all-gather.7.cloned.1.call-done.refs_4_.refs_5_.refs_6_, bf16[2304,2048]{1,0:T(8,128)(2,1)} %constant_dynamic-update-slice_fusion.x_ref), kind=kOutput, calls=%fused_computation.14 | convolution fusion | flops 14502592512 | bytes 22812672 | tf_op jit(solution)/shard_map/td,cdh->cth/dot_general | solution.py:611
  180.5 3.2 collective-permute-done.6
  184.3 3.4 constant_dynamic-update-slice_fusion.8
  187.7 3.4 constant_dynamic-update-slice_fusion.7
  194.7 26.8 %convolution_convert_fusion = bf16[2048,2048]{1,0:T(8,128)(2,1)} fusion(bf16[2304,2048]{1,0:T(8,128)(2,1)} %get-tuple-element.103.refs_1_, bf16[2304,2048]{1,0:T(8,128)(2,1)} %constant_dynamic-update-slice_fusion.5.c_ref), kind=kOutput, calls=%fused_computation.8 | convolution fusion | flops 19331547136 | bytes 27262976 | tf_op jit(solution)/shard_map/dot_general | solution.py:293
  221.6 9.5 %convolution_convert_fusion.1.do_in = bf16[2304,512]{1,0:T(8,128)(2,1)S(1)} fusion(bf16[2304,2048]{1,0:T(8,128)(2,1)} %constant_dynamic-update-slice_fusion.5.c_ref, bf16[512,2048]{1,0:T(8,128)(2,1)} %all-gather.9.cloned.1.call-done.refs_2_), kind=kOutput, calls=%fused_computation.31 | convolution fusion | flops 4833017856 | bytes 13893632 | tf_op jit(solution)/shard_map/dot_general | solution.py:28
  231.2 93.3 %shard_map.195 = (bf16[2304,512]{1,0:T(8,128)(2,1)S(1)}, bf16[3,2304,512]{2,1,0:T(8,128)(2,1)S(1)}, f32[4,8,128]{2,1,0:T(8,128)S(1)}) custom-call(s32[18]{0:T(128)S(1)} %bitcast.60, s32[1]{0:T(128)} %bitcast.1.me, f32[2304,128]{1,0:T(8,128)S(1)} %concatenate.42.cos_ref, f32[2304,128]{1,0:T(8,128)S(1)} %concatenate.43.sin_ref, ...), custom_call_target="tpu_custom_call" | custom-call | flops 60000002048 | bytes 25165824 | tf_op jit(solution)/shard_map/pallas_call | solution.py:254
  328.7 6.6 %convolution_convert_fusion.2 = bf16[512,2048]{1,0:T(8,128)(2,1)} fusion(bf16[2304,512]{1,0:T(8,128)(2,1)S(1)} %get-tuple-element.114.refs_0_, bf16[2304,2048]{1,0:T(8,128)(2,1)S(1)} %bitcast.62), kind=kOutput, calls=%fused_computation.33 | convolution fusion | flops 4832886784 | bytes 13893632 | tf_op jit(solution)/shard_map/dot_general | solution.py:293
  335.5 32.3 %shard_map.196 = (bf16[288,2048]{1,0:T(8,128)(2,1)S(1)}, bf16[288,2048]{1,0:T(8,128)(2,1)S(1)}, bf16[288,2048]{1,0:T(8,128)(2,1)S(1)}, bf16[288,2048]{1,0:T(8,12...) custom-call(bf16[2304,512]{1,0:T(8,128)(2,1)} %copy-done.19, ...), custom_call_target="tpu_custom_call" | custom-call | flops 10000000000 | bytes 2097152 | tf_op jit(solution)/shard_map/pallas_call | solution.py:441
  368.8 29.3 %shard_map.197 = (bf16[3,2048,512]{2,1,0:T(8,128)(2,1)}, bf16[288,2048]{1,0:T(8,128)(2,1)S(1)}, bf16[288,2048]{1,0:T(8,128)(2,1)S(1)}) custom-call(bf16[2304,2048]{1,0:T(8,128)(2,1)} %constant_dynamic-update-slice_fusion.x_ref, bf16[3,2304,512]{2,1,0:T(8,128)(2,1)} %copy-done, bf16[288,2048]{1,0:T(8,128)(2,1)S(1)} %get-tuple-element.118.refs_0_, ...), custom_call_target="tpu_custom_call" | custom-call | flops 10000000000 | bytes 2097152 | tf_op jit(solution)/shard_map/pallas_call | solution.py:480
  398.2 3.9 add_convert_fusion.4
  402.1 28.3 %shard_map.198 = (bf16[2304,2048]{1,0:T(8,128)(2,1)}, f32[8,2048]{1,0:T(8,128)S(1)}, bf16[288,2048]{1,0:T(8,128)(2,1)S(1)}, bf16[288,2048]{1,0:T(8,128)(2,1)S(1)}) custom-call(bf16[2304,2048]{1,0:T(8,128)(2,1)} %constant_dynamic-update-slice_fusion.5.c_ref, bf16[2048,2048]{1,0:T(8,128)(2,1)} %all-gather.11.cloned.1.call-done.refs_3_.w_ref, ...), custom_call_target="tpu_custom_call" | custom-call | flops 10000000000 | bytes 2097152 | tf_op jit(solution)/shard_map/pallas_call | solution.py:517
  433.1 28.2 %shard_map.199 = (bf16[288,2048]{1,0:T(8,128)(2,1)S(1)}, bf16[288,2048]{1,0:T(8,128)(2,1)S(1)}, bf16[288,2048]{1,0:T(8,128)(2,1)S(1)}, bf16[288,2048]{1,0:T(8,12...) custom-call(bf16[3,2304,512]{2,1,0:T(8,128)(2,1)} %copy-done, bf16[3,2304,512]{2,1,0:T(8,128)(2,1)} %copy-done, ...), custom_call_target="tpu_custom_call" | custom-call | flops 10000000000 | bytes 2097152 | tf_op jit(solution)/shard_map/pallas_call | solution.py:441
  468.1 27.6 %shard_map.200 = (bf16[2048,2048]{1,0:T(8,128)(2,1)}, bf16[288,2048]{1,0:T(8,128)(2,1)S(1)}, bf16[288,2048]{1,0:T(8,128)(2,1)S(1)}) custom-call(bf16[2304,2048]{1,0:T(8,128)(2,1)} %constant_dynamic-update-slice_fusion.x_ref, bf16[2304,2048]{1,0:T(8,128)(2,1)} %get-tuple-element.140.refs_3_.y_ref, bf16[288,2048]{1,0:T(8,128)(2,1)S(1)} %copy-done.15, ...), custom_call_target="tpu_custom_call" | custom-call | flops 10000000000 | bytes 2097152 | tf_op jit(solution)/shard_map/pallas_call | solution.py:480
  500.5 3.4 convert_add_fusion.5
  508.9 34.2 %shard_map.201 = (bf16[288,2048]{1,0:T(8,128)(2,1)S(1)}, bf16[288,2048]{1,0:T(8,128)(2,1)}, bf16[288,2048]{1,0:T(8,128)(2,1)S(1)}, bf16[288,2048]{1,0:T(8,128)(2,1)S(1)}, bf16[288,2048]{1,0:T(8,128)(2,1)S(1)}) custom-call(bf16[3,2304,512]{2,1,0:T(8,128)(2,1)} %copy-done, bf16[3,2304,512]{2,1,0:T(8,128)(2,1)} %copy-done, bf16[3,2304,512]{2,1,0:T(8,128)(2,1)} %copy-done, ...), custom_call_target="tpu_custom_call" | custom-call | flops 10000000000 | bytes 2097152 | tf_op jit(solution)/shard_map/pallas_call | solution.py:441
  562.6 11.6 %collective-permute-done.8 = bf16[288,2048]{1,0:T(8,128)(2,1)} collective-permute-done((bf16[288,2048]{1,0:T(8,128)(2,1)}, bf16[288,2048]{1,0:T(8,128)(2,1)}, u32[]{:S(2)}, u32[]{:S(2)}) %collective-permute-start.8) | collective-permute-done | bytes 1179680 | tf_op jit(solution)/shard_map/ppermute | solution.py:297
  574.2 3.3 fusion.33
  577.5 20.7 %collective-permute-done.10 = bf16[288,2048]{1,0:T(8,128)(2,1)} collective-permute-done((bf16[288,2048]{1,0:T(8,128)(2,1)}, bf16[288,2048]{1,0:T(8,128)(2,1)}, u32[]{:S(2)}, u32[]{:S(2)}) %collective-permute-start.10) | collective-permute-done | bytes 1179680 | tf_op jit(solution)/shard_map/ppermute | solution.py:297
  598.3 3.8 fusion.32
  602.2 3.7 fusion.18
  606.0 5.5 convert_reduce_fusion.1
  612.4 4.2 all-to-all-start
  617.8 6.1 all-to-all-done
  (205 shorter events, 90.3 us)
Async XLA Ops:
  7.2 99.9 %all-gather.5.cloned.1.call-start = ((), (), s32[]{:S(2)}) async-start(), calls=%async_computation.5 | async-start | bytes 9437184 | tf_op jit(solution)/shard_map/all_gather | solution.py:595
  7.9 151.8 %all-gather.7.cloned.1.call-start = ((), (), s32[]{:S(2)}) async-start(), calls=%async_computation.6 | async-start | bytes 7077888 | tf_op jit(solution)/shard_map/all_gather | solution.py:596
  8.7 213.0 %all-gather.9.cloned.1.call-start = ((), (), s32[]{:S(2)}) async-start(), calls=%async_computation.7 | async-start | bytes 2359296 | tf_op jit(solution)/shard_map/all_gather | solution.py:597
  9.4 326.0 %all-gather.11.cloned.1.call-start = ((), (), s32[]{:S(2)}) async-start(), calls=%async_computation.8 | async-start | bytes 9437184 | tf_op jit(solution)/shard_map/all_gather | solution.py:598
  15.5 54.4 %collective-permute-start.1 = (bf16[576,2048]{1,0:T(8,128)(2,1)}, bf16[576,2048]{1,0:T(8,128)(2,1)S(1)}, u32[]{:S(2)}, u32[]{:S(2)}) collective-permute-start(bf16[576,2048]{1,0:T(8,128)(2,1)} %get-tuple-element.164), channel_id=1, source_target_pairs={{0,2},{1,3},{2,0},{3,1},{4,6},{5,7},{6,4},{7,5},{8,10},{9,11},{10,... | collective-permute-start | bytes 7077896 | tf_op jit(solution)/shard_map/ppermute | solution.py:297
  18.5 54.3 %collective-permute-start = (bf16[576,2048]{1,0:T(8,128)(2,1)}, bf16[576,2048]{1,0:T(8,128)(2,1)}, u32[]{:S(2)}, u32[]{:S(2)}) collective-permute-start(bf16[576,2048]{1,0:T(8,128)(2,1)} %get-tuple-element.164), channel_id=1, source_target_pairs={{0,1},{1,0},{2,3},{3,2},{4,5},{5,4},{6,7},{7,6},{8,9},{9,8},{10,11... | collective-permute-start | bytes 7077896 | tf_op jit(solution)/shard_map/ppermute | solution.py:297
  20.0 413.1 %reduce-scatter.5.cloned.1.call-start = ((), (), s32[]{:S(2)}) async-start(), calls=%async_computation.9 | async-start | bytes 9437184 | tf_op jit(solution)/shard_map/reduce_scatter | solution.py:617
  71.1 31.0 %collective-permute-start.2 = (bf16[288,2048]{1,0:T(8,128)(2,1)}, bf16[288,2048]{1,0:T(8,128)(2,1)}, u32[]{:S(2)}, u32[]{:S(2)}) collective-permute-start(bf16[288,2048]{1,0:T(8,128)(2,1)} %slice.113), channel_id=1, source_target_pairs={{0,1},{1,0},{2,3},{3,2},{4,5},{5,4},{6,7},{7,6},{8,9},{9,8},{10,11... | collective-permute-start | bytes 3538952 | tf_op jit(solution)/shard_map/ppermute | solution.py:297
  75.2 29.4 %collective-permute-start.3 = (bf16[288,2048]{1,0:T(8,128)(2,1)}, bf16[288,2048]{1,0:T(8,128)(2,1)}, u32[]{:S(2)}, u32[]{:S(2)}) collective-permute-start(bf16[288,2048]{1,0:T(8,128)(2,1)} %slice.114), channel_id=1, source_target_pairs={{0,2},{1,3},{2,0},{3,1},{4,6},{5,7},{6,4},{7,5},{8,10},{9,11},{10,... | collective-permute-start | bytes 3538952 | tf_op jit(solution)/shard_map/ppermute | solution.py:297
  96.2 56.6 %collective-permute-start.5 = (bf16[576,2048]{1,0:T(8,128)(2,1)}, bf16[576,2048]{1,0:T(8,128)(2,1)}, u32[]{:S(2)}, u32[]{:S(2)}) collective-permute-start(bf16[576,2048]{1,0:T(8,128)(2,1)} %param.19), channel_id=1, source_target_pairs={{0,2},{1,3},{2,0},{3,1},{4,6},{5,7},{6,4},{7,5},{8,10},{9,11},{10,... | collective-permute-start | bytes 7077896 | tf_op jit(solution)/shard_map/ppermute | solution.py:297
  96.7 56.1 %collective-permute-start.4 = (bf16[576,2048]{1,0:T(8,128)(2,1)}, bf16[576,2048]{1,0:T(8,128)(2,1)}, u32[]{:S(2)}, u32[]{:S(2)}) collective-permute-start(bf16[576,2048]{1,0:T(8,128)(2,1)} %param.19), channel_id=1, source_target_pairs={{0,1},{1,0},{2,3},{3,2},{4,5},{5,4},{6,7},{7,6},{8,9},{9,8},{10,11... | collective-permute-start | bytes 7077896 | tf_op jit(solution)/shard_map/ppermute | solution.py:297
  143.8 15.9 %copy-start.44 = (f32[3,512]{1,0:T(4,128)S(1)}, f32[3,512]{1,0:T(4,128)}, u32[]{:S(2)}) copy-start(f32[3,512]{1,0:T(4,128)} %param.23) | copy-start | bytes 18436
  157.7 26.0 %collective-permute-start.6 = (bf16[288,2048]{1,0:T(8,128)(2,1)}, bf16[288,2048]{1,0:T(8,128)(2,1)S(1)}, u32[]{:S(2)}, u32[]{:S(2)}) collective-permute-start(bf16[288,2048]{1,0:T(8,128)(2,1)} %slice.99), channel_id=1, source_target_pairs={{0,1},{1,0},{2,3},{3,2},{4,5},{5,4},{6,7},{7,6},{8,9},{9,8},{10,11... | collective-permute-start | bytes 3538952 | tf_op jit(solution)/shard_map/ppermute | solution.py:297
  158.3 26.1 %collective-permute-start.7 = (bf16[288,2048]{1,0:T(8,128)(2,1)}, bf16[288,2048]{1,0:T(8,128)(2,1)}, u32[]{:S(2)}, u32[]{:S(2)}) collective-permute-start(bf16[288,2048]{1,0:T(8,128)(2,1)} %slice.100), channel_id=1, source_target_pairs={{0,2},{1,3},{2,0},{3,1},{4,6},{5,7},{6,4},{7,5},{8,10},{9,11},{10,... | collective-permute-start | bytes 3538952 | tf_op jit(solution)/shard_map/ppermute | solution.py:297
  221.5 244.0 %reduce-scatter.7.cloned.1.call-start = ((), (), s32[]{:S(2)}) async-start(), calls=%async_computation.10 | async-start | bytes 2359296 | tf_op jit(solution)/shard_map/reduce_scatter | solution.py:631
  221.6 107.1 %slice-start = ((s8[9437184]{0:T(1024)(128)(4,1)}), s8[4194304]{0:T(1024)(128)(4,1)S(1)}, s32[]{:S(2)}) async-start(s8[9437184]{0:T(1024)(128)(4,1)} %bitcast.61), calls=%async_computation.13 | async-start | bytes 8388608
  231.2 97.5 %slice-start.1 = ((s8[9437184]{0:T(1024)(128)(4,1)}), s8[4194304]{0:T(1024)(128)(4,1)S(1)}, s32[]{:S(2)}) async-start(s8[9437184]{0:T(1024)(128)(4,1)} %bitcast.61), calls=%async_computation.14 | async-start | bytes 8388608
  231.2 97.5 %slice-start.2 = ((s8[9437184]{0:T(1024)(128)(4,1)}), s8[1048576]{0:T(1024)(128)(4,1)S(1)}, s32[]{:S(2)}) async-start(s8[9437184]{0:T(1024)(128)(4,1)} %bitcast.61), calls=%async_computation.15 | async-start | bytes 2097152
  335.4 220.7 %reduce-scatter.9.cloned.1.call-start = ((), (), s32[]{:S(2)}) async-start(), calls=%async_computation.11 | async-start | bytes 7077888 | tf_op jit(solution)/shard_map/reduce_scatter | solution.py:638
  368.8 29.3 %copy-start.20 = (bf16[288,2048]{1,0:T(8,128)(2,1)}, bf16[288,2048]{1,0:T(8,128)(2,1)S(1)}, u32[]{:S(2)}) copy-start(bf16[288,2048]{1,0:T(8,128)(2,1)S(1)} %get-tuple-element.128.refs_1_) | copy-start | bytes 3538948
  398.1 226.5 %reduce-scatter.11.cloned.1.call-start = ((), (), s32[]{:S(2)}) async-start(), calls=%async_computation.12 | async-start | bytes 9437184 | tf_op jit(solution)/shard_map/reduce_scatter | solution.py:658
  508.9 38.2 %collective-permute-start.11 = (f32[29,128]{1,0:T(8,128)S(1)}, f32[29,128]{1,0:T(8,128)S(1)}, u32[]{:S(2)}, u32[]{:S(2)}) collective-permute-start(f32[29,128]{1,0:T(8,128)S(1)} %select_maximum_fusion.2), channel_id=1, source_target_pairs={{0,4},{4,0},{8,12},{12,8},{16,20},{20,16},{24,28},{28,24},{1,5},{5... | collective-permute-start | bytes 44552 | tf_op jit(solution)/shard_map/ppermute | solution.py:546
  545.0 10.3 %copy-start.33 = (bf16[512,256]{1,0:T(8,128)(2,1)S(1)}, bf16[512,256]{1,0:T(8,128)(2,1)}, u32[]{:S(2)}) copy-start(bf16[512,256]{1,0:T(8,128)(2,1)} %reduce-scatter.7.cloned.1.call-done) | copy-start | bytes 786436
  545.0 29.2 %collective-permute-start.8 = (bf16[288,2048]{1,0:T(8,128)(2,1)}, bf16[288,2048]{1,0:T(8,128)(2,1)}, u32[]{:S(2)}, u32[]{:S(2)}) collective-permute-start(bf16[288,2048]{1,0:T(8,128)(2,1)} %add_convert_fusion.3), channel_id=1, source_target_pairs={{0,2},{1,3},{2,0},{3,1},{4,6},{5,7},{6,4},{7,5},{8,10},{9,11},{10,... | collective-permute-start | bytes 3538952 | tf_op jit(solution)/shard_map/ppermute | solution.py:297
  546.5 51.8 %collective-permute-start.10 = (bf16[288,2048]{1,0:T(8,128)(2,1)}, bf16[288,2048]{1,0:T(8,128)(2,1)}, u32[]{:S(2)}, u32[]{:S(2)}) collective-permute-start(bf16[288,2048]{1,0:T(8,128)(2,1)} %get-tuple-element.149), channel_id=1, source_target_pairs={{0,2},{1,3},{2,0},{3,1},{4,6},{5,7},{6,4},{7,5},{8,10},{9,11},{10,... | collective-permute-start | bytes 3538952 | tf_op jit(solution)/shard_map/ppermute | solution.py:297
  547.7 4.4 collective-permute-start.12
  550.5 47.7 %collective-permute-start.9 = (bf16[288,2048]{1,0:T(8,128)(2,1)}, bf16[288,2048]{1,0:T(8,128)(2,1)}, u32[]{:S(2)}, u32[]{:S(2)}) collective-permute-start(bf16[288,2048]{1,0:T(8,128)(2,1)} %add_convert_fusion.2), channel_id=1, source_target_pairs={{0,1},{1,0},{2,3},{3,2},{4,5},{5,4},{6,7},{7,6},{8,9},{9,8},{10,11... | collective-permute-start | bytes 3538952 | tf_op jit(solution)/shard_map/ppermute | solution.py:297
  552.8 8.7 %collective-permute-start.13 = (f32[29,128]{1,0:T(8,128)S(1)}, f32[29,128]{1,0:T(8,128)S(1)}, u32[]{:S(2)}, u32[]{:S(2)}) collective-permute-start(f32[29,128]{1,0:T(8,128)S(1)} %select_maximum_fusion), channel_id=1, source_target_pairs={{0,16},{4,20},{8,24},{12,28},{16,0},{20,4},{24,8},{28,12},{1,17},{... | collective-permute-start | bytes 44552 | tf_op jit(solution)/shard_map/ppermute | solution.py:546
  558.7 15.5 %copy-start.4 = (bf16[288,2048]{1,0:T(8,128)(2,1)S(1)}, bf16[288,2048]{1,0:T(8,128)(2,1)}, u32[]{:S(2)}) copy-start(bf16[288,2048]{1,0:T(8,128)(2,1)} %copy-done.3) | copy-start | bytes 3538948
  558.7 15.5 %copy-start.6 = (bf16[288,2048]{1,0:T(8,128)(2,1)S(1)}, bf16[288,2048]{1,0:T(8,128)(2,1)}, u32[]{:S(2)}) copy-start(bf16[288,2048]{1,0:T(8,128)(2,1)} %copy-done.5) | copy-start | bytes 3538948
  574.2 24.0 %copy-start.2 = (bf16[288,2048]{1,0:T(8,128)(2,1)S(1)}, bf16[288,2048]{1,0:T(8,128)(2,1)}, u32[]{:S(2)}) copy-start(bf16[288,2048]{1,0:T(8,128)(2,1)} %copy-done.1) | copy-start | bytes 3538948
  612.4 11.5 %all-to-all-start = ((f32[32,1,192]{2,1,0:T(1,128)}), f32[32,1,192]{2,1,0:T(1,128)S(1)}, u32[]{:S(2)}, u32[]{:S(2)}) async-start(f32[32,1,192]{2,1,0:T(1,128)} %all_to_all.8), calls=%async_computation.2 | async-start | bytes 65536 | tf_op jit(solution)/shard_map/all_to_all | solution.py:696
  (39 other events, 130.5 us)
Sparse Core Ops, SparseCore 0:
  9.6 84.7 all-gather.4
  96.0 63.2 all-gather.6
  160.9 29.5 all-gather.8
  191.9 81.5 all-gather.10
  275.6 87.7 reduce-scatter.4
  366.2 34.1 reduce-scatter.6
  402.7 68.3 reduce-scatter.8
  495.8 89.9 reduce-scatter.10

commit v3 on v2

v3 whole, which is shorter than its diff:
```python
import functools

import jax
import jax.numpy as jnp
import numpy as np
from jax import lax
from jax.experimental import pallas as pl
from jax.experimental.pallas import tpu as pltpu
from jax.sharding import PartitionSpec as P

HDIM = 64
ROT = 32
SEG = 128
TRUNK = 6
BRANCHES = 4
LEAVES = 2
TREE_SEGS = TRUNK + BRANCHES + BRANCHES * LEAVES
bf16 = jnp.bfloat16
f32 = jnp.float32
NEG = -1e30
rope_base = 10000.0


def dot_nn(a, b):
    return lax.dot_general(a, b, (((1,), (0,)), ((), ())), preferred_element_type=f32)


def dot_nt(a, b):
    return lax.dot_general(a, b, (((1,), (1,)), ((), ())), preferred_element_type=f32)


def rope_tables():
    lane = np.arange(2 * HDIM) % HDIM
    freq = np.where(lane < ROT, rope_base ** (-2.0 * (lane % (ROT // 2)) / ROT), 0.0)
    angles = np.concatenate([np.arange(SEG), SEG * np.arange(TRUNK + 2)])[:, None] * freq[None, :]
    return np.cos(angles).astype(np.float32), np.sin(angles).astype(np.float32)


def partner(x):
    lane = lax.broadcasted_iota(jnp.int32, x.shape, 1) % HDIM
    half = ROT // 2
    return jnp.where(lane < half, pltpu.roll(x, 2 * HDIM - half, 1), pltpu.roll(x, half, 1))


def attn_kernel(size, par, me, cos_in, sin_in, qkv_ref, do_in, att_ref, g_ref, aux_ref,
                qs, kr, vr, do_ref, kt, vt, dot_t, att, dqn, dk, dv, s_ref, top, cos_ref, sin_ref):
    rows = TREE_SEGS * SEG
    step = 2 * SEG
    local = rows // size
    lane_low = lax.broadcasted_iota(jnp.int32, (step, 2 * HDIM), 1) < HDIM

    def unit(n):
        return jnp.where(
            lax.broadcasted_iota(jnp.int32, (n, n), 0) == lax.broadcasted_iota(jnp.int32, (n, n), 1),
            1.0, 0.0).astype(bf16)

    unit_wide = unit(2 * HDIM)

    def places(i):
        here = pl.ds(i * local, local)
        there = pl.ds(pl.multiple_of((me[0] ^ i) * local, local), local)
        return here, there

    @pl.when(pl.program_id(0) == 0)
    def _():
        sign = jnp.where(lax.broadcasted_iota(jnp.int32, (SEG, 2 * HDIM), 1) % HDIM < ROT // 2, -1.0, 1.0)
        cos_place, sin_place = cos_in[:SEG, :], sin_in[:SEG, :]
        for depth in range(TRUNK + 2):
            cos_seg, sin_seg = cos_in[SEG + depth : SEG + depth + 1, :], sin_in[SEG + depth : SEG + depth + 1, :]
            cos = cos_place * cos_seg - sin_place * sin_seg
            sin = (sin_place * cos_seg + cos_place * sin_seg) * sign
            first = [depth] if depth < TRUNK else range(TRUNK, TRUNK + BRANCHES)
            for seg in first if depth <= TRUNK else range(TRUNK + BRANCHES, TREE_SEGS):
                cos_ref[seg * SEG : (seg + 1) * SEG, :] = cos
                sin_ref[seg * SEG : (seg + 1) * SEG, :] = sin

    for i in range(size):
        here, there = places(i)
        cos, sin = cos_ref[there, :], sin_ref[there, :]
        q = qkv_ref[0, here, :].astype(f32)
        k = qkv_ref[1, here, :].astype(f32)
        qs[there, :] = ((q * cos + partner(q) * sin) * (HDIM ** -0.5)).astype(bf16)
        kr[there, :] = (k * cos + partner(k) * sin).astype(bf16)
        vr[there, :] = qkv_ref[2, here, :]
        do_ref[there, :] = do_in[here, :]

    for i in range(rows // step):
        at = pl.ds(i * step, step)
        kt[:, at] = dot_nt(unit_wide, kr[at, :]).astype(bf16)
        vt[:, at] = dot_nt(unit_wide, vr[at, :]).astype(bf16)
        dot_t[:, at] = dot_nt(unit_wide, do_ref[at, :]).astype(bf16)
        dk[at, :] = jnp.zeros((step, 2 * HDIM), f32)
        dv[at, :] = jnp.zeros((step, 2 * HDIM), f32)

    top[...] = jnp.full((2, 8, step), NEG, f32)
    key_id = lax.broadcasted_iota(jnp.int32, (SEG, step), 0)
    query_id = lax.broadcasted_iota(jnp.int32, (SEG, step), 1) % SEG
    pair_mask = key_id <= query_id
    tri_mask = lax.broadcasted_iota(jnp.int32, (step, step), 0) <= lax.broadcasted_iota(
        jnp.int32, (step, step), 1)

    def seg_at(start, size):
        if isinstance(start, int):
            return pl.ds(start, size)
        return pl.ds(pl.multiple_of(start, SEG), size)

    def block(q0, q1, chunks, diag):
        halves = [seg_at(q0, SEG), seg_at(q1, SEG)]
        q_all = jnp.concatenate([qs[halves[0], :], qs[halves[1], :]], axis=0)
        do_all = jnp.concatenate([do_ref[halves[0], :], do_ref[halves[1], :]], axis=0)
        zero = jnp.zeros_like(q_all)
        pieces = []
        off = 0
        for start, size in chunks:
            pieces.append((off, start, size, 'full'))
            off += size
        pieces.append((off, q0, step, 'tri') if diag else (off, None, SEG, 'pair'))
        both = range(2)
        qh = [jnp.where(lane_low if h == 0 else ~lane_low, q_all, zero) for h in both]
        dh = [jnp.where(lane_low if h == 0 else ~lane_low, do_all, zero) for h in both]
        q_stack = jnp.concatenate(qh, axis=0)
        d_stack = jnp.concatenate(dh, axis=0)

        def part(x, i):
            return x[i * SEG:(i + 1) * SEG]

        def lanes(x, i):
            return x[:, i * SEG:(i + 1) * SEG]

        def left(ref, piece, rhs):
            o, start, size, kind = piece
            if kind == 'pair':
                return jnp.concatenate(
                    [dot_nt(ref[halves[i], :], part(rhs, i)) for i in both], axis=1)
            return dot_nt(ref[seg_at(start, size), :], rhs)

        def turned(ref, h, piece, x):
            o, start, size, kind = piece
            rows_h = slice(h * HDIM, (h + 1) * HDIM)
            if kind == 'pair':
                return jnp.concatenate(
                    [dot_nn(ref[rows_h, halves[i]], lanes(x, i)) for i in both], axis=1)
            return dot_nn(ref[rows_h, seg_at(start, size)], x)

        def add_rows(ref, piece, xs, stack):
            o, start, size, kind = piece
            if kind == 'pair':
                for i in both:
                    ref[halves[i], :] += dot_nn(
                        jnp.concatenate([lanes(x, i) for x in xs], axis=1),
                        jnp.concatenate([part(stack, i), part(stack, 2 + i)], axis=0))
            else:
                ref[seg_at(start, size), :] += dot_nn(jnp.concatenate(xs, axis=1), stack)

        def fold(x, op):
            return op(x.reshape(x.shape[0] // 8, 8, step), axis=0)

        tops = [[], []]
        sums = [[], []]
        for piece in pieces:
            o, start, size, kind = piece
            for h in both:
                s = left(kr, piece, qh[h])
                if kind == 'tri':
                    s = jnp.where(tri_mask, s, NEG)
                if kind == 'pair':
                    s = jnp.where(pair_mask, s, NEG)
                m = fold(s, jnp.max)
                top[h] = jnp.maximum(top[h], m)
                m = jnp.max(m, axis=0, keepdims=True)
                e = jnp.exp(s - m)
                s_ref[h, o:o + size, :] = e
                tops[h].append(m)
                sums[h].append(jnp.sum(fold(e, jnp.sum), axis=0, keepdims=True))
        scales = []
        for h in both:
            m = functools.reduce(jnp.maximum, tops[h])
            w = [jnp.exp(mc - m) for mc in tops[h]]
            inv = 1.0 / sum(wc * sc for wc, sc in zip(w, sums[h]))
            scales.append([wc * inv for wc in w])
        o_acc = [jnp.zeros((HDIM, step), f32)] * 2
        for n, piece in enumerate(pieces):
            o, start, size, kind = piece
            low = []
            for h in both:
                p = s_ref[h, o:o + size, :] * scales[h][n]
                s_ref[h, o:o + size, :] = p
                low.append(p.astype(bf16))
                o_acc[h] = o_acc[h] + turned(vt, h, piece, low[h])
            add_rows(dv, piece, low, d_stack)
        deltas = []
        for h in both:
            d_turned = jnp.concatenate(
                [dot_t[h * HDIM:(h + 1) * HDIM, halves[i]] for i in both], axis=1)
            deltas.append(jnp.sum(o_acc[h] * d_turned.astype(f32), axis=0, keepdims=True))
        dq_acc = [jnp.zeros((HDIM, step), f32)] * 2
        for n, piece in enumerate(pieces):
            o, start, size, kind = piece
            low = []
            for h in both:
                dp = left(vr, piece, dh[h])
                low.append((s_ref[h, o:o + size, :] * (dp - deltas[h])).astype(bf16))
                dq_acc[h] = dq_acc[h] + turned(kt, h, piece, low[h])
            add_rows(dk, piece, low, q_stack)
        o_rows = jnp.concatenate(o_acc, axis=0).T.astype(bf16)
        dq_rows = jnp.concatenate(dq_acc, axis=0).T
        for i in both:
            att[halves[i], :] = part(o_rows, i)
            dqn[halves[i], :] = part(dq_rows, i)

    for b in range(TRUNK // 2):
        block(b * step, b * step + SEG, [(c * step, step) for c in range(b)], True)
    trunk_chunks = [(c * step, step) for c in range(TRUNK // 2)]

    @pl.loop(0, BRANCHES // 2)
    def _(i):
        start = (TRUNK + 2 * i) * SEG
        block(start, start + SEG, trunk_chunks, False)

    @pl.loop(0, BRANCHES)
    def _(i):
        branch = TRUNK + i
        first = TREE_SEGS - 1
        last = TRUNK + BRANCHES
        for leaf in range(TREE_SEGS - 1, TRUNK + BRANCHES - 1, -1):
            first = jnp.where(par[leaf] == branch, leaf, first)
        for leaf in range(TRUNK + BRANCHES, TREE_SEGS):
            last = jnp.where(par[leaf] == branch, leaf, last)
        block(first * SEG, last * SEG, trunk_chunks + [(branch * SEG, SEG)], False)

    totals = [jnp.zeros((8, 2 * HDIM), f32)] * 3
    for i in range(size):
        here, there = places(i)
        cos, sin = cos_ref[there, :], sin_ref[there, :]
        att_ref[here, :] = att[there, :]
        dq = dqn[there, :] * (HDIM ** -0.5)
        dkr = dk[there, :]
        parts = [dq * cos - partner(dq) * sin, dkr * cos - partner(dkr) * sin, dv[there, :]]
        for c in range(3):
            low = parts[c].astype(bf16)
            g_ref[c, here, :] = low
            totals[c] = totals[c] + jnp.sum(low.astype(f32).reshape(local // 8, 8, 2 * HDIM), axis=0)

    rows_out = [jnp.sum(t, axis=0, keepdims=True) for t in totals]
    for h in range(2):
        rows_out.append(jnp.full((1, 2 * HDIM), jnp.max(top[h]), f32))
    rows_out.append(jnp.zeros((3, 2 * HDIM), f32))
    aux_ref[0] = jnp.concatenate(rows_out, axis=0)


def attention(parents, me, size, cos, sin, qkv, grad_att):
    rows, width = grad_att.shape
    pairs = width // (2 * HDIM)
    step = 2 * SEG
    wide = 2 * HDIM
    keys = TRUNK * SEG + 2 * SEG
    blk = lambda: pl.BlockSpec((rows, wide), lambda p, par, me: (0, p))
    blk3 = lambda: pl.BlockSpec((3, rows, wide), lambda p, par, me: (0, 0, p))
    tab = lambda: pl.BlockSpec((SEG + TRUNK + 2, wide), lambda p, par, me: (0, 0))
    return pl.pallas_call(
        functools.partial(attn_kernel, size),
        out_shape=(
            jax.ShapeDtypeStruct((rows, width), bf16),
            jax.ShapeDtypeStruct((3, rows, width), bf16),
            jax.ShapeDtypeStruct((pairs, 8, wide), f32),
        ),
        grid_spec=pltpu.PrefetchScalarGridSpec(
            num_scalar_prefetch=2,
            grid=(pairs,),
            in_specs=[tab(), tab(), blk3(), blk()],
            out_specs=[blk(), blk3(), pl.BlockSpec((1, 8, wide), lambda p, par, me: (p, 0, 0))],
            scratch_shapes=[
                pltpu.VMEM((rows, wide), bf16),
                pltpu.VMEM((rows, wide), bf16),
                pltpu.VMEM((rows, wide), bf16),
                pltpu.VMEM((rows, wide), bf16),
                pltpu.VMEM((wide, rows), bf16),
                pltpu.VMEM((wide, rows), bf16),
                pltpu.VMEM((wide, rows), bf16),
                pltpu.VMEM((rows, wide), bf16),
                pltpu.VMEM((rows, wide), f32),
                pltpu.VMEM((rows, wide), f32),
                pltpu.VMEM((rows, wide), f32),
                pltpu.VMEM((2, keys, step), f32),
                pltpu.VMEM((2, 8, step), f32),
                pltpu.VMEM((rows, wide), f32),
                pltpu.VMEM((rows, wide), f32),
            ],
        ),
        compiler_params=pltpu.CompilerParams(
            dimension_semantics=("arbitrary",), vmem_limit_bytes=63 << 20),
        cost_estimate=pl.CostEstimate(flops=60 * 10**9, transcendentals=17 * 10**6, bytes_accessed=24 << 20),
    )(parents, me, cos, sin, qkv, grad_att)


clip_tau = 10.0
norm_eps = 1e-05


def dot_tn(a, b):
    return lax.dot_general(a, b, (((0,), (0,)), ((), ())), preferred_element_type=f32)


def xor_send(x, bits, size):
    return lax.ppermute(x, "tensor", [(i, i ^ bits) for i in range(size)])


def add_low(a, b):
    return (a.astype(f32) + b.astype(f32)).astype(bf16)


def scatter_rest(parts, size):
    low, high = parts[0].astype(f32), parts[1].astype(f32)
    for i in range(1, size):
        low = low + xor_send(parts[2 * i], i, size).astype(f32)
        high = high + xor_send(parts[2 * i + 1], i, size).astype(f32)
    return [low, high]


def after(x, *others):
    return lax.optimization_barrier((x,) + others)[0]


class Carry:
    def __init__(self, tag=0, arrays=(), shapes=(), links=None, count=0, alias=False):
        self.tag, self.arrays, self.links, self.count, self.alias = tag, list(arrays), links, count, alias
        self.shapes = [jax.ShapeDtypeStruct(*shape) for shape in shapes]


def sending(tag, *sends):
    return Carry(
        tag, [a for a, axis, bits in sends], [(a.shape, a.dtype) for a, axis, bits in sends],
        lambda src, dst: [(src[n], dst[n], axis, bits) for n, (a, axis, bits) in enumerate(sends)], len(sends))


def other_device(axis, bits):
    t = lax.axis_index(axis)
    at = t
    for n in range(8):
        if bits >> n & 1:
            at = at + (1 << n) - (2 << n) * ((t // (1 << n)) % 2)
    return {axis: at}


def meet(partners):
    barrier = pltpu.get_barrier_semaphore()
    for axis, bits in partners:
        pl.semaphore_signal(
            barrier, inc=1, device_id=other_device(axis, bits), device_id_type=pl.DeviceIdType.MESH)
    pl.semaphore_wait(barrier, len(partners))


def remote_copies(links, sems):
    return [
        pltpu.make_async_copy(src, dst, sems.at[0, n])
        if axis is None
        else pltpu.make_async_remote_copy(
            src_ref=src,
            dst_ref=dst,
            send_sem=sems.at[0, n],
            recv_sem=sems.at[1, n],
            device_id=other_device(axis, bits),
            device_id_type=pl.DeviceIdType.MESH,
        )
        for n, (src, dst, axis, bits) in enumerate(links)
    ]


def hint():
    return pl.CostEstimate(flops=10**10, transcendentals=0, bytes_accessed=2 << 20)


def tiled(inner, grid, ins, outs, carry=None, vmem=63):
    carry = carry or Carry()
    n_in, n_out, n_src, n_dst = len(ins), len(outs), len(carry.arrays), len(carry.shapes)
    in_specs = [pl.BlockSpec(block, at) for a, block, at in ins]
    out_specs = [pl.BlockSpec(block, at) for shape, dtype, block, at in outs]
    any_spec = pl.BlockSpec(memory_space=pltpu.HBM)
    arrays = [a for a, block, at in ins]
    shapes = [jax.ShapeDtypeStruct(shape, dtype) for shape, dtype, block, at in outs]
    if not carry.count:
        results = pl.pallas_call(
            inner, grid=grid, in_specs=in_specs, out_specs=out_specs, out_shape=shapes,
            compiler_params=pltpu.CompilerParams(
                dimension_semantics=("arbitrary",) * len(grid), vmem_limit_bytes=vmem << 20),
            cost_estimate=hint(),
        )(*arrays)
        return list(results), []

    def kernel(*refs):
        sources = refs[n_in : n_in + n_src]
        places = refs[n_in + n_src : n_in + n_src + n_out]
        targets = refs[n_in + n_src + n_out : -1]
        links = carry.links(sources, targets)
        meet(sorted(set((axis, bits) for src, dst, axis, bits in links if axis is not None)))
        copies = remote_copies(links, refs[-1])
        for copy in copies:
            copy.start()
        if grid:
            pltpu.emit_pipeline(inner, grid=grid, in_specs=in_specs, out_specs=out_specs)(*refs[:n_in], *places)
        for copy in copies:
            copy.wait()

    results = pl.pallas_call(
        kernel,
        in_specs=[any_spec] * (n_in + n_src),
        out_specs=[any_spec] * (n_out + n_dst),
        out_shape=shapes + carry.shapes,
        scratch_shapes=[pltpu.SemaphoreType.DMA((2, carry.count))],
        input_output_aliases={n_in: n_out} if carry.alias else {},
        compiler_params=pltpu.CompilerParams(
            vmem_limit_bytes=vmem << 20, collective_id=carry.tag, has_side_effects=True),
        cost_estimate=hint(),
    )(*arrays, *carry.arrays)
    return list(results[:n_out]), list(results[n_out:])


def side_sums(adds, grid):
    at = lambda j, i: (0, j * grid[1] + i)
    block = lambda a: (a.shape[0], a.shape[1] // (grid[0] * grid[1]))
    ins = [(a, block(a), at) for pair in adds for a in pair]
    outs = [(a.shape, a.dtype, block(a), at) for a, b in adds]
    return ins, outs


def chunk_matmul(pairs, columns, tile, count, blocks, at, carry=None, adds=(), cut=1):
    local = pairs[0][0].shape[-2] // count
    grid = (columns // tile, blocks)
    ins = []
    for x, w, c, d in pairs:
        depth = x.shape[-1]
        if c < 0:
            ins.append((x, (local, depth), lambda j, i: (at(i), 0)))
        else:
            ins.append((x, (None, local, depth), lambda j, i, c=c: (c, at(i), 0)))
        if d is None:
            ins.append((w, (depth, tile), lambda j, i: (0, j)))
        elif d < 0:
            ins.append((w, (tile, depth), lambda j, i: (j, 0)))
        else:
            ins.append((w, (None, tile, depth), lambda j, i, d=d: (d, j, 0)))
    terms = len(pairs)
    adds = dict(adds)
    more = [(adds[b], (local, tile), lambda j, i: (0, j)) for b in sorted(adds)]
    part = local // cut
    outs = [((part, columns), bf16, (part, tile), lambda j, i: (0, j))] * (blocks * cut)

    def inner(*refs):
        sides, results = dict(zip(sorted(adds), refs[2 * terms :])), refs[2 * terms + len(more) :]
        acc = None
        for n in range(terms):
            dot = dot_nn if pairs[n][3] is None else dot_nt
            term = dot(refs[2 * n][...], refs[2 * n + 1][...])
            acc = term if acc is None else acc + term
        for i in range(blocks):
            @pl.when(pl.program_id(1) == i)
            def _(i=i):
                whole = acc
                if at(i) in sides:
                    whole = whole + sides[at(i)][...].astype(f32)
                low = whole.astype(bf16)
                for n in range(cut):
                    results[i * cut + n][...] = low[n * part : (n + 1) * part]

    results, got = tiled(inner, grid, ins + more, outs, carry)
    return {at(i) * cut + n: results[i * cut + n] for i in range(blocks) for n in range(cut)}, got


def head_grads(normed, grad_qkv, cot, attended, tile, carry):
    rows, model = normed.shape
    width = attended.shape[1]
    last = model // tile - 1

    def inner(n_ref, g_ref, c_ref, a_ref, o_ref):
        @pl.when(pl.program_id(0) < 3)
        def _():
            o_ref[...] = dot_tn(n_ref[...], g_ref[...]).astype(bf16)

        @pl.when(pl.program_id(0) == 3)
        def _():
            o_ref[...] = dot_tn(c_ref[...], a_ref[...]).astype(bf16)

    (grads,), got = tiled(
        inner, (4, model // tile),
        [
            (normed, (rows, tile), lambda c, i: (0, i + (last - i) * (c // 3))),
            (grad_qkv, (None, rows, width), lambda c, i: (c - c // 3, 0, 0)),
            (cot, (rows, tile), lambda c, i: (0, i * (c // 3))),
            (attended, (rows, width), lambda c, i: (0, 0)),
        ],
        [((4, model, width), bf16, (None, tile, width), lambda c, i: (c, i, 0))], carry)
    return grads, got


def weight_grad(x, y, m_tile, n_tile, carry):
    rows, m = x.shape
    n = y.shape[1]

    def inner(x_ref, y_ref, o_ref):
        o_ref[...] = dot_tn(x_ref[...], y_ref[...]).astype(bf16)

    (grad,), got = tiled(
        inner, (m // m_tile, n // n_tile),
        [(x, (rows, m_tile), lambda i, j: (0, i)), (y, (rows, n_tile), lambda i, j: (0, j))],
        [((m, n), bf16, (m_tile, n_tile), lambda i, j: (i, j))], carry)
    return grad, got


def hidden_forward(normed, up_w, b_fc1, r_tile, f_tile, carry):
    rows, model = normed.shape
    ff = up_w.shape[1]

    def inner(n_ref, w_ref, b_ref, a_ref, s_ref):
        value, slope = gelu_parts(dot_nn(n_ref[...], w_ref[...]) + b_ref[...])
        a_ref[...] = value.astype(bf16)
        s_ref[...] = slope.astype(bf16)

    out = ((rows, ff), bf16, (r_tile, f_tile), lambda j, i: (i, j))
    (value, slope), got = tiled(
        inner, (ff // f_tile, rows // r_tile),
        [
            (normed, (r_tile, model), lambda j, i: (i, 0)),
            (up_w, (model, f_tile), lambda j, i: (0, j)),
            (b_fc1[None], (1, f_tile), lambda j, i: (0, j)),
        ],
        [out, out], carry, 48)
    return value, slope, got


def hidden_grad(cot, down_w, slope, r_tile, f_tile, carry, adds):
    rows, model = cot.shape
    ff = down_w.shape[0]
    grid = (ff // f_tile, rows // r_tile)
    extra_in, extra_out = side_sums(adds, grid)

    def inner(c_ref, w_ref, s_ref, *refs):
        sides, (g_ref, b_ref, *results) = refs[: len(extra_in)], refs[len(extra_in) :]
        for n in range(len(adds)):
            results[n][...] = add_low(sides[2 * n][...], sides[2 * n + 1][...])
        low = (dot_nt(c_ref[...], w_ref[...]) * s_ref[...].astype(f32)).astype(bf16)
        g_ref[...] = low
        part = jnp.sum(low.astype(f32).reshape(r_tile // 8, 8, f_tile), axis=0)

        @pl.when(pl.program_id(1) == 0)
        def _():
            b_ref[...] = part

        @pl.when(pl.program_id(1) > 0)
        def _():
            b_ref[...] += part

    (grad, sums, *results), got = tiled(
        inner, grid,
        [
            (cot, (r_tile, model), lambda j, i: (i, 0)),
            (down_w, (f_tile, model), lambda j, i: (j, 0)),
            (slope, (r_tile, f_tile), lambda j, i: (i, j)),
        ] + extra_in,
        [
            ((rows, ff), bf16, (r_tile, f_tile), lambda j, i: (i, j)),
            ((8, ff), f32, (8, f_tile), lambda j, i: (0, j)),
        ] + extra_out, carry)
    return grad, sums, results, got


def norm_gather(tokens, ln_gain, ln_bias, tag):
    local, model = tokens.shape
    half, tile = local // 2, local // 6

    def kernel(x_ref, gain_ref, bias_ref, all_ref, mine, sems):
        meet([("tensor", 1), ("tensor", 2)])
        part = lambda n: mine.at[pl.ds(n * half, half)]
        rows = lambda at, size: all_ref.at[pl.ds(at, size)]
        copies = remote_copies([
            (part(1), rows(local + half, half), "tensor", 1),
            (part(0), rows(2 * local, half), "tensor", 2),
            (part(0), rows(local, half), "tensor", 1),
            (part(1), rows(2 * local + half, half), "tensor", 2),
            (rows(2 * local, half), rows(3 * local, half), "tensor", 1),
            (rows(local + half, half), rows(3 * local + half, half), "tensor", 2),
            (mine, rows(0, local), None, 0),
        ], sems)

        def normalize(n):
            @pl.loop(0, 3)
            def _(i):
                at = pl.ds(pl.multiple_of(n * half + i * tile, tile), tile)
                xhat, inverse = norm_parts(x_ref[at, :].astype(f32))
                mine[at, :] = (xhat * gain_ref[...] + bias_ref[...]).astype(bf16)

        normalize(1)
        copies[0].start()
        normalize(0)
        for n in (1, 2, 3, 6):
            copies[n].start()
        copies[1].wait_recv()
        copies[4].start()
        copies[0].wait_recv()
        copies[5].start()
        copies[0].wait_send()
        copies[1].wait_send()
        for n in (2, 3, 4, 5, 6):
            copies[n].wait()

    return pl.pallas_call(
        kernel,
        in_specs=[pl.BlockSpec(memory_space=pltpu.VMEM)] * 3,
        out_specs=pl.BlockSpec(memory_space=pltpu.HBM),
        out_shape=jax.ShapeDtypeStruct((4 * local, model), bf16),
        scratch_shapes=[pltpu.VMEM((local, model), bf16), pltpu.SemaphoreType.DMA((2, 7))],
        compiler_params=pltpu.CompilerParams(
            vmem_limit_bytes=63 << 20, collective_id=tag, has_side_effects=True),
        cost_estimate=hint(),
    )(tokens, ln_gain[None], ln_bias[None])


def gather_sides(x, tag):
    local, model = x.shape
    return Carry(
        tag, [x], [((4 * local, model), bf16)],
        lambda src, dst: [
            (src[0], dst[0].at[pl.ds(local, local)], "tensor", 1),
            (src[0], dst[0].at[pl.ds(2 * local, local)], "tensor", 2),
            (src[0], dst[0].at[pl.ds(0, local)], None, 0),
        ], 3)


def gather_corner(whole, tag):
    local = whole.shape[0] // 4
    half = local // 2
    return Carry(
        tag, [whole], [(whole.shape, bf16)],
        lambda src, dst: [
            (dst[0].at[pl.ds(2 * local, half)], dst[0].at[pl.ds(3 * local, half)], "tensor", 1),
            (dst[0].at[pl.ds(local + half, half)], dst[0].at[pl.ds(3 * local + half, half)], "tensor", 2),
        ], 2, True)


def norm_back(own, low_parts, high_parts, tokens, cotangent, ln_gain):
    rows, model = tokens.shape
    tiles = 6
    tile = rows // tiles
    half = tiles // 2

    def inner(own_low, own_high, l0, l1, h0, h1, t_ref, c_ref, gain_ref, o_ref, s_ref):
        step = pl.program_id(0)

        def compute(a, b, c):
            grad = a[...].astype(f32) + b[...].astype(f32) + c[...].astype(f32)
            cot = c_ref[...].astype(f32)
            xhat, inverse = norm_parts(t_ref[...].astype(f32))
            scaled = grad * gain_ref[...]
            both = grad * xhat
            o_ref[...] = cot + inverse * (
                scaled
                - jnp.mean(scaled, axis=-1, keepdims=True)
                - xhat * jnp.mean(scaled * xhat, axis=-1, keepdims=True))
            terms = [jnp.sum(v.reshape(tile // 8, 8, model), axis=0) for v in (both, grad, cot)]

            @pl.when(step == 0)
            def _():
                for n in range(3):
                    s_ref[n] = terms[n]

            @pl.when(step > 0)
            def _():
                for n in range(3):
                    s_ref[n] += terms[n]

        @pl.when(step < half)
        def _():
            compute(own_low, l0, l1)

        @pl.when(step >= half)
        def _():
            compute(own_high, h0, h1)

    low = lambda i: (jnp.minimum(i, half - 1), 0)
    high = lambda i: (jnp.maximum(i - half, 0), 0)
    each = lambda i: (i, 0)
    block = (tile, model)
    (grad, sums), ignored = tiled(
        inner, (tiles,),
        [(own[0], block, low), (own[1], block, high)]
        + [(a, block, low) for a in low_parts] + [(a, block, high) for a in high_parts]
        + [(tokens, block, each), (cotangent, block, each), (ln_gain[None], (1, model), lambda i: (0, 0))],
        [((rows, model), f32, block, each), ((3, 8, model), f32, (3, 8, model), lambda i: (0, 0, 0))])
    return grad, jnp.sum(sums, axis=1)


def norm_parts(rows_in):
    row_mean = jnp.mean(rows_in, axis=-1, keepdims=True)
    centred = rows_in - row_mean
    inverse = lax.rsqrt(jnp.mean(centred * centred, axis=-1, keepdims=True) + norm_eps)
    return centred * inverse, inverse


def gelu_parts(v):
    scale = (2.0 / jnp.pi) ** 0.5
    square = v * v
    t = jnp.tanh(v * (scale + (scale * 0.044715) * square))
    half = 0.5 * (1.0 + t)
    slope = half + (half * (1.0 - t)) * (v * (scale + (scale * 3 * 0.044715) * square))
    return v * half, slope


def body(
    tokens,
    cotangent,
    ln_gain,
    ln_bias,
    w_qkv,
    b_qkv,
    w_out,
    w_fc1,
    b_fc1,
    w_fc2,
    resid_bias,
    parents,
):
    size = lax.axis_size("tensor")
    groups = lax.axis_size("dp")
    local_rows, model = tokens.shape
    me = lax.axis_index("tensor")
    width = w_qkv.shape[2]
    four = size == 4
    t1, t2 = ("tensor", 1), ("tensor", 2)
    half_cols = model // 2

    tables = rope_tables()
    up_w = lax.all_gather(w_fc1, "dp", axis=0, tiled=True)
    w_heads = jnp.concatenate([w_qkv, jnp.transpose(w_out)[None]], axis=0)
    heads_w = lax.all_gather(w_heads, "dp", axis=1, tiled=True)
    down_w = lax.all_gather(w_fc2, "dp", axis=1, tiled=True)
    if four:
        normed = norm_gather(tokens, ln_gain, ln_bias, 1)
    else:
        normed_local = (norm_parts(tokens.astype(f32))[0] * ln_gain + ln_bias).astype(bf16)
        normed, cot_full = (
            jnp.concatenate([x] + [xor_send(x, i, size) for i in range(1, size)], axis=0)
            for x in (normed_local, cotangent))
    activated, slope, got = hidden_forward(
        normed, up_w, b_fc1, local_rows, half_cols, gather_sides(cotangent, 2) if four else None)
    if four:
        cot_full = tiled(None, (), [], [], gather_corner(got[0], 3))[1][0]
    projected = (
        jnp.einsum(
            "td,cdh->cth", after(normed, activated, cot_full), heads_w[:3], preferred_element_type=f32)
        + b_qkv[:, None, :]
    ).astype(bf16)
    grad_w_fc2 = dot_tn(after(activated, projected), cot_full).astype(bf16)
    summed_fc2 = lax.psum_scatter(grad_w_fc2, "dp", scatter_dimension=1, tiled=True)
    grad_attended = dot_nn(after(cot_full, grad_w_fc2), heads_w[3]).astype(bf16)
    attended, grad_qkv, aux = attention(parents[0], me[None], size, *tables, projected, grad_attended)

    branch, ignored = chunk_matmul(
        [(attended, heads_w, -1, 3), (activated, down_w, -1, None)],
        model, half_cols, size, size, lambda i: i, cut=2)
    grad_w_heads, got = head_grads(
        after(normed, branch[0]), grad_qkv, cot_full, attended, half_cols,
        sending(4, (branch[6],) + t1, (branch[7],) + t2) if four else None)
    summed_heads = lax.psum_scatter(grad_w_heads, "dp", scatter_dimension=1, tiled=True)
    grad_hidden, sums_fc1, branch_next, side = hidden_grad(
        after(cot_full, grad_w_heads), down_w, slope, local_rows, half_cols,
        sending(5, (branch[2],) + t1, (branch[5],) + t2) if four else None,
        [(branch[3], got[1]), (branch[4], got[0])] if four else [])
    dp_bits = range(1, groups)
    backs = [(grad_qkv, heads_w, c, c) for c in range(3)] + [(after(grad_hidden, summed_fc2), up_w, -1, -1)]
    if four:
        far, last = chunk_matmul(
            backs, model, half_cols, 8, 4, lambda i: 7 - i - 2 * (i // 3),
            sending(6, (branch_next[0],) + t1, (branch_next[1],) + t2))
        branch_sum = [
            branch[0].astype(f32) + side[0].astype(f32) + last[1].astype(f32),
            branch[1].astype(f32) + last[0].astype(f32) + side[1].astype(f32)]
        grad_w_fc1, got = weight_grad(
            after(normed, far[7]), grad_hidden, half_cols, half_cols,
            sending(
                7, (far[6],) + t1, (far[7],) + t2,
                *[(aux, "dp", bits) for bits in dp_bits], *[(sums_fc1, "dp", bits) for bits in dp_bits]))
        all_aux = [aux] + got[2 : 1 + groups]
        all_fc1 = [sums_fc1] + got[1 + groups :]
        backs[3] = (after(grad_hidden, grad_w_fc1),) + backs[3][1:]
        near, side = chunk_matmul(
            backs, model, half_cols, 8, 4, lambda i: 4 - i - i // 2,
            sending(8, (far[2],) + t1, (far[5],) + t2), {3: got[1], 4: got[0]})
        one, two = xor_send(near[3], 1, size), xor_send(near[4], 2, size)
        input_grad, terms = norm_back(
            [near[0], near[1]], [side[0], two], [one, side[1]], tokens, cotangent, ln_gain)
        branch_sum[0] = after(branch_sum[0], near[0])
        all_aux[0] = after(aux, near[0])
        all_fc1[0] = after(sums_fc1, near[0])
    else:
        parts, ignored = chunk_matmul(backs, model, half_cols, size, size, lambda i: i, cut=2)
        grad_w_fc1, ignored = weight_grad(normed, grad_hidden, half_cols, half_cols, None)
        all_aux, all_fc1 = (list(lax.all_gather(x, "dp")) for x in (aux, sums_fc1))
        branch_sum = scatter_rest(branch, size)
        grad_normed = jnp.concatenate(scatter_rest(parts, size), axis=0)
        xhat, inverse = norm_parts(tokens.astype(f32))
        grad_xhat = grad_normed * ln_gain
        cot_local = cotangent.astype(f32)
        input_grad = cot_local + inverse * (
            grad_xhat
            - jnp.mean(grad_xhat, axis=-1, keepdims=True)
            - xhat * jnp.mean(grad_xhat * xhat, axis=-1, keepdims=True)
        )
        terms = jnp.stack(
            [jnp.sum(grad_normed * xhat, axis=0), jnp.sum(grad_normed, axis=0), jnp.sum(cot_local, axis=0)]
        )
    summed_fc1 = lax.psum_scatter(grad_w_fc1, "dp", scatter_dimension=0, tiled=True)
    output_rows = (
        tokens.astype(f32) + jnp.concatenate(branch_sum, axis=0) + resid_bias).astype(bf16)
    summed_fc1, summed_heads, summed_fc2 = (
        w.astype(f32) for w in (summed_fc1, summed_heads, summed_fc2))
    summed_qkv, summed_out = summed_heads[:3], jnp.transpose(summed_heads[3])

    bias_qkv = jnp.transpose(sum(a[:, :3] for a in all_aux), (1, 0, 2)).reshape(3, width)
    bias_fc1 = jnp.sum(sum(all_fc1), axis=0)
    head_top = functools.reduce(jnp.maximum, [a[:, 3:5, 0] for a in all_aux]).reshape(-1)
    factor = jnp.sqrt(clip_tau / jnp.maximum(head_top, clip_tau))
    clipped_qk = (w_qkv[:2].astype(f32) * jnp.repeat(factor, HDIM)[None, None, :]).astype(bf16)

    every = size * groups
    pieces = jnp.transpose(terms.reshape(3, every, model // every), (1, 0, 2)).reshape(every, -1)
    pieces = lax.all_to_all(pieces, ("dp", "tensor"), 0, 0, tiled=True)
    grad_small = jnp.sum(pieces, axis=0).reshape(3, model // every)
    return (
        output_rows,
        input_grad,
        grad_small,
        summed_qkv,
        bias_qkv,
        summed_out,
        summed_fc1,
        bias_fc1,
        summed_fc2,
        clipped_qk,
    )


def solution(mesh):
    return jax.shard_map(
        body,
        mesh=mesh,
        in_specs=(
            P(("dp", "tensor"), None),
            P(("dp", "tensor"), None),
            P(),
            P(),
            P(None, "dp", "tensor"),
            P(None, "tensor"),
            P("tensor", "dp"),
            P("dp", "tensor"),
            P("tensor"),
            P("tensor", "dp"),
            P(),
            P("dp", None),
        ),
        out_specs=(
            P(("dp", "tensor"), None),
            P(("dp", "tensor"), None),
            P(None, ("dp", "tensor")),
            P(None, "dp", "tensor"),
            P(None, "tensor"),
            P("tensor", "dp"),
            P("dp", "tensor"),
            P("tensor"),
            P("tensor", "dp"),
            P(None, "dp", "tensor"),
        ),
        check_vma=False,
    )
```

time: 638 us -> 602 us (0.944)
  Pallas kernels: 273 us -> 451 us
  waiting for transfers between devices: 103 us -> 42.7 us
  local copies, waits for them, and re-layouts: 65.1 us -> 8.1 us
  matrix products: 100 us -> 54.3 us
  other arithmetic: 55 us -> 17.6 us
  starting transfers between devices: 22.5 us -> 5.03 us
    pallas_call x6 -> x10, Pallas kernels: 180 us -> 358 us  [the longest x7 230 us: tiled(): pl.pallas_call(kernel, in_specs=[any_spec] * (n_in + n_src), out_specs=[a...]
    ppermute x11 -> x2, waiting for transfers between devices: 94.7 us -> 17.2 us  [xor_send(): return lax.ppermute(x, 'tensor', [(i, i ^ bits) for i in range(size)])]
    unnamed x103 -> x58, local copies, waits for them, and re-layouts: 35.1 us -> 4.96 us
    dot_general x1, matrix products: 36.7 us -> 10.3 us  [dot_nn(): lax.dot_general(a, b, (((1,), (0,)), ((), ())), preferred_element_type=f32)]
    reduce_scatter x1, waiting for transfers between devices: 0.01 us -> 21.5 us  [body(): lax.psum_scatter(grad_w_fc1, 'dp', scatter_dimension=0, tiled=True)]
    reduce_sum x8 -> x2, other arithmetic: 20 us -> 2.65 us  [the longest x1 1.57 us: body(): bias_fc1 = jnp.sum(sum(all_fc1), axis=0)]
    concatenate x4 -> x0, local copies, waits for them, and re-layouts: 13.2 us -> none  [the longest x1 4.59 us: rope_tables(): jnp.concatenate([sin_h, sin_h], axis=1)]
    ppermute x11 -> x2, starting transfers between devices: 13.8 us -> 2 us  [xor_send(): return lax.ppermute(x, 'tensor', [(i, i ^ bits) for i in range(size)])]
  transfers between devices with their start and end apart: 23 -> 9, of which waited for: 8 -> 5; matrix products, arithmetic and copies ran while one was open for 32% -> 12% of each run, Pallas kernels for 43% -> 76%
where the time goes in v3:
time: 602 us; the launch traced here: 593 us
  Pallas kernels  451 us (75%)
  matrix products  54.3 us (9%)
  waiting for transfers between devices  42.7 us (7%)
  other arithmetic  17.6 us (3%)
  between operations  14.8 us (2%)
  local copies, waits for them, and re-layouts  8.1 us (1%)
    pallas_call x7, Pallas kernels, tiled(): pl.pallas_call(kernel, in_specs=[any_spec] * (n_in + n_src), out_specs=[a...  230 us
    pallas_call x1, Pallas kernels, attention(): pl.pallas_call(functools.partial(attn_kernel, size), out_shape=(jax.Shape...  92.8 us
    pallas_call x1, Pallas kernels, norm_gather(): pl.pallas_call(kernel, in_specs=[pl.BlockSpec(memory_space=pltpu.VMEM)] *...  84.6 us
    pallas_call x2, Pallas kernels, tiled(): pl.pallas_call(inner, grid=grid, in_specs=in_specs, out_specs=out_specs,...  43.5 us
    dot_general x1, matrix products, dot_tn(): lax.dot_general(a, b, (((0,), (0,)), ((), ())), preferred_element_type=f32)  23.6 us
    reduce_scatter x1, waiting for transfers between devices, body(): lax.psum_scatter(grad_w_fc1, 'dp', scatter_dimension=0, tiled=True)  21.5 us
    dot_general x1, matrix products, body(): jnp.einsum('td,cdh->cth', after(normed, activated, cot_full), heads_w[:3]...  20.4 us
    ppermute x2, waiting for transfers between devices, xor_send(): return lax.ppermute(x, 'tensor', [(i, i ^ bits) for i in range(size)])  17.2 us
  transfers between devices with their start and end apart: 9, of which 5 were waited for; matrix products, arithmetic and copies ran while one was open for 12% of the time, Pallas kernels for 76%

profile of v3, /device:TPU:0, one launch (start us, length us, event | category | flops | bytes accessed | tf_op | source)
XLA Modules:
  0.0 593.1 jit_solution(388527660189800842)
XLA Ops:
  8.0 1.1 copy.38
  9.1 2.2 pad_maximum_fusion
  12.1 84.6 %shard_map.213.refs_0_ = bf16[2304,2048]{1,0:T(8,128)(2,1)} custom-call(bf16[576,2048]{1,0:T(8,128)(2,1)} %t_ref.1, f32[1,2048]{1,0:T(1,128)} %bitcast.36, f32[1,2048]{1,0:T(1,128)} %bitcast.35), custom_call_target="tpu_custom_call" | custom-call | flops 10000000000 | bytes 2097152 | tf_op jit(solution)/shard_map/pallas_call | solution.py:605
  96.7 1.7 copy-done
  98.4 52.3 %shard_map.214 = (bf16[2304,2048]{1,0:T(8,128)(2,1)}, bf16[2304,2048]{1,0:T(8,128)(2,1)}, bf16[2304,2048]{1,0:T(8,128)(2,1)}) custom-call(bf16[2304,2048]{1,0:T(8,128)(2,1)} %shard_map.213.refs_0_, bf16[2048,2048]{1,0:T(8,128)(2,1)} %all-gather.6.cloned.1.call-done.refs_1_.refs_7_, f32[1,2048]{1,0:T(1,128)S(1)} %bitcast.32, bf16[576,2048]{1,0:T(8,128)(2,1)S(1)} %copy-done), custom_call_target="tpu_custom_call" | custom-call | flops 10000000000 | bytes 2097152 | tf_op jit(solution)/shard_map/pallas_call | solution.py:404
  150.7 26.3 %shard_map.215.refs_2_.refs_0_ = bf16[2304,2048]{1,0:T(8,128)(2,1)} custom-call(bf16[2304,2048]{1,0:T(8,128)(2,1)} %get-tuple-element.76.refs_0_), custom_call_target="tpu_custom_call", output_to_operand_aliasing={{}: (0, {})} | custom-call | flops 10000000000 | bytes 2097152 | tf_op jit(solution)/shard_map/pallas_call | solution.py:404
  177.2 20.4 %fusion.5.qkv_ref = bf16[3,2304,512]{2,1,0:T(8,128)(2,1)} fusion(f32[3,512]{1,0:T(4,128)S(1)} %copy-done.26, bf16[4,2048,512]{2,1,0:T(8,128)(2,1)} %all-gather.4.cloned.1.call-done.refs_1_.refs_3_.refs_5_, bf16[2304,2048]{1,0:T(8,128)(2,1)} %shard_map.213.refs_0_), kind=kOutput, calls=%fused_computation.5 | convolution fusion | flops 14502592512 | bytes 22812672 | tf_op jit(solution)/shard_map/td,cdh->cth/dot_general | solution.py:747
  197.6 23.6 %convolution_convert_fusion = bf16[2048,2048]{1,0:T(8,128)(2,1)} fusion(bf16[2304,2048]{1,0:T(8,128)(2,1)} %get-tuple-element.78.refs_2_, bf16[2304,2048]{1,0:T(8,128)(2,1)S(1)} %copy-done.27), kind=kOutput, calls=%fused_computation.3 | convolution fusion | flops 19331547136 | bytes 27262976 | tf_op jit(solution)/shard_map/dot_general | solution.py:301
  221.5 10.3 %convolution_convert_fusion.1.do_in = bf16[2304,512]{1,0:T(8,128)(2,1)} fusion(bf16[2304,2048]{1,0:T(8,128)(2,1)} %shard_map.215.refs_2_.refs_0_, bf16[4,2048,512]{2,1,0:T(8,128)(2,1)} %all-gather.4.cloned.1.call-done.refs_1_.refs_3_.refs_5_), kind=kOutput, calls=%fused_computation.9 | convolution fusion | flops 4833017856 | bytes 13893632 | tf_op jit(solution)/shard_map/dot_general | solution.py:25
  231.8 92.8 %shard_map.216 = (bf16[2304,512]{1,0:T(8,128)(2,1)}, bf16[3,2304,512]{2,1,0:T(8,128)(2,1)}, f32[4,8,128]{2,1,0:T(8,128)}) custom-call(s32[18]{0:T(128)} %bitcast.38, s32[1]{0:T(128)} %bitcast.1.me, f32[136,128]{1,0:T(8,128)} %constant.12.clone.cos_in, f32[136,128]{1,0:T(8,128)} %constant.13.clone.sin_in, bf16[3,2304,512]{2,1,0:T(8,128)(2,1)} %fusion.5.qkv_ref, ...), custom_call_target="tpu_custom_call" | custom-call | flops 60000002048 | bytes 25165824 | tf_op jit(solution)/shard_map/pallas_call | solution.py:260
  324.6 33.5 %shard_map.217 = (bf16[288,2048]{1,0:T(8,128)(2,1)}, bf16[288,2048]{1,0:T(8,128)(2,1)}, bf16[288,2048]{1,0:T(8,128)(2,1)}, bf16[288,2048]{1,0:T(8,128)(2,1)}, bf...) custom-call(bf16[2304,512]{1,0:T(8,128)(2,1)} %get-tuple-element.80., ...), custom_call_target="tpu_custom_call" | custom-call | flops 10000000000 | bytes 2097152 | tf_op jit(solution)/shard_map/pallas_call | solution.py:382
  358.1 31.9 %shard_map.218 = (bf16[4,2048,512]{2,1,0:T(8,128)(2,1)}, bf16[288,2048]{1,0:T(8,128)(2,1)}, bf16[288,2048]{1,0:T(8,128)(2,1)}) custom-call(bf16[2304,2048]{1,0:T(8,128)(2,1)} %shard_map.213.refs_0_, bf16[3,2304,512]{2,1,0:T(8,128)(2,1)} %get-tuple-element.83.refs_1_.refs_0_.refs_2_.refs_4_, bf16[2304,2048]{1,0:T(8,128)(2,1)} %shard_map.215.refs_2_.refs_0_, ...), custom_call_target="tpu_custom_call" | custom-call | flops 10000000000 | bytes 2097152 | tf_op jit(solution)/shard_map/pallas_call | solution.py:404
  390.1 30.4 %shard_map.219 = (bf16[2304,2048]{1,0:T(8,128)(2,1)}, f32[8,2048]{1,0:T(8,128)}, bf16[288,2048]{1,0:T(8,128)(2,1)}, bf16[288,2048]{1,0:T(8,128)(2,1)}, bf16[288,...) custom-call(bf16[2304,2048]{1,0:T(8,128)(2,1)} %shard_map.215.refs_2_.refs_0_, ...), custom_call_target="tpu_custom_call" | custom-call | flops 10000000000 | bytes 2097152 | tf_op jit(solution)/shard_map/pallas_call | solution.py:404
  420.6 28.3 %shard_map.220 = (bf16[288,2048]{1,0:T(8,128)(2,1)}, bf16[288,2048]{1,0:T(8,128)(2,1)}, bf16[288,2048]{1,0:T(8,128)(2,1)}, bf16[288,2048]{1,0:T(8,128)(2,1)}, bf...) custom-call(bf16[3,2304,512]{2,1,0:T(8,128)(2,1)} %get-tuple-element.83.refs_1_.refs_0_.refs_2_.refs_4_, ...), custom_call_target="tpu_custom_call" | custom-call | flops 10000000000 | bytes 2097152 | tf_op jit(solution)/shard_map/pallas_call | solution.py:404
  448.9 31.3 %shard_map.221 = (bf16[2048,2048]{1,0:T(8,128)(2,1)}, bf16[288,2048]{1,0:T(8,128)(2,1)}, bf16[288,2048]{1,0:T(8,128)(2,1)}, f32[4,8,128]{2,1,0:T(8,128)}, f32[4,...) custom-call(bf16[2304,2048]{1,0:T(8,128)(2,1)} %shard_map.213.refs_0, ...), custom_call_target="tpu_custom_call" | custom-call | flops 10000000000 | bytes 2097152 | tf_op jit(solution)/shard_map/pallas_call | solution.py:404
  480.3 29.0 %shard_map.222 = (bf16[288,2048]{1,0:T(8,128)(2,1)}, bf16[288,2048]{1,0:T(8,128)(2,1)}, bf16[288,2048]{1,0:T(8,128)(2,1)}, bf16[288,2048]{1,0:T(8,128)(2,1)}, bf...) custom-call(bf16[3,2304,512]{2,1,0:T(8,128)(2,1)} %get-tuple-element.83.refs_1_.refs_0_.refs_2_.refs_4_, ...), custom_call_target="tpu_custom_call" | custom-call | flops 10000000000 | bytes 2097152 | tf_op jit(solution)/shard_map/pallas_call | solution.py:404
  509.7 1.5 collective-permute-start
  511.7 1.5 convert_element_type.62
  514.2 2.4 convert_add_fusion.1
  517.9 1.1 copy-done.3
  519.0 2.3 fusion.11
  521.3 16.0 %collective-permute-done.l1 = bf16[288,2048]{1,0:T(8,128)(2,1)} collective-permute-done((bf16[288,2048]{1,0:T(8,128)(2,1)}, bf16[288,2048]{1,0:T(8,128)(2,1)}, u32[]{:S(2)}, u32[]{:S(2)}) %collective-permute-start) | collective-permute-done | bytes 1179680 | tf_op jit(solution)/shard_map/ppermute | solution.py:305
  537.2 1.2 collective-permute-done.1.h0
  538.5 10.1 %shard_map.223 = (f32[576,2048]{1,0:T(8,128)}, f32[3,8,2048]{2,1,0:T(8,128)}) custom-call(bf16[288,2048]{1,0:T(8,128)(2,1)} %get-tuple-element.112.own_low, bf16[288,2048]{1,0:T(8,128)(2,1)} %get-tuple-element.117.own_high, bf16[288,2048]{1,0:T(8,128)(2,1)} %get-tuple-element.118.l0, bf16[288,2048]{1,0:T(8,128)(2,1)} %collective-permute-done.l1, ...), custom_call_target="tpu_custom_call" | custom-call | flops 10000000000 | bytes 2097152 | tf_op jit(solution)/shard_map/pallas_call | solution.py:382
  548.6 1.1 reduce_sum.27
  550.5 2.6 all-to-all-start
  553.2 1.6 add_reduce_fusion
  555.8 1.5 convert_element_type.64
  557.2 1.4 slice.86
  558.6 2.3 all-to-all-done
  561.7 21.5 %reduce-scatter.8.cloned.1.call-done = bf16[256,2048]{1,0:T(8,128)(2,1)} async-done(((bf16[2048,2048]{1,0:T(8,128)(2,1)}), bf16[256,2048]{1,0:T(8,128)(2,1)}) %reduce-scatter.8.cloned.1.call-update) | async-done | bytes 1048592 | tf_op jit(solution)/shard_map/reduce_scatter | solution.py:810
  583.2 2.8 convert_element_type.63
  (86 shorter events, 7.8 us)
Async XLA Ops:
  7.2 89.5 %all-gather.6.cloned.1.call-start = ((), (), s32[]{:S(2)}) async-start(), calls=%async_computation.5 | async-start | bytes 9437184 | tf_op jit(solution)/shard_map/all_gather | solution.py:731
  7.9 169.3 %all-gather.4.cloned.1.call-start = ((), (), s32[]{:S(2)}) async-start(), calls=%async_computation.4 | async-start | bytes 9437184 | tf_op jit(solution)/shard_map/all_gather | solution.py:733
  11.3 313.3 %all-gather.8.cloned.1.call-start = ((), (), s32[]{:S(2)}) async-start(), calls=%async_computation.6 | async-start | bytes 9437184 | tf_op jit(solution)/shard_map/all_gather | solution.py:734
  12.0 408.6 %reduce-scatter.4.cloned.1.call-start = ((), (), s32[]{:S(2)}) async-start(), calls=%async_computation.7 | async-start | bytes 9437184 | tf_op jit(solution)/shard_map/reduce_scatter | solution.py:752
  12.1 84.7 %copy-start.1 = (f32[2048]{0:T(1024)S(1)}, f32[2048]{0:T(1024)}, u32[]{:S(2)}) copy-start(f32[2048]{0:T(1024)} %param.22) | copy-start | bytes 24580
  150.7 26.5 %copy-start.26 = (f32[3,512]{1,0:T(4,128)S(1)}, f32[3,512]{1,0:T(4,128)}, u32[]{:S(2)}) copy-start(f32[3,512]{1,0:T(4,128)} %param.19) | copy-start | bytes 18436
  177.2 20.4 %copy-start.27 = (bf16[2304,2048]{1,0:T(8,128)(2,1)S(1)}, bf16[2304,2048]{1,0:T(8,128)(2,1)}, u32[]{:S(2)}) copy-start(bf16[2304,2048]{1,0:T(8,128)(2,1)} %shard_map.215.refs_2_.refs_0_) | copy-start | bytes 28311556
  221.2 290.5 %reduce-scatter.6.cloned.1.call-start = ((), (), s32[]{:S(2)}) async-start(), calls=%async_computation.8 | async-start | bytes 9437184 | tf_op jit(solution)/shard_map/reduce_scatter | solution.py:762
  390.1 193.1 %reduce-scatter.8.cloned.1.call-start = ((), (), s32[]{:S(2)}) async-start(), calls=%async_computation.9 | async-start | bytes 9437184 | tf_op jit(solution)/shard_map/reduce_scatter | solution.py:810
  480.2 29.1 %copy-start.17 = (f32[4,8,128]{2,1,0:T(8,128)S(1)}, f32[4,8,128]{2,1,0:T(8,128)}, u32[]{:S(2)}) copy-start(f32[4,8,128]{2,1,0:T(8,128)} %get-tuple-element.124.refs_4_.refs_5_.refs_6_.refs_7_.refs_8_.refs_9_.refs_10_) | copy-start | bytes 49156
  480.2 29.1 %copy-start.18 = (f32[4,8,128]{2,1,0:T(8,128)S(1)}, f32[4,8,128]{2,1,0:T(8,128)}, u32[]{:S(2)}) copy-start(f32[4,8,128]{2,1,0:T(8,128)} %get-tuple-element.125) | copy-start | bytes 49156
  480.2 29.1 %copy-start.19 = (f32[4,8,128]{2,1,0:T(8,128)S(1)}, f32[4,8,128]{2,1,0:T(8,128)}, u32[]{:S(2)}) copy-start(f32[4,8,128]{2,1,0:T(8,128)} %get-tuple-element.126) | copy-start | bytes 49156
  480.2 29.1 %copy-start.20 = (f32[4,8,128]{2,1,0:T(8,128)S(1)}, f32[4,8,128]{2,1,0:T(8,128)}, u32[]{:S(2)}) copy-start(f32[4,8,128]{2,1,0:T(8,128)} %get-tuple-element.127) | copy-start | bytes 49156
  480.2 29.1 %copy-start.21 = (f32[4,8,128]{2,1,0:T(8,128)S(1)}, f32[4,8,128]{2,1,0:T(8,128)}, u32[]{:S(2)}) copy-start(f32[4,8,128]{2,1,0:T(8,128)} %get-tuple-element.128) | copy-start | bytes 49156
  480.3 29.1 %copy-start.22 = (f32[4,8,128]{2,1,0:T(8,128)S(1)}, f32[4,8,128]{2,1,0:T(8,128)}, u32[]{:S(2)}) copy-start(f32[4,8,128]{2,1,0:T(8,128)} %get-tuple-element.129) | copy-start | bytes 49156
  480.3 29.1 %copy-start.23 = (f32[4,8,128]{2,1,0:T(8,128)S(1)}, f32[4,8,128]{2,1,0:T(8,128)}, u32[]{:S(2)}) copy-start(f32[4,8,128]{2,1,0:T(8,128)} %get-tuple-element.130) | copy-start | bytes 49156
  480.3 29.1 %copy-start.24 = (f32[4,8,128]{2,1,0:T(8,128)S(1)}, f32[4,8,128]{2,1,0:T(8,128)}, u32[]{:S(2)}) copy-start(f32[4,8,128]{2,1,0:T(8,128)} %get-tuple-element.131) | copy-start | bytes 49156
  509.3 4.0 copy-start.4
  509.7 27.5 %collective-permute-start = (bf16[288,2048]{1,0:T(8,128)(2,1)}, bf16[288,2048]{1,0:T(8,128)(2,1)}, u32[]{:S(2)}, u32[]{:S(2)}) collective-permute-start(bf16[288,2048]{1,0:T(8,128)(2,1)} %get-tuple-element.119), channel_id=1, source_target_pairs={{0,2},{1,3},{2,0},{3,1},{4,6},{5,7},{6,4},{7,5},{8,10},{9,11},{10,... | collective-permute-start | bytes 3538952 | tf_op jit(solution)/shard_map/ppermute | solution.py:305
  511.2 27.2 %collective-permute-start.1 = (bf16[288,2048]{1,0:T(8,128)(2,1)}, bf16[288,2048]{1,0:T(8,128)(2,1)}, u32[]{:S(2)}, u32[]{:S(2)}) collective-permute-start(bf16[288,2048]{1,0:T(8,128)(2,1)} %get-tuple-element.120), channel_id=1, source_target_pairs={{0,1},{1,0},{2,3},{3,2},{4,5},{5,4},{6,7},{7,6},{8,9},{9,8},{10,11... | collective-permute-start | bytes 3538952 | tf_op jit(solution)/shard_map/ppermute | solution.py:305
  514.2 3.1 copy-start.7
  514.2 3.1 copy-start.8
  538.5 14.6 %copy-start.10 = (f32[8,2048]{1,0:T(8,128)S(1)}, f32[8,2048]{1,0:T(8,128)}, u32[]{:S(2)}) copy-start(f32[8,2048]{1,0:T(8,128)} %get-tuple-element.132.refs_11_.refs_12_.refs_13_.refs_14_.refs_15_.refs_16_.refs_17_) | copy-start | bytes 196612
  538.5 14.6 %copy-start.11 = (f32[8,2048]{1,0:T(8,128)S(1)}, f32[8,2048]{1,0:T(8,128)}, u32[]{:S(2)}) copy-start(f32[8,2048]{1,0:T(8,128)} %get-tuple-element.133) | copy-start | bytes 196612
  538.5 14.7 %copy-start.12 = (f32[8,2048]{1,0:T(8,128)S(1)}, f32[8,2048]{1,0:T(8,128)}, u32[]{:S(2)}) copy-start(f32[8,2048]{1,0:T(8,128)} %get-tuple-element.134) | copy-start | bytes 196612
  538.5 14.7 %copy-start.13 = (f32[8,2048]{1,0:T(8,128)S(1)}, f32[8,2048]{1,0:T(8,128)}, u32[]{:S(2)}) copy-start(f32[8,2048]{1,0:T(8,128)} %get-tuple-element.135) | copy-start | bytes 196612
  538.5 14.7 %copy-start.14 = (f32[8,2048]{1,0:T(8,128)S(1)}, f32[8,2048]{1,0:T(8,128)}, u32[]{:S(2)}) copy-start(f32[8,2048]{1,0:T(8,128)} %get-tuple-element.136) | copy-start | bytes 196612
  538.5 14.7 %copy-start.15 = (f32[8,2048]{1,0:T(8,128)S(1)}, f32[8,2048]{1,0:T(8,128)}, u32[]{:S(2)}) copy-start(f32[8,2048]{1,0:T(8,128)} %get-tuple-element.137) | copy-start | bytes 196612
  538.5 14.7 %copy-start.16 = (f32[8,2048]{1,0:T(8,128)S(1)}, f32[8,2048]{1,0:T(8,128)}, u32[]{:S(2)}) copy-start(f32[8,2048]{1,0:T(8,128)} %get-tuple-element.138) | copy-start | bytes 196612
  548.6 7.2 %copy-start.9 = (bf16[2048,256]{1,0:T(8,128)(2,1)S(1)}, bf16[2048,256]{1,0:T(8,128)(2,1)}, u32[]{:S(2)}) copy-start(bf16[2048,256]{1,0:T(8,128)(2,1)} %reduce-scatter.4.cloned.1.call-done) | copy-start | bytes 3145732
  550.5 10.4 %all-to-all-start = ((f32[32,1,192]{2,1,0:T(1,128)}), f32[32,1,192]{2,1,0:T(1,128)S(1)}, u32[]{:S(2)}, u32[]{:S(2)}) async-start(f32[32,1,192]{2,1,0:T(1,128)} %all_to_all.8), calls=%async_computation.1 | async-start | bytes 65536 | tf_op jit(solution)/shard_map/all_to_all | solution.py:825
  553.2 4.1 copy-start.2
  (5 other events, 11.2 us)
Sparse Core Ops, SparseCore 0:
  9.6 84.7 all-gather.5
  96.6 80.5 all-gather.3
  178.8 81.0 all-gather.7
  262.0 87.8 reduce-scatter.3
  390.2 99.5 reduce-scatter.5
  491.9 91.2 reduce-scatter.7

commit v4 on v3

--- a/solution.py
+++ b/solution.py
@@ -127,12 +127,15 @@
         def lanes(x, i):
             return x[:, i * SEG:(i + 1) * SEG]
 
-        def left(ref, piece, rhs):
+        def left(ref, piece, stack):
             o, start, size, kind = piece
             if kind == 'pair':
-                return jnp.concatenate(
-                    [dot_nt(ref[halves[i], :], part(rhs, i)) for i in both], axis=1)
-            return dot_nt(ref[seg_at(start, size), :], rhs)
+                each = [
+                    dot_nt(ref[halves[i], :], jnp.concatenate([part(stack, i), part(stack, 2 + i)], axis=0))
+                    for i in both]
+                return [jnp.concatenate([lanes(x, h) for x in each], axis=1) for h in both]
+            x = dot_nt(ref[seg_at(start, size), :], stack)
+            return [x[:, h * step : (h + 1) * step] for h in both]
 
         def turned(ref, h, piece, x):
             o, start, size, kind = piece
@@ -159,8 +162,9 @@
         sums = [[], []]
         for piece in pieces:
             o, start, size, kind = piece
+            scores = left(kr, piece, q_stack)
             for h in both:
-                s = left(kr, piece, qh[h])
+                s = scores[h]
                 if kind == 'tri':
                     s = jnp.where(tri_mask, s, NEG)
                 if kind == 'pair':
@@ -197,9 +201,9 @@
         for n, piece in enumerate(pieces):
             o, start, size, kind = piece
             low = []
+            dps = left(vr, piece, d_stack)
             for h in both:
-                dp = left(vr, piece, dh[h])
-                low.append((s_ref[h, o:o + size, :] * (dp - deltas[h])).astype(bf16))
+                low.append((s_ref[h, o:o + size, :] * (dps[h] - deltas[h])).astype(bf16))
                 dq_acc[h] = dq_acc[h] + turned(kt, h, piece, low[h])
             add_rows(dk, piece, low, q_stack)
         o_rows = jnp.concatenate(o_acc, axis=0).T.astype(bf16)
@@ -466,29 +470,20 @@
     return {at(i) * cut + n: results[i * cut + n] for i in range(blocks) for n in range(cut)}, got
 
 
-def head_grads(normed, grad_qkv, cot, attended, tile, carry):
+def qkv_grads(normed, grad_qkv, tile, carry):
     rows, model = normed.shape
-    width = attended.shape[1]
-    last = model // tile - 1
-
-    def inner(n_ref, g_ref, c_ref, a_ref, o_ref):
-        @pl.when(pl.program_id(0) < 3)
-        def _():
-            o_ref[...] = dot_tn(n_ref[...], g_ref[...]).astype(bf16)
-
-        @pl.when(pl.program_id(0) == 3)
-        def _():
-            o_ref[...] = dot_tn(c_ref[...], a_ref[...]).astype(bf16)
+    width = grad_qkv.shape[2]
+
+    def inner(n_ref, g_ref, o_ref):
+        o_ref[...] = dot_tn(n_ref[...], g_ref[...]).astype(bf16)
 
     (grads,), got = tiled(
-        inner, (4, model // tile),
+        inner, (3, model // tile),
         [
-            (normed, (rows, tile), lambda c, i: (0, i + (last - i) * (c // 3))),
-            (grad_qkv, (None, rows, width), lambda c, i: (c - c // 3, 0, 0)),
-            (cot, (rows, tile), lambda c, i: (0, i * (c // 3))),
-            (attended, (rows, width), lambda c, i: (0, 0)),
+            (normed, (rows, tile), lambda c, i: (0, i)),
+            (grad_qkv, (None, rows, width), lambda c, i: (c, 0, 0)),
         ],
-        [((4, model, width), bf16, (None, tile, width), lambda c, i: (c, i, 0))], carry)
+        [((3, model, width), bf16, (None, tile, width), lambda c, i: (c, i, 0))], carry)
     return grads, got
 
 
@@ -525,6 +520,24 @@
         ],
         [out, out], carry, 48)
     return value, slope, got
+
+
+def project(normed, qkv_w, b_qkv, r_tile, carry):
+    rows, model = normed.shape
+    width = qkv_w.shape[2]
+
+    def inner(n_ref, w_ref, b_ref, o_ref):
+        o_ref[...] = (dot_nn(n_ref[...], w_ref[...]) + b_ref[...]).astype(bf16)
+
+    (out,), got = tiled(
+        inner, (3, rows // r_tile),
+        [
+            (normed, (r_tile, model), lambda c, i: (i, 0)),
+            (qkv_w, (None, model, width), lambda c, i: (c, 0, 0)),
+            (b_qkv[:, None], (None, 1, width), lambda c, i: (c, 0, 0)),
+        ],
+        [((3, rows, width), bf16, (None, r_tile, width), lambda c, i: (c, i, 0))], carry)
+    return out, got
 
 
 def hidden_grad(cot, down_w, slope, r_tile, f_tile, carry, adds):
@@ -729,8 +742,8 @@
 
     tables = rope_tables()
     up_w = lax.all_gather(w_fc1, "dp", axis=0, tiled=True)
-    w_heads = jnp.concatenate([w_qkv, jnp.transpose(w_out)[None]], axis=0)
-    heads_w = lax.all_gather(w_heads, "dp", axis=1, tiled=True)
+    qkv_w = lax.all_gather(w_qkv, "dp", axis=1, tiled=True)
+    out_w = lax.all_gather(w_out, "dp", axis=1, tiled=True)
     down_w = lax.all_gather(w_fc2, "dp", axis=1, tiled=True)
     if four:
         normed = norm_gather(tokens, ln_gain, ln_bias, 1)
@@ -741,31 +754,30 @@
             for x in (normed_local, cotangent))
     activated, slope, got = hidden_forward(
         normed, up_w, b_fc1, local_rows, half_cols, gather_sides(cotangent, 2) if four else None)
+    projected, got = project(
+        after(normed, activated), qkv_w, b_qkv, local_rows, gather_corner(got[0], 3) if four else None)
     if four:
-        cot_full = tiled(None, (), [], [], gather_corner(got[0], 3))[1][0]
-    projected = (
-        jnp.einsum(
-            "td,cdh->cth", after(normed, activated, cot_full), heads_w[:3], preferred_element_type=f32)
-        + b_qkv[:, None, :]
-    ).astype(bf16)
+        cot_full = got[0]
     grad_w_fc2 = dot_tn(after(activated, projected), cot_full).astype(bf16)
     summed_fc2 = lax.psum_scatter(grad_w_fc2, "dp", scatter_dimension=1, tiled=True)
-    grad_attended = dot_nn(after(cot_full, grad_w_fc2), heads_w[3]).astype(bf16)
+    grad_attended = dot_nt(after(cot_full, grad_w_fc2), out_w).astype(bf16)
     attended, grad_qkv, aux = attention(parents[0], me[None], size, *tables, projected, grad_attended)
 
+    grad_w_out = dot_tn(attended, cot_full).astype(bf16)
+    summed_out = lax.psum_scatter(grad_w_out, "dp", scatter_dimension=1, tiled=True)
     branch, ignored = chunk_matmul(
-        [(attended, heads_w, -1, 3), (activated, down_w, -1, None)],
+        [(after(attended, grad_w_out), out_w, -1, None), (activated, down_w, -1, None)],
         model, half_cols, size, size, lambda i: i, cut=2)
-    grad_w_heads, got = head_grads(
-        after(normed, branch[0]), grad_qkv, cot_full, attended, half_cols,
+    grad_w_qkv, got = qkv_grads(
+        after(normed, branch[0]), grad_qkv, half_cols,
         sending(4, (branch[6],) + t1, (branch[7],) + t2) if four else None)
-    summed_heads = lax.psum_scatter(grad_w_heads, "dp", scatter_dimension=1, tiled=True)
+    summed_qkv = lax.psum_scatter(grad_w_qkv, "dp", scatter_dimension=1, tiled=True)
     grad_hidden, sums_fc1, branch_next, side = hidden_grad(
-        after(cot_full, grad_w_heads), down_w, slope, local_rows, half_cols,
+        after(cot_full, grad_w_qkv), down_w, slope, local_rows, half_cols,
         sending(5, (branch[2],) + t1, (branch[5],) + t2) if four else None,
         [(branch[3], got[1]), (branch[4], got[0])] if four else [])
     dp_bits = range(1, groups)
-    backs = [(grad_qkv, heads_w, c, c) for c in range(3)] + [(after(grad_hidden, summed_fc2), up_w, -1, -1)]
+    backs = [(grad_qkv, qkv_w, c, c) for c in range(3)] + [(after(grad_hidden, summed_fc2), up_w, -1, -1)]
     if four:
         far, last = chunk_matmul(
             backs, model, half_cols, 8, 4, lambda i: 7 - i - 2 * (i // 3),
@@ -774,7 +786,7 @@
             branch[0].astype(f32) + side[0].astype(f32) + last[1].astype(f32),
             branch[1].astype(f32) + last[0].astype(f32) + side[1].astype(f32)]
         grad_w_fc1, got = weight_grad(
-            after(normed, far[7]), grad_hidden, half_cols, half_cols,
+            after(normed, far[7], summed_out), grad_hidden, half_cols, half_cols,
             sending(
                 7, (far[6],) + t1, (far[7],) + t2,
                 *[(aux, "dp", bits) for bits in dp_bits], *[(sums_fc1, "dp", bits) for bits in dp_bits]))
@@ -790,6 +802,7 @@
         branch_sum[0] = after(branch_sum[0], near[0])
         all_aux[0] = after(aux, near[0])
         all_fc1[0] = after(sums_fc1, near[0])
+        summed_qkv, summed_out, summed_fc2 = lax.optimization_barrier((summed_qkv, summed_out, summed_fc2, near[0]))[:3]
     else:
         parts, ignored = chunk_matmul(backs, model, half_cols, size, size, lambda i: i, cut=2)
         grad_w_fc1, ignored = weight_grad(normed, grad_hidden, half_cols, half_cols, None)
@@ -810,9 +823,8 @@
     summed_fc1 = lax.psum_scatter(grad_w_fc1, "dp", scatter_dimension=0, tiled=True)
     output_rows = (
         tokens.astype(f32) + jnp.concatenate(branch_sum, axis=0) + resid_bias).astype(bf16)
-    summed_fc1, summed_heads, summed_fc2 = (
-        w.astype(f32) for w in (summed_fc1, summed_heads, summed_fc2))
-    summed_qkv, summed_out = summed_heads[:3], jnp.transpose(summed_heads[3])
+    summed_fc1, summed_qkv, summed_out, summed_fc2 = (
+        w.astype(f32) for w in (summed_fc1, summed_qkv, summed_out, summed_fc2))
 
     bias_qkv = jnp.transpose(sum(a[:, :3] for a in all_aux), (1, 0, 2)).reshape(3, width)
     bias_fc1 = jnp.sum(sum(all_fc1), axis=0)

time: 602 us -> 593 us (0.985)
  matrix products: 54.3 us -> 46.6 us
    dot_general x2 -> x1, matrix products: 30.7 us -> 10.5 us  [dot_nt(): lax.dot_general(a, b, (((1,), (1,)), ((), ())), preferred_element_type=f32)]
    dot_general x1 -> x2, matrix products: 23.6 us -> 36.1 us  [dot_tn(): lax.dot_general(a, b, (((0,), (0,)), ((), ())), preferred_element_type=f32)]
    all_gather x1 -> x2, waiting for transfers between devices: 0.18 us -> 8.71 us  [the longest x1 8.69 us: body(): qkv_w = lax.all_gather(w_qkv, 'dp', axis=1, tiled=True)]
  transfers between devices with their start and end apart: 9 -> 11, of which waited for: 5 -> 5; matrix products, arithmetic and copies ran while one was open for 12% -> 11% of each run, Pallas kernels for 76% -> 76%
where the time goes in v4:
time: 593 us; the launch traced here: 585 us
  Pallas kernels  446 us (75%)
  waiting for transfers between devices  48.5 us (8%)
  matrix products  46.6 us (8%)
  other arithmetic  16.6 us (3%)
  between operations  14.8 us (2%)
  local copies, waits for them, and re-layouts  6.48 us (1%)
  starting transfers between devices  6.4 us (1%)
    pallas_call x7, Pallas kernels, tiled(): pl.pallas_call(kernel, in_specs=[any_spec] * (n_in + n_src), out_specs=[a...  228 us
    pallas_call x1, Pallas kernels, attention(): pl.pallas_call(functools.partial(attn_kernel, size), out_shape=(jax.Shape...  89.5 us
    pallas_call x1, Pallas kernels, norm_gather(): pl.pallas_call(kernel, in_specs=[pl.BlockSpec(memory_space=pltpu.VMEM)] *...  84.6 us
    pallas_call x2, Pallas kernels, tiled(): pl.pallas_call(inner, grid=grid, in_specs=in_specs, out_specs=out_specs,...  43.2 us
    dot_general x2, matrix products, dot_tn(): lax.dot_general(a, b, (((0,), (0,)), ((), ())), preferred_element_type=f32)  36.1 us
    reduce_scatter x1, waiting for transfers between devices, body(): lax.psum_scatter(grad_w_fc1, 'dp', scatter_dimension=0, tiled=True)  17.6 us
    ppermute x2, waiting for transfers between devices, xor_send(): return lax.ppermute(x, 'tensor', [(i, i ^ bits) for i in range(size)])  17.2 us
  transfers between devices with their start and end apart: 11, of which 5 were waited for; matrix products, arithmetic and copies ran while one was open for 11% of the time, Pallas kernels for 76%

profile of v4, /device:TPU:0, one launch (start us, length us, event | category | flops | bytes accessed | tf_op | source)
XLA Modules:
  0.0 585.2 jit_solution(12202373021716962820)
XLA Ops:
  10.6 84.6 %shard_map.213.refs_0_ = bf16[2304,2048]{1,0:T(8,128)(2,1)} custom-call(bf16[576,2048]{1,0:T(8,128)(2,1)} %t_ref.1, f32[1,2048]{1,0:T(1,128)} %bitcast.19, f32[1,2048]{1,0:T(1,128)} %bitcast.18), custom_call_target="tpu_custom_call" | custom-call | flops 10000000000 | bytes 2097152 | tf_op jit(solution)/shard_map/pallas_call | solution.py:618
  95.3 1.7 copy-done
  97.0 53.6 %shard_map.214 = (bf16[2304,2048]{1,0:T(8,128)(2,1)}, bf16[2304,2048]{1,0:T(8,128)(2,1)}, bf16[2304,2048]{1,0:T(8,128)(2,1)}) custom-call(bf16[2304,2048]{1,0:T(8,128)(2,1)} %shard_map.213.refs_0_, bf16[2048,2048]{1,0:T(8,128)(2,1)} %all-gather.5.cloned.1.call-done.refs_1_.refs_7_, f32[1,2048]{1,0:T(1,128)S(1)} %bitcast.16, bf16[576,2048]{1,0:T(8,128)(2,1)S(1)} %copy-done), custom_call_target="tpu_custom_call" | custom-call | flops 10000000000 | bytes 2097152 | tf_op jit(solution)/shard_map/pallas_call | solution.py:408
  150.6 8.7 %all-gather.7.cloned.1.call-done.refs_1_.refs_3_.refs_5_ = bf16[3,2048,512]{2,1,0:T(8,128)(2,1)} async-done(((bf16[3,256,512]{2,1,0:T(8,128)(2,1)}), bf16[3,2048,512]{2,1,0:T(8,128)(2,1)}) %all-gather.7.cloned.1.call-update) | async-done | bytes 6291472 | tf_op jit(solution)/shard_map/all_gather | solution.py:745
  159.3 29.4 %shard_map.215 = (bf16[3,2304,512]{2,1,0:T(8,128)(2,1)}, bf16[2304,2048]{1,0:T(8,128)(2,1)}) custom-call(bf16[2304,2048]{1,0:T(8,128)(2,1)} %shard_map.213.refs_0_, bf16[3,2048,512]{2,1,0:T(8,128)(2,1)} %all-gather.7.cloned.1.call-done.refs_1_.refs_3_.refs_5_, f32[3,1,512]{2,1,0:T(1,128)} %broadcast_in_dim.24.refs_2_, ...), custom_call_target="tpu_custom_call", output_to_operand_aliasing={{1}: (3, {})} | custom-call | flops 10000000000 | bytes 2097152 | tf_op jit(solution)/shard_map/pallas_call | solution.py:408
  188.7 26.3 %convolution_convert_fusion = bf16[2048,2048]{1,0:T(8,128)(2,1)} fusion(bf16[2304,2048]{1,0:T(8,128)(2,1)} %get-tuple-element.86.refs_2_, bf16[2304,2048]{1,0:T(8,128)(2,1)} %get-tuple-element.96.refs_0_), kind=kOutput, calls=%fused_computation | convolution fusion | flops 19331547136 | bytes 27262976 | tf_op jit(solution)/shard_map/dot_general | solution.py:305
  215.3 10.5 %convolution_convert_fusion.1.do_in = bf16[2304,512]{1,0:T(8,128)(2,1)} fusion(bf16[2304,2048]{1,0:T(8,128)(2,1)} %get-tuple-element.96.refs_0_, bf16[512,2048]{1,0:T(8,128)(2,1)} %all-gather.9.cloned.1.call-done.refs_1_), kind=kOutput, calls=%fused_computation.4 | convolution fusion | flops 4833017856 | bytes 13893632 | tf_op jit(solution)/shard_map/dot_general | solution.py:29
  225.8 89.5 %shard_map.216 = (bf16[2304,512]{1,0:T(8,128)(2,1)}, bf16[3,2304,512]{2,1,0:T(8,128)(2,1)}, f32[4,8,128]{2,1,0:T(8,128)}) custom-call(s32[18]{0:T(128)} %bitcast.21, s32[1]{0:T(128)} %bitcast.1.me, f32[136,128]{1,0:T(8,128)} %constant.12.clone.cos_in, f32[136,128]{1,0:T(8,128)} %constant.13.clone.sin_in, bf16[3,2304,512]{2,1,0:T(8,128)(2,1)} %get-tuple-element.84.qkv_ref, ...), custom_call_target="tpu_custom_call" | custom-call | flops 60000002048 | bytes 25165824 | tf_op jit(solution)/shard_map/pallas_call | solution.py:264
  315.3 9.8 %convolution_convert_fusion.2 = bf16[512,2048]{1,0:T(8,128)(2,1)} fusion(bf16[2304,512]{1,0:T(8,128)(2,1)} %get-tuple-element.89.refs_0_, bf16[2304,2048]{1,0:T(8,128)(2,1)} %get-tuple-element.96.refs_0_), kind=kOutput, calls=%fused_computation.5 | convolution fusion | flops 4832886784 | bytes 13893632 | tf_op jit(solution)/shard_map/dot_general | solution.py:305
  325.2 33.0 %shard_map.217 = (bf16[288,2048]{1,0:T(8,128)(2,1)}, bf16[288,2048]{1,0:T(8,128)(2,1)}, bf16[288,2048]{1,0:T(8,128)(2,1)}, bf16[288,2048]{1,0:T(8,128)(2,1)}, bf...) custom-call(bf16[2304,512]{1,0:T(8,128)(2,1)} %get-tuple-element.89., ...), custom_call_target="tpu_custom_call" | custom-call | flops 10000000000 | bytes 2097152 | tf_op jit(solution)/shard_map/pallas_call | solution.py:386
  358.2 27.8 %shard_map.218 = (bf16[3,2048,512]{2,1,0:T(8,128)(2,1)}, bf16[288,2048]{1,0:T(8,128)(2,1)}, bf16[288,2048]{1,0:T(8,128)(2,1)}) custom-call(bf16[2304,2048]{1,0:T(8,128)(2,1)} %shard_map.213.refs_0_, bf16[3,2304,512]{2,1,0:T(8,128)(2,1)} %get-tuple-element.92.refs_1_.refs_0_.refs_2_.refs_4_, bf16[288,2048]{1,0:T(8,128)(2,1)} %get-tuple-element.93.refs_2_, ...), custom_call_target="tpu_custom_call" | custom-call | flops 10000000000 | bytes 2097152 | tf_op jit(solution)/shard_map/pallas_call | solution.py:408
  386.1 29.6 %shard_map.219 = (bf16[2304,2048]{1,0:T(8,128)(2,1)}, f32[8,2048]{1,0:T(8,128)}, bf16[288,2048]{1,0:T(8,128)(2,1)}, bf16[288,2048]{1,0:T(8,128)(2,1)}, bf16[288,...) custom-call(bf16[2304,2048]{1,0:T(8,128)(2,1)} %get-tuple-element.96.refs_0_, ...), custom_call_target="tpu_custom_call" | custom-call | flops 10000000000 | bytes 2097152 | tf_op jit(solution)/shard_map/pallas_call | solution.py:408
  415.7 29.3 %shard_map.220 = (bf16[288,2048]{1,0:T(8,128)(2,1)}, bf16[288,2048]{1,0:T(8,128)(2,1)}, bf16[288,2048]{1,0:T(8,128)(2,1)}, bf16[288,2048]{1,0:T(8,128)(2,1)}, bf...) custom-call(bf16[3,2304,512]{2,1,0:T(8,128)(2,1)} %get-tuple-element.92.refs_1_.refs_0_.refs_2_.refs_4_, ...), custom_call_target="tpu_custom_call" | custom-call | flops 10000000000 | bytes 2097152 | tf_op jit(solution)/shard_map/pallas_call | solution.py:408
  445.0 28.5 %shard_map.221 = (bf16[2048,2048]{1,0:T(8,128)(2,1)}, bf16[288,2048]{1,0:T(8,128)(2,1)}, bf16[288,2048]{1,0:T(8,128)(2,1)}, f32[4,8,128]{2,1,0:T(8,128)}, f32[4,...) custom-call(bf16[2304,2048]{1,0:T(8,128)(2,1)} %shard_map.213.refs_0, ...), custom_call_target="tpu_custom_call" | custom-call | flops 10000000000 | bytes 2097152 | tf_op jit(solution)/shard_map/pallas_call | solution.py:408
  473.6 30.2 %shard_map.222 = (bf16[288,2048]{1,0:T(8,128)(2,1)}, bf16[288,2048]{1,0:T(8,128)(2,1)}, bf16[288,2048]{1,0:T(8,128)(2,1)}, bf16[288,2048]{1,0:T(8,128)(2,1)}, bf...) custom-call(bf16[3,2304,512]{2,1,0:T(8,128)(2,1)} %get-tuple-element.92.refs_1_.refs_0_.refs_2_.refs_4_, ...), custom_call_target="tpu_custom_call" | custom-call | flops 10000000000 | bytes 2097152 | tf_op jit(solution)/shard_map/pallas_call | solution.py:408
  504.6 1.5 collective-permute-start.1
  506.1 0.9 multiply_convert_fusion
  507.0 2.8 convert_add_fusion.1
  511.1 1.0 copy-done.2
  512.1 2.3 fusion.1
  514.3 17.2 %collective-permute-done.l1 = bf16[288,2048]{1,0:T(8,128)(2,1)S(1)} collective-permute-done((bf16[288,2048]{1,0:T(8,128)(2,1)}, bf16[288,2048]{1,0:T(8,128)(2,1)S(1)}, u32[]{:S(2)}, u32[]{:S(2)}) %collective-permute-start) | collective-permute-done | bytes 1179680 | tf_op jit(solution)/shard_map/ppermute | solution.py:309
  531.6 1.0 copy-done.27
  533.0 10.2 %shard_map.223 = (f32[576,2048]{1,0:T(8,128)}, f32[3,8,2048]{2,1,0:T(8,128)}) custom-call(bf16[288,2048]{1,0:T(8,128)(2,1)} %get-tuple-element.121.own_low, bf16[288,2048]{1,0:T(8,128)(2,1)} %get-tuple-element.126.own_high, bf16[288,2048]{1,0:T(8,128)(2,1)} %get-tuple-element.127.l0, bf16[288,2048]{1,0:T(8,128)(2,1)} %copy-done.27, ...), custom_call_target="tpu_custom_call" | custom-call | flops 10000000000 | bytes 2097152 | tf_op jit(solution)/shard_map/pallas_call | solution.py:386
  543.2 1.1 reduce_sum.27
  544.4 0.7 all_to_all.8
  545.1 4.1 all-to-all-start
  549.9 0.8 convert_element_type.63
  550.7 2.5 convert_element_type.62
  553.2 1.5 convert_element_type.65
  554.7 2.3 all-to-all-done
  557.7 17.6 %reduce-scatter.11.cloned.1.call-done = bf16[256,2048]{1,0:T(8,128)(2,1)} async-done(((bf16[2048,2048]{1,0:T(8,128)(2,1)}), bf16[256,2048]{1,0:T(8,128)(2,1)}) %reduce-scatter.11.cloned.1.call-update) | async-done | bytes 1048592 | tf_op jit(solution)/shard_map/reduce_scatter | solution.py:823
  575.3 2.8 convert_element_type.64
  (91 shorter events, 7.8 us)
Async XLA Ops:
  7.2 88.1 %all-gather.5.cloned.1.call-start = ((), (), s32[]{:S(2)}) async-start(), calls=%async_computation.5 | async-start | bytes 9437184 | tf_op jit(solution)/shard_map/all_gather | solution.py:744
  7.9 151.4 %all-gather.7.cloned.1.call-start = ((), (), s32[]{:S(2)}) async-start(), calls=%async_computation.6 | async-start | bytes 7077888 | tf_op jit(solution)/shard_map/all_gather | solution.py:745
  8.7 206.6 %all-gather.9.cloned.1.call-start = ((), (), s32[]{:S(2)}) async-start(), calls=%async_computation.7 | async-start | bytes 2359296 | tf_op jit(solution)/shard_map/all_gather | solution.py:746
  9.4 315.8 %all-gather.11.cloned.1.call-start = ((), (), s32[]{:S(2)}) async-start(), calls=%async_computation.8 | async-start | bytes 9437184 | tf_op jit(solution)/shard_map/all_gather | solution.py:747
  10.0 405.7 %reduce-scatter.5.cloned.1.call-start = ((), (), s32[]{:S(2)}) async-start(), calls=%async_computation.9 | async-start | bytes 9437184 | tf_op jit(solution)/shard_map/reduce_scatter | solution.py:762
  10.6 84.7 %copy-start.1 = (f32[2048]{0:T(1024)S(1)}, f32[2048]{0:T(1024)}, u32[]{:S(2)}) copy-start(f32[2048]{0:T(1024)} %param.22) | copy-start | bytes 24580
  215.0 229.9 %reduce-scatter.7.cloned.1.call-start = ((), (), s32[]{:S(2)}) async-start(), calls=%async_computation.10 | async-start | bytes 2359296 | tf_op jit(solution)/shard_map/reduce_scatter | solution.py:767
  325.1 224.8 %reduce-scatter.9.cloned.1.call-start = ((), (), s32[]{:S(2)}) async-start(), calls=%async_computation.11 | async-start | bytes 7077888 | tf_op jit(solution)/shard_map/reduce_scatter | solution.py:774
  386.0 189.3 %reduce-scatter.11.cloned.1.call-start = ((), (), s32[]{:S(2)}) async-start(), calls=%async_computation.12 | async-start | bytes 9437184 | tf_op jit(solution)/shard_map/reduce_scatter | solution.py:823
  473.5 30.3 %copy-start.17 = (f32[4,8,128]{2,1,0:T(8,128)S(1)}, f32[4,8,128]{2,1,0:T(8,128)}, u32[]{:S(2)}) copy-start(f32[4,8,128]{2,1,0:T(8,128)} %get-tuple-element.134.refs_4_.refs_5_.refs_6_.refs_7_.refs_8_.refs_9_.refs_10_) | copy-start | bytes 49156
  473.5 30.3 %copy-start.18 = (f32[4,8,128]{2,1,0:T(8,128)S(1)}, f32[4,8,128]{2,1,0:T(8,128)}, u32[]{:S(2)}) copy-start(f32[4,8,128]{2,1,0:T(8,128)} %get-tuple-element.135) | copy-start | bytes 49156
  473.6 30.3 %copy-start.19 = (f32[4,8,128]{2,1,0:T(8,128)S(1)}, f32[4,8,128]{2,1,0:T(8,128)}, u32[]{:S(2)}) copy-start(f32[4,8,128]{2,1,0:T(8,128)} %get-tuple-element.136) | copy-start | bytes 49156
  473.6 30.3 %copy-start.20 = (f32[4,8,128]{2,1,0:T(8,128)S(1)}, f32[4,8,128]{2,1,0:T(8,128)}, u32[]{:S(2)}) copy-start(f32[4,8,128]{2,1,0:T(8,128)} %get-tuple-element.137) | copy-start | bytes 49156
  473.6 30.3 %copy-start.21 = (f32[4,8,128]{2,1,0:T(8,128)S(1)}, f32[4,8,128]{2,1,0:T(8,128)}, u32[]{:S(2)}) copy-start(f32[4,8,128]{2,1,0:T(8,128)} %get-tuple-element.138) | copy-start | bytes 49156
  473.6 30.3 %copy-start.22 = (f32[4,8,128]{2,1,0:T(8,128)S(1)}, f32[4,8,128]{2,1,0:T(8,128)}, u32[]{:S(2)}) copy-start(f32[4,8,128]{2,1,0:T(8,128)} %get-tuple-element.139) | copy-start | bytes 49156
  473.6 30.3 %copy-start.23 = (f32[4,8,128]{2,1,0:T(8,128)S(1)}, f32[4,8,128]{2,1,0:T(8,128)}, u32[]{:S(2)}) copy-start(f32[4,8,128]{2,1,0:T(8,128)} %get-tuple-element.140) | copy-start | bytes 49156
  473.6 30.3 %copy-start.24 = (f32[4,8,128]{2,1,0:T(8,128)S(1)}, f32[4,8,128]{2,1,0:T(8,128)}, u32[]{:S(2)}) copy-start(f32[4,8,128]{2,1,0:T(8,128)} %get-tuple-element.141) | copy-start | bytes 49156
  473.6 32.5 %copy-start.3 = (bf16[3,256,512]{2,1,0:T(8,128)(2,1)S(1)}, bf16[3,256,512]{2,1,0:T(8,128)(2,1)}, u32[]{:S(2)}) copy-start(bf16[3,256,512]{2,1,0:T(8,128)(2,1)} %param.18) | copy-start | bytes 2359300
  504.3 27.2 %collective-permute-start = (bf16[288,2048]{1,0:T(8,128)(2,1)}, bf16[288,2048]{1,0:T(8,128)(2,1)S(1)}, u32[]{:S(2)}, u32[]{:S(2)}) collective-permute-start(bf16[288,2048]{1,0:T(8,128)(2,1)} %get-tuple-element.128), channel_id=1, source_target_pairs={{0,2},{1,3},{2,0},{3,1},{4,6},{5,7},{6,4},{7,5},{8,10},{9,11},{10,... | collective-permute-start | bytes 3538952 | tf_op jit(solution)/shard_map/ppermute | solution.py:309
  504.6 27.0 %collective-permute-start.1 = (bf16[288,2048]{1,0:T(8,128)(2,1)}, bf16[288,2048]{1,0:T(8,128)(2,1)S(1)}, u32[]{:S(2)}, u32[]{:S(2)}) collective-permute-start(bf16[288,2048]{1,0:T(8,128)(2,1)} %get-tuple-element.129), channel_id=1, source_target_pairs={{0,1},{1,0},{2,3},{3,2},{4,5},{5,4},{6,7},{7,6},{8,9},{9,8},{10,11... | collective-permute-start | bytes 3538952 | tf_op jit(solution)/shard_map/ppermute | solution.py:309
  507.0 3.4 copy-start.6
  532.9 16.3 %copy-start.9 = (f32[8,2048]{1,0:T(8,128)S(1)}, f32[8,2048]{1,0:T(8,128)}, u32[]{:S(2)}) copy-start(f32[8,2048]{1,0:T(8,128)} %get-tuple-element.143.refs_11_.refs_12_.refs_13_.refs_14_.refs_15_.refs_16_.refs_17_) | copy-start | bytes 196612
  532.9 16.3 %copy-start.10 = (f32[8,2048]{1,0:T(8,128)S(1)}, f32[8,2048]{1,0:T(8,128)}, u32[]{:S(2)}) copy-start(f32[8,2048]{1,0:T(8,128)} %get-tuple-element.144) | copy-start | bytes 196612
  532.9 16.3 %copy-start.11 = (f32[8,2048]{1,0:T(8,128)S(1)}, f32[8,2048]{1,0:T(8,128)}, u32[]{:S(2)}) copy-start(f32[8,2048]{1,0:T(8,128)} %get-tuple-element.145) | copy-start | bytes 196612
  532.9 16.3 %copy-start.12 = (f32[8,2048]{1,0:T(8,128)S(1)}, f32[8,2048]{1,0:T(8,128)}, u32[]{:S(2)}) copy-start(f32[8,2048]{1,0:T(8,128)} %get-tuple-element.146) | copy-start | bytes 196612
  532.9 16.3 %copy-start.13 = (f32[8,2048]{1,0:T(8,128)S(1)}, f32[8,2048]{1,0:T(8,128)}, u32[]{:S(2)}) copy-start(f32[8,2048]{1,0:T(8,128)} %get-tuple-element.147) | copy-start | bytes 196612
  532.9 16.3 %copy-start.14 = (f32[8,2048]{1,0:T(8,128)S(1)}, f32[8,2048]{1,0:T(8,128)}, u32[]{:S(2)}) copy-start(f32[8,2048]{1,0:T(8,128)} %get-tuple-element.148) | copy-start | bytes 196612
  533.0 16.3 %copy-start.15 = (f32[8,2048]{1,0:T(8,128)S(1)}, f32[8,2048]{1,0:T(8,128)}, u32[]{:S(2)}) copy-start(f32[8,2048]{1,0:T(8,128)} %get-tuple-element.149) | copy-start | bytes 196612
  533.0 16.3 %copy-start.16 = (f32[8,2048]{1,0:T(8,128)S(1)}, f32[8,2048]{1,0:T(8,128)}, u32[]{:S(2)}) copy-start(f32[8,2048]{1,0:T(8,128)} %get-tuple-element.150) | copy-start | bytes 196612
  533.0 16.9 %copy-start.8 = (bf16[512,256]{1,0:T(8,128)(2,1)S(1)}, bf16[512,256]{1,0:T(8,128)(2,1)}, u32[]{:S(2)}) copy-start(bf16[512,256]{1,0:T(8,128)(2,1)} %reduce-scatter.7.cloned.1.call-done) | copy-start | bytes 786436
  543.2 10.1 %copy-start.7 = (bf16[2048,256]{1,0:T(8,128)(2,1)S(1)}, bf16[2048,256]{1,0:T(8,128)(2,1)}, u32[]{:S(2)}) copy-start(bf16[2048,256]{1,0:T(8,128)(2,1)} %reduce-scatter.5.cloned.1.call-done) | copy-start | bytes 3145732
  545.1 11.9 %all-to-all-start = ((f32[32,1,192]{2,1,0:T(1,128)}), f32[32,1,192]{2,1,0:T(1,128)S(1)}, u32[]{:S(2)}, u32[]{:S(2)}) async-start(f32[32,1,192]{2,1,0:T(1,128)} %all_to_all.8), calls=%async_computation.2 | async-start | bytes 65536 | tf_op jit(solution)/shard_map/all_to_all | solution.py:837
  (8 other events, 17.0 us)
Sparse Core Ops, SparseCore 0:
  9.6 84.7 all-gather.4
  96.0 63.2 all-gather.6
  160.9 29.5 all-gather.8
  191.9 81.5 all-gather.10
  275.6 87.7 reduce-scatter.4
  366.2 33.9 reduce-scatter.6
  402.5 79.1 reduce-scatter.8
  484.0 91.2 reduce-scatter.10
